TPU v7x, 256 devices: a whole 4x4x8 slice. The times are simulated.
256 devices in a mesh: dp: 8 (over x, core), grid: 32 (over y, z).
Axes of the slice: x: 4, y: 4, z: 8, core: 2. Of those that a mesh axis runs over, the one named last changes fastest.
Arguments:
- q_row: bfloat16 [16, 96, 96, 1536], P('dp', 'grid'), may hold values from -8 to 8, as said below
- k_row: bfloat16 [16, 96, 96, 1536], P('dp', 'grid'), may hold values from -8 to 8
- v_row: bfloat16 [16, 96, 96, 1536], P('dp', 'grid'), may hold values from -6 to 6
- q_col: bfloat16 [16, 96, 96, 1536], P('dp', None, 'grid'), may hold values from -8 to 8, as said below
- k_col: bfloat16 [16, 96, 96, 1536], P('dp', None, 'grid'), may hold values from -8 to 8
- cotangent: bfloat16 [16, 96, 96, 1536], P('dp', None, 'grid'), may hold values from -6 to 6
- w_value: bfloat16 [1536, 1536], P(('dp', 'grid')), may hold values from -0.15625 to 0.15625
- row_positions: int32 [96], replicated, may hold values from 0 to 95, each once
- col_positions: int32 [96], replicated, may hold values from 0 to 95, each once
- mlp_in: float32 [512], P('grid'), may hold values from -8 to 8
- mlp_bias: float32 [512], P('grid'), may hold values from -4 to 4
- mlp_out: float32 [512, 48], P('grid'), may hold values from -0.08 to 0.08
Outputs:
- attended: bfloat16 [16, 96, 96, 1536], P('dp', None, 'grid')
- grad_mlp_in: float32 [512], P('grid')
- grad_mlp_bias: float32 [512], P('grid')
- grad_mlp_out: float32 [512, 48], P('grid')
Inputs may be any that keep to these rules, and one draw needn't show every extreme that they name: q_row and k_row lie within the range. q_col and k_col lie within the range. `row_positions`: each of 0 to 95 appears once. `col_positions`: each of 0 to 95 appears once.
All inputs are finite; a program needn't handle non-finite values.
Results may differ from a plain program's by a relative error of at most 0.007.
Values may be sent and summed in bfloat16 or wider, within the bound.
No kernel may reach another device: no remote copies, remote signals or barrier semaphores. Data moves between devices by JAX's collectives and lax.ppermute only.
A program may use at most 192 MiB of HBM per device.

v0:
```python
import jax
import jax.numpy as jnp
from jax import lax
from jax.sharding import PartitionSpec as P

G = 96
D = 1536
NH = 48
HD = 32
NOFF = 191


PRECISE = lax.Precision.HIGHEST


def offset_coords():
    delta = jnp.arange(NOFF, dtype=jnp.float32) - (G - 1)
    scaled = delta * (8.0 / (G - 1))
    return jnp.sign(scaled) * jnp.log2(jnp.abs(scaled) + 1.0) / 3.0


def offset_one_hot(positions):
    spread = positions[:, None] - positions[None, :] + (G - 1)
    levels = jnp.arange(NOFF, dtype=jnp.int32)
    return (spread.reshape(-1)[:, None] == levels[None, :]).astype(jnp.float32)


def expand_bias(one_hot, bias_table):
    flat_bias = jnp.dot(one_hot, bias_table, precision=PRECISE)
    return flat_bias.reshape(G, G, NH).transpose(2, 0, 1)


def fold_bias(one_hot, bias_grad):
    flat_grad = bias_grad.transpose(1, 2, 0).reshape(G * G, NH)
    return lax.dot_general(one_hot, flat_grad, (((0,), (0,)), ((), ())), precision=PRECISE)


def soft_grad(attn_probs, d_probs):
    return attn_probs * (d_probs - jnp.sum(attn_probs * d_probs, axis=-1, keepdims=True))


def fetch_weight(w_value):
    return lax.all_gather(w_value, ("dp", "grid"), axis=0, tiled=True)


def shards(
    q_row,
    k_row,
    v_row,
    q_col,
    k_col,
    cotangent,
    w_value,
    row_positions,
    col_positions,
    mlp_in,
    mlp_bias,
    mlp_out,
):
    images = q_row.shape[0]
    row_count = q_row.shape[1]
    col_count = q_col.shape[2]
    coords = offset_coords()
    pre_act = coords[:, None] * mlp_in[None, :] + mlp_bias[None, :]
    hidden_units = jnp.maximum(pre_act, 0.0)
    partial_table = jnp.dot(hidden_units, mlp_out, precision=PRECISE)
    table_pre = lax.psum(partial_table, "grid")
    squashed = jax.nn.sigmoid(table_pre)
    bias_table = 16.0 * squashed
    hot_cols = offset_one_hot(col_positions)
    hot_rows = offset_one_hot(row_positions)
    bias_row = expand_bias(hot_cols, bias_table)
    bias_col = expand_bias(hot_rows, bias_table)
    score_scale = HD ** (-0.5)
    query_rows = q_row.reshape(images * row_count, G, NH, HD)
    key_rows = k_row.reshape(images * row_count, G, NH, HD)
    value_rows = v_row.reshape(images * row_count, G, NH, HD)
    scores = (
        jnp.einsum("nqhd,nkhd->nhqk", query_rows, key_rows, preferred_element_type=jnp.float32)
        * score_scale
        + bias_row[None]
    )
    p_row = jax.nn.softmax(scores, axis=-1)
    p_row_b = p_row.astype(jnp.bfloat16)
    row_out = jnp.einsum(
        "nhqk,nkhd->nqhd", p_row_b, value_rows, preferred_element_type=jnp.float32
    ).astype(jnp.bfloat16)
    flat_out = row_out.reshape(images * row_count * G, D)
    whole_weight = fetch_weight(w_value)
    projected = jnp.dot(flat_out, whole_weight, preferred_element_type=jnp.float32)
    values = projected.astype(jnp.bfloat16).reshape(images, row_count, G, D)
    col_values = lax.all_to_all(values, "grid", split_axis=2, concat_axis=1, tiled=True)
    query_cols = q_col.reshape(images, G, col_count, NH, HD)
    key_cols = k_col.reshape(images, G, col_count, NH, HD)
    value_cols = col_values.reshape(images, G, col_count, NH, HD)
    scores_col = (
        jnp.einsum("bqchd,bkchd->bchqk", query_cols, key_cols, preferred_element_type=jnp.float32)
        * score_scale
        + bias_col
    )
    p_col = jax.nn.softmax(scores_col, axis=-1)
    p_col_b = p_col.astype(jnp.bfloat16)
    attended = (
        jnp.einsum("bchqk,bkchd->bqchd", p_col_b, value_cols, preferred_element_type=jnp.float32)
        .astype(jnp.bfloat16)
        .reshape(images, G, col_count, D)
    )
    grad_cols = cotangent.reshape(images, G, col_count, NH, HD)
    dprob_col = jnp.einsum(
        "bqchd,bkchd->bchqk", grad_cols, value_cols, preferred_element_type=jnp.float32
    )
    ds_col = soft_grad(p_col, dprob_col)
    col_table = fold_bias(hot_rows, jnp.sum(ds_col, axis=(0, 1)))
    col_summed = lax.psum(col_table, ("dp", "grid"))
    d_values = (
        jnp.einsum("bchqk,bqchd->bkchd", p_col_b, grad_cols, preferred_element_type=jnp.float32)
        .astype(jnp.bfloat16)
        .reshape(images, G, col_count, D)
    )
    d_rows = lax.all_to_all(d_values, "grid", split_axis=1, concat_axis=2, tiled=True)
    flat_grad = d_rows.reshape(images * row_count * G, D)
    d_flat = lax.dot_general(
        flat_grad, whole_weight, (((1,), (1,)), ((), ())), preferred_element_type=jnp.float32
    )
    d_row_out = d_flat.astype(jnp.bfloat16).reshape(images * row_count, G, NH, HD)
    dprob_row = jnp.einsum(
        "nqhd,nkhd->nhqk", d_row_out, value_rows, preferred_element_type=jnp.float32
    )
    ds_row = soft_grad(p_row, dprob_row)
    row_table = fold_bias(hot_cols, jnp.sum(ds_row, axis=0))
    table_sum = col_summed + lax.psum(row_table, ("dp", "grid"))
    batch_size = lax.axis_size("dp") * images
    table_grad = table_sum / (batch_size * G)
    pre_grad = table_grad * 16.0 * squashed * (1.0 - squashed)
    grad_mlp_out = lax.dot_general(
        hidden_units, pre_grad, (((0,), (0,)), ((), ())), precision=PRECISE
    )
    back_units = lax.dot_general(pre_grad, mlp_out, (((1,), (1,)), ((), ())), precision=PRECISE)
    unit_grad = jnp.where(pre_act > 0, back_units, 0.0)
    grad_mlp_in = jnp.sum(unit_grad * coords[:, None], axis=0)
    grad_mlp_bias = jnp.sum(unit_grad, axis=0)
    return (attended, grad_mlp_in, grad_mlp_bias, grad_mlp_out)


def solution(mesh):
    return jax.shard_map(
        shards,
        mesh=mesh,
        in_specs=(
            P("dp", "grid", None, None),
            P("dp", "grid", None, None),
            P("dp", "grid", None, None),
            P("dp", None, "grid", None),
            P("dp", None, "grid", None),
            P("dp", None, "grid", None),
            P(("dp", "grid"), None),
            P(),
            P(),
            P("grid"),
            P("grid"),
            P("grid", None),
        ),
        out_specs=(P("dp", None, "grid", None), P("grid"), P("grid"), P("grid", None)),
        check_vma=False,
    )
```

profile of v0, /device:TPU:1, one launch (start us, length us, event | category | flops | bytes accessed | tf_op | source)
XLA Modules:
  0.0 479.7 jit_solution(3552161299242555741)
XLA Ops:
  7.2 0.0 copy-start
  7.2 0.0 all-gather.3.cloned.1.call-start
  7.2 0.7 all-gather.3.cloned.1.call-update
  7.9 0.8 subtract_add_fusion
  8.7 0.1 add.83
  8.8 0.0 copy-start.10
  8.9 0.0 copy-start.15
  8.9 0.6 copy-done.15
  9.4 0.9 fusion.55
  10.4 119.0 %psum.21 = f32[191,48]{0,1:T(8,128)S(1)} all-reduce(f32[191,48]{0,1:T(8,128)S(1)} %fusion.55), channel_id=1, replica_groups=mesh['dp'=8,'grid'=32] {'grid'}, use_global_device_ids=true, to_apply=%region_0.0 | all-reduce | flops 9168 | bytes 73344 | tf_op jit(solution)/shard_map/psum | solution.py:67
  129.4 4.4 fusion.11
  133.8 2.2 reshape.130
  136.1 1.9 copy.134
  138.0 4.1 copy.132
  142.2 2.4 copy.133
  144.6 2.9 copy.137
  147.5 0.0 copy-start.1
  147.5 11.3 %fusion.79 = (f32[2,3,48,96]{3,2,1,0:T(8,128)S(1)}, f32[2,3,48,96,96]{3,4,2,1,0:T(8,128)}) fusion(f32[48,96,96]{1,2,0:T(8,128)} %bitcast.78, bf16[2,96,3,48,32]{1,4,3,2,0:T(8,128)(2,1)} %bitcast.86, bf16[2,96,3,48,32]{1,4,3,2,0:T(8,128)(2,1)} %bitcast.87), kind=kOutput, calls=%fused_computation.87 | convolution fusion | flops 180486240 | bytes 16035840 | tf_op jit(solution)/shard_map/sub | solution.py:101
  158.8 10.2 %fusion.35 = bf16[2,3,48,96,32]{3,4,2,1,0:T(8,128)(2,1)} fusion(bf16[2,96,3,48,32]{1,4,3,2,0:T(8,128)(2,1)S(1)} %bitcast.75, f32[2,3,48,96,96]{3,4,2,1,0:T(8,128)} %get-tuple-element.33, f32[2,3,48,96]{3,2,1,0:T(8,128)S(1)} %get-tuple-element.32), kind=kOutput, calls=%fused_computation.47 | convolution fusion | flops 176062464 | bytes 14266368 | tf_op jit(solution)/shard_map/bchqk,bqchd->bkchd/dot_general | solution.py:116
  169.1 5.3 %copy.141 = bf16[2,96,3,1536]{3,0,2,1:T(2,128)(2,1)} copy(bf16[2,96,3,1536]{1,3,2,0:T(8,128)(2,1)} %bitcast.90) | data formatting | bytes 3538944 | tf_op jit(solution)/shard_map/reshape | solution.py:118
  174.4 5.0 %all-to-all-start.1 = ((bf16[2,96,3,1536]{3,0,2,1:T(2,128)(2,1)}), bf16[2,96,3,1536]{3,0,2,1:T(2,128)(2,1)}, u32[]{:S(2)}, u32[]{:S(2)}) async-start(bf16[2,96,3,1536]{3,0,2,1:T(2,128)(2,1)} %copy.141), calls=%async_computation.1 | async-start | bytes 3538944 | tf_op jit(solution)/shard_map/all_to_all | solution.py:120
  179.4 0.0 copy-done.12
  179.4 0.1 subtract_add_fusion.1
  179.5 0.1 add.74
  179.6 4.5 fusion.17
  184.0 2.2 reshape.123
  186.3 1.9 copy.125
  188.2 4.1 copy.123
  192.3 0.0 copy-done.8
  192.3 2.4 copy.124
  194.8 4.2 copy.126
  198.9 11.3 %fusion.78 = (f32[6,48,96]{2,1,0:T(8,128)S(1)}, f32[6,48,96,96]{2,3,1,0:T(8,128)}) fusion(f32[48,96,96]{1,2,0:T(8,128)S(1)} %bitcast.79, bf16[6,96,48,32]{1,3,2,0:T(8,128)(2,1)} %bitcast.88, bf16[6,96,48,32]{1,3,2,0:T(8,128)(2,1)} %bitcast.89), kind=kOutput, calls=%fused_computation.86 | convolution fusion | flops 180486240 | bytes 16035840 | tf_op jit(solution)/shard_map/sub | solution.py:83
  210.2 7.7 %convert_bitcast_fusion = bf16[6,96,48,32]{1,3,2,0:T(8,128)(2,1)S(1)} fusion(bf16[6,96,48,32]{1,3,2,0:T(8,128)(2,1)} %bitcast.82, f32[6,48,96,96]{2,3,1,0:T(8,128)} %get-tuple-element.31, f32[6,48,96]{2,1,0:T(8,128)S(1)} %get-tuple-element.30), kind=kOutput, calls=%fused_computation.44 | convolution fusion | flops 176062464 | bytes 14266368 | tf_op jit(solution)/shard_map/nhqk,nkhd->nqhd/dot_general | solution.py:85
  218.0 2.8 copy.128
  220.8 3.1 reshape.125
  223.9 0.0 all-to-all-done.1
  223.9 2.4 copy.142
  226.3 3.2 reshape.135
  229.5 8.5 %reshape.139 = bf16[1536,1536]{1,0:T(8,128)(2,1)} reshape(bf16[256,6,1536]{2,1,0:T(8,128)(2,1)} %all-gather.3.cloned.1.call-done) | data formatting | bytes 9437184
  238.0 6.4 %convolution_convert_fusion.1 = bf16[576,1536]{1,0:T(8,128)(2,1)} fusion(bf16[576,1536]{1,0:T(8,128)(2,1)S(1)} %copy-done.9, bf16[1536,1536]{1,0:T(8,128)(2,1)} %reshape.139), kind=kOutput, calls=%fused_computation.41 | convolution fusion | flops 2718793728 | bytes 8257536 | tf_op jit(solution)/shard_map/dot_general | solution.py:122
  244.4 2.7 copy.143
  247.1 3.6 reshape.136
  250.8 5.9 %convolution_convert_fusion = bf16[576,1536]{1,0:T(8,128)(2,1)S(1)} fusion(bf16[576,1536]{0,1:T(8,128)(2,1)} %reshape.125, bf16[1536,1536]{1,0:T(8,128)(2,1)} %reshape.139), kind=kOutput, calls=%fused_computation.40 | convolution fusion | flops 2718793728 | bytes 8257536 | tf_op jit(solution)/shard_map/dot_general | solution.py:90
  256.6 3.0 copy.129
  259.7 10.2 %all-to-all-start = ((bf16[2,3,96,1536]{3,0,1,2:T(2,128)(2,1)}), bf16[2,3,96,1536]{3,0,1,2:T(2,128)(2,1)}, u32[]{:S(2)}, u32[]{:S(2)}) async-start(bf16[2,3,96,1536]{3,0,1,2:T(2,128)(2,1)} %copy.129), calls=%async_computation | async-start | bytes 3538944 | tf_op jit(solution)/shard_map/all_to_all | solution.py:92
  269.9 10.4 %fusion = f32[6,48,96,96]{2,3,1,0:T(8,128)} fusion(bf16[6,96,48,32]{1,3,2,0:T(8,128)(2,1)} %bitcast.83, bf16[6,96,48,32]{1,0,3,2:T(8,128)(2,1)S(1)} %copy-done.4, f32[6,48,96,96]{2,3,1,0:T(8,128)} %get-tuple-element.31, f32[6,48,96]{2,1,0:T(8,128)S(1)} %get-tuple-element.30), kind=kOutput, calls=%fused_computation | convolution fusion | flops 175205472 | bytes 24883200 | tf_op jit(solution)/shard_map/sub | solution.py:39
  280.3 13.5 %multiply_reduce_fusion = f32[48,96,96]{1,2,0:T(8,128)} fusion(f32[6,48,96,96]{2,3,1,0:T(8,128)} %fusion, f32[6,48,96,96]{2,3,1,0:T(8,128)} %get-tuple-element.31, f32[6,48,96]{2,1,0:T(8,128)S(1)} %get-tuple-element.30, bf16[6,96,48,32]{1,3,2,0:T(8,128)(2,1)} %bitcast.84, bf16[6,96,48,32]{1,0,3,2:T(8,128)(2,1)S(1)} %copy-done.4), kind=kOutput, calls=%fused_computation.8 | convolution fusion | flops 180043776 | bytes 26652672 | tf_op jit(solution)/shard_map/nqhd,nkhd->nhqk/dot_general | solution.py:126
  293.8 2.0 copy.145
  295.8 2.5 reshape.137
  298.3 0.0 all-to-all-done
  298.4 2.7 copy.131
  301.0 6.1 %reshape.127 = bf16[2,96,3,48,32]{4,3,0,2,1:T(8,128)(2,1)} reshape(bf16[2,32,3,3,1536]{4,0,3,2,1:T(2,128)(2,1)S(1)} %copy.131) | data formatting | bytes 3538944 | tf_op jit(solution)/shard_map/reshape | solution.py:95
  307.2 8.3 %copy.135 = bf16[2,96,3,48,32]{1,4,3,2,0:T(8,128)(2,1)} copy(bf16[2,96,3,48,32]{4,3,0,2,1:T(8,128)(2,1)} %reshape.127) | data formatting | bytes 3538944 | tf_op jit(solution)/shard_map/reshape | solution.py:95
  315.5 9.4 %fusion.32 = bf16[2,3,48,32,96]{4,3,2,1,0:T(8,128)(2,1)} fusion(bf16[2,96,3,48,32]{1,4,3,2,0:T(8,128)(2,1)} %copy.135, f32[2,3,48,96,96]{3,4,2,1,0:T(8,128)} %get-tuple-element.33, f32[2,3,48,96]{3,2,1,0:T(8,128)S(1)} %get-tuple-element.32), kind=kOutput, calls=%fused_computation.46 | convolution fusion | flops 176062464 | bytes 14266368 | tf_op jit(solution)/shard_map/bchqk,bkchd->bqchd/dot_general | solution.py:104
  325.0 6.3 %fusion.80 = f32[2,3,48,96,96]{4,3,2,1,0:T(8,128)} fusion(bf16[2,96,3,48,32]{1,4,3,2,0:T(8,128)(2,1)S(1)} %copy-done.3, bf16[2,96,3,48,32]{1,4,3,2,0:T(8,128)(2,1)S(1)} %bitcast.76), kind=kOutput, calls=%fused_computation.88 | convolution fusion | flops 169869312 | bytes 14155776 | tf_op jit(solution)/shard_map/bqchd,bkchd->bchqk/dot_general | solution.py:109
  331.2 17.8 %fusion.5 = f32[48,96,96]{1,2,0:T(8,128)} fusion(f32[2,3,48,96,96]{4,3,2,1,0:T(8,128)} %fusion.80, f32[2,3,48,96,96]{3,4,2,1,0:T(8,128)} %get-tuple-element.33, f32[2,3,48,96]{3,2,1,0:T(8,128)S(1)} %get-tuple-element.32, bf16[2,96,3,48,32]{1,4,3,2,0:T(8,128)(2,1)} %copy.135, bf16[2,96,3,48,32]{1,4,3,2,0:T(8,128)(2,1)S(1)} %bitcast.77), kind=kOutput, calls=%fused_computation.7 | convolution fusion | flops 185379936 | bytes 26652672 | tf_op jit(solution)/shard_map/sub | solution.py:39
  349.0 2.0 copy.139
  351.0 2.5 reshape.133
  353.6 5.4 %fusion.10 = f32[191,48]{0,1:T(8,128)S(1)} fusion(f32[9216,48]{0,1:T(8,128)} %reshape.133, s32[9216]{0:T(1024)S(1)} %copy-done.11), kind=kOutput, calls=%fused_computation.20 | convolution fusion | flops 1015667712 | bytes 1843008 | tf_op jit(solution)/shard_map/dot_general | solution.py:35
  359.0 5.3 %fusion.46 = f32[191,48]{0,1:T(8,128)S(1)} fusion(f32[191,48]{0,1:T(8,128)S(1)} %fusion.10, f32[9216,48]{0,1:T(8,128)} %reshape.137, s32[9216]{0:T(1024)S(1)} %add.74), kind=kOutput, calls=%fused_computation.49 | convolution fusion | flops 1015676864 | bytes 1879680 | tf_op jit(solution)/shard_map/dot_general | solution.py:35
  364.3 104.5 %psum.24 = f32[191,48]{0,1:T(8,128)S(1)} all-reduce(f32[191,48]{0,1:T(8,128)S(1)} %fusion.46), channel_id=1, replica_groups=mesh['dp'=8,'grid'=32] {'dp','grid'}, use_global_device_ids=true, to_apply=%region_7.0 | all-reduce | flops 9168 | bytes 73344 | tf_op jit(solution)/shard_map/psum | solution.py:114
  468.8 0.8 fusion.77
  469.6 0.8 fusion.53
  470.4 2.3 copy.146
  (29 shorter events, 0.1 us)
Async XLA Ops:
  7.2 2.3 copy-start
  7.2 222.3 %all-gather.3.cloned.1.call-start = ((), (), s32[]{:S(2)}) async-start(), calls=%async_computation.2 | async-start | bytes 6316032 | tf_op jit(solution)/shard_map/all_gather | solution.py:43
  8.8 120.6 %copy-start.10 = (s32[9216]{0:T(1024)}, s32[9216]{0:T(1024)S(1)}, u32[]{:S(2)}) copy-start(s32[9216]{0:T(1024)S(1)} %add.83) | copy-start | bytes 110596
  8.9 0.6 copy-start.15
  138.0 4.1 copy-start.7
  147.5 11.3 %copy-start.1 = (bf16[2,96,3,1536]{1,3,2,0:T(8,128)(2,1)}, bf16[2,96,3,1536]{1,3,2,0:T(8,128)(2,1)S(1)}, u32[]{:S(2)}) copy-start(bf16[2,96,3,1536]{1,3,2,0:T(8,128)(2,1)S(1)} %copy.137) | copy-start | bytes 5308420
  174.3 5.0 %copy-start.12 = (s32[96]{0:T(128)S(1)}, s32[96]{0:T(128)}, u32[]{:S(2)}) copy-start(s32[96]{0:T(128)} %param.20) | copy-start | bytes 1156
  174.4 49.6 %all-to-all-start.1 = ((bf16[2,96,3,1536]{3,0,2,1:T(2,128)(2,1)}), bf16[2,96,3,1536]{3,0,2,1:T(2,128)(2,1)}, u32[]{:S(2)}, u32[]{:S(2)}) async-start(bf16[2,96,3,1536]{3,0,2,1:T(2,128)(2,1)} %copy.141), calls=%async_computation.1 | async-start | bytes 3538944 | tf_op jit(solution)/shard_map/all_to_all | solution.py:120
  188.2 4.1 copy-start.8
  194.8 4.2 copy-start.5
  229.5 8.5 %copy-start.9 = (bf16[576,1536]{1,0:T(8,128)(2,1)S(1)}, bf16[576,1536]{1,0:T(8,128)(2,1)}, u32[]{:S(2)}) copy-start(bf16[576,1536]{1,0:T(8,128)(2,1)} %reshape.135) | copy-start | bytes 5308420
  259.7 10.2 %copy-start.4 = (bf16[6,96,48,32]{1,0,3,2:T(8,128)(2,1)S(1)}, bf16[6,96,48,32]{1,0,3,2:T(8,128)(2,1)}, u32[]{:S(2)}) copy-start(bf16[6,96,48,32]{1,0,3,2:T(8,128)(2,1)} %reshape.136) | copy-start | bytes 5308420
  259.7 38.7 %all-to-all-start = ((bf16[2,3,96,1536]{3,0,1,2:T(2,128)(2,1)}), bf16[2,3,96,1536]{3,0,1,2:T(2,128)(2,1)}, u32[]{:S(2)}, u32[]{:S(2)}) async-start(bf16[2,3,96,1536]{3,0,1,2:T(2,128)(2,1)} %copy.129), calls=%async_computation | async-start | bytes 3538944 | tf_op jit(solution)/shard_map/all_to_all | solution.py:92
  315.5 9.4 %copy-start.2 = (bf16[2,96,3,1536]{1,3,2,0:T(8,128)(2,1)S(1)}, bf16[2,96,3,1536]{1,3,2,0:T(8,128)(2,1)}, u32[]{:S(2)}) copy-start(bf16[2,96,3,1536]{1,3,2,0:T(8,128)(2,1)} %copy-done.1) | copy-start | bytes 5308420
  315.5 9.4 %copy-start.3 = (bf16[2,96,3,48,32]{1,4,3,2,0:T(8,128)(2,1)S(1)}, bf16[2,96,3,48,32]{1,4,3,2,0:T(8,128)(2,1)}, u32[]{:S(2)}) copy-start(bf16[2,96,3,48,32]{1,4,3,2,0:T(8,128)(2,1)} %copy.135) | copy-start | bytes 5308420
  351.0 2.5 copy-start.11
  353.6 115.2 %copy-start.13 = (f32[16]{0:T(128)S(1)}, f32[16]{0:T(128)}, u32[]{:S(2)}) copy-start(f32[16]{0:T(128)} %param.22) | copy-start | bytes 196
  353.6 115.2 %copy-start.14 = (f32[16]{0:T(128)S(1)}, f32[16]{0:T(128)}, u32[]{:S(2)}) copy-start(f32[16]{0:T(128)} %param.21) | copy-start | bytes 196
  353.6 115.2 %copy-start.16 = (f32[191]{0:T(256)S(1)}, f32[191]{0:T(256)}, u32[]{:S(2)}) copy-start(f32[191]{0:T(256)} %copy-done.15) | copy-start | bytes 2296
  353.6 116.8 %copy-start.6 = (bf16[2,3,48,32,96]{4,3,2,1,0:T(8,128)(2,1)S(1)}, bf16[2,3,48,32,96]{4,3,2,1,0:T(8,128)(2,1)}, u32[]{:S(2)}) copy-start(bf16[2,3,48,32,96]{4,3,2,1,0:T(8,128)(2,1)} %fusion.32) | copy-start | bytes 5308420
Sparse Core Ops, SparseCore 0:
  11.8 121.0 all-gather.2
where the time goes:
time: 489 us; the launch traced here: 480 us
  blocking collectives  224 us (46%)
  matrix products  132 us (27%)
  local copies, waits for them, and re-layouts  92.6 us (19%)
  starting transfers between devices  15.2 us (3%)
  between operations  14.5 us (3%)
    psum x1, blocking collectives, shards(): table_pre = lax.psum(partial_table, 'grid')  119 us
    psum x1, blocking collectives, shards(): col_summed = lax.psum(col_table, ('dp', 'grid'))  104 us
    unnamed x42, local copies, waits for them, and re-layouts  31.6 us
    sub x2, matrix products, soft_grad(): d_probs - jnp.sum(attn_probs * d_probs, axis=-1, keepdims=True)  28.2 us
    reshape x2, local copies, waits for them, and re-layouts, shards(): value_cols = col_values.reshape(images, G, col_count, NH, HD)  14.5 us
    dot_general x1, matrix products, shards(): jnp.einsum('nqhd,nkhd->nhqk', d_row_out, value_rows, preferred_element_ty...  13.5 us
    sub x1, matrix products, shards(): p_col = jax.nn.softmax(scores_col, axis=-1)  11.3 us
    sub x1, matrix products, shards(): p_row = jax.nn.softmax(scores, axis=-1)  11.3 us
  transfers between devices with their start and end apart: 3, of which 0 were waited for; matrix products, arithmetic and copies ran while one was open for 26% of the time, Pallas kernels for 0%

commit v1 on v0

v1 whole, which is shorter than its diff:
```python
import functools

import jax
import jax.numpy as jnp
import numpy as np
from jax import lax
from jax.experimental import pallas as pl
from jax.experimental.pallas import tpu as pltpu
from jax.sharding import PartitionSpec as P

G = 96
D = 1536
NH = 48
HD = 32
HM = 512
NOFF = 191
GRID = 32
DP = 8
LANES = 128
PACK = LANES // HD
GROUPS = D // LANES
ROWS = PACK * G
LOG2E = 1.4426950408889634

PRECISE = lax.Precision.HIGHEST
NT = (((1,), (1,)), ((), ()))
TN = (((0,), (0,)), ((), ()))
NN = (((1,), (0,)), ((), ()))

STACK = 2
UNROLL = GROUPS


def head_masks():
    lane = lax.broadcasted_iota(jnp.int32, (G, LANES), 1)
    return [(lane >= j * HD) & (lane < (j + 1) * HD) for j in range(PACK)]


def stack_heads(x, masks):
    zero = jnp.zeros_like(x)
    return jnp.concatenate([jnp.where(m, x, zero) for m in masks], axis=0)


def lane_group(g):
    return pl.ds(pl.multiple_of(g * LANES, LANES), LANES)


def head_rows(g, first):
    return pl.ds(pl.multiple_of(g * ROWS + first * G, G), STACK * G)


def softmax_rows(key, query, bias, masks):
    s = lax.dot_general(stack_heads(key, masks), query, NT, preferred_element_type=jnp.float32)
    s = s * (HD ** (-0.5) * LOG2E) + bias
    s = s.reshape(STACK, G, G)
    e = jnp.exp2(s - jnp.max(s, axis=1, keepdims=True))
    p = e * (1.0 / jnp.sum(e, axis=1, keepdims=True))
    return p.reshape(STACK * G, G).astype(jnp.bfloat16)


def forward_kernel(q_ref, k_ref, x_ref, bias_ref, p_ref, o_ref, *, transpose):
    masks = head_masks()

    def body(g, carry):
        sl = lane_group(g)
        query, key, x = q_ref[0, :, sl], k_ref[0, :, sl], x_ref[0, :, sl]
        o = None
        for first in range(0, PACK, STACK):
            own = masks[first:first + STACK]
            rows = head_rows(g, first)
            p = softmax_rows(key, query, bias_ref[rows, :G], own)
            p_ref[0, rows, :] = p
            if transpose:
                r = lax.dot_general(p, x, NN, preferred_element_type=jnp.float32)
                for j in range(STACK):
                    o = jnp.where(own[j], r[j * G:(j + 1) * G], 0.0 if o is None else o)
            else:
                r = lax.dot_general(
                    p, stack_heads(x, own), TN, preferred_element_type=jnp.float32
                )
                o = r if o is None else o + r
        o_ref[0, :, sl] = o.astype(jnp.bfloat16)
        return carry

    lax.fori_loop(0, GROUPS, body, 0, unroll=UNROLL)


def backward_kernel(p_ref, v_ref, g_ref, *outs, attend):
    sum_ref = outs[-1]
    masks = head_masks()

    @pl.when(pl.program_id(0) == 0)
    def _():
        sum_ref[...] = jnp.zeros_like(sum_ref)

    def body(g, carry):
        sl = lane_group(g)
        value, grad = v_ref[0, :, sl], g_ref[0, :, sl]
        o = None
        for first in range(0, PACK, STACK):
            rows = head_rows(g, first)
            vs = stack_heads(value, masks[first:first + STACK])
            p = p_ref[0, rows, :]
            if attend:
                r = lax.dot_general(p, vs, TN, preferred_element_type=jnp.float32)
                o = r if o is None else o + r
            dp = lax.dot_general(vs, grad, NT, preferred_element_type=jnp.float32)
            dp = dp.reshape(STACK, G, G)
            pf = p.astype(jnp.float32).reshape(STACK, G, G)
            ds = pf * (dp - jnp.sum(pf * dp, axis=1, keepdims=True))
            sum_ref[rows, :G] += ds.reshape(STACK * G, G)
        if attend:
            outs[0][0, :, sl] = o.astype(jnp.bfloat16)
        return carry

    lax.fori_loop(0, GROUPS, body, 0, unroll=UNROLL)


BLOCK = (1, G, D)
PSHAPE = (1, NH * G, G)


def each(shape):
    return pl.BlockSpec(shape, lambda i: (i, 0, 0))


def whole(shape):
    return pl.BlockSpec(shape, lambda i: (0,) * len(shape))


def attention_forward(q, k, x, bias, transpose):
    n = q.shape[0]
    return pl.pallas_call(
        functools.partial(forward_kernel, transpose=transpose),
        grid=(n,),
        in_specs=[each(BLOCK)] * 3 + [whole((NH * G, LANES))],
        out_specs=[each(PSHAPE), each(BLOCK)],
        out_shape=[
            jax.ShapeDtypeStruct((n, NH * G, G), jnp.bfloat16),
            jax.ShapeDtypeStruct((n, G, D), jnp.bfloat16),
        ],
        cost_estimate=pl.CostEstimate(flops=n * NH * 16 * G * G * LANES, transcendentals=n * NH * G * G, bytes_accessed=20_000_000),
    )(q, k, x, bias)


def attention_backward(p, v, g, attend):
    n = p.shape[0]
    specs = [each(BLOCK)] if attend else []
    shapes = [jax.ShapeDtypeStruct((n, G, D), jnp.bfloat16)] if attend else []
    return pl.pallas_call(
        functools.partial(backward_kernel, attend=attend),
        grid=(n,),
        in_specs=[each(PSHAPE), each(BLOCK), each(BLOCK)],
        out_specs=specs + [whole((NH * G, LANES))],
        out_shape=shapes + [jax.ShapeDtypeStruct((NH * G, LANES), jnp.float32)],
        cost_estimate=pl.CostEstimate(flops=n * NH * 16 * G * G * LANES, transcendentals=0, bytes_accessed=20_000_000),
    )(p, v, g)


def expand_kernel(pos_ref, table_ref, lane_ref, out_ref):
    low, high = table_ref[:, :LANES], table_ref[:, LANES:]
    lane = jnp.broadcast_to(lane_ref[...], (NH, LANES)) + (G - 1)

    def body(b, carry):
        level = lane - pos_ref[b]
        index = jnp.bitwise_and(level, LANES - 1)
        x = jnp.take_along_axis(low, index, axis=1, mode="promise_in_bounds")
        y = jnp.take_along_axis(high, index, axis=1, mode="promise_in_bounds")
        out_ref[pl.ds(b, NH, stride=G), :] = jnp.where(level >= LANES, y, x)
        return carry

    lax.fori_loop(0, G, body, 0, unroll=16)


def expand(table, positions):
    lane = jnp.pad(positions, (0, LANES - G))[None]
    return pl.pallas_call(
        expand_kernel,
        in_specs=[
            pl.BlockSpec(memory_space=pltpu.SMEM),
            pl.BlockSpec(memory_space=pltpu.VMEM),
            pl.BlockSpec(memory_space=pltpu.VMEM),
        ],
        out_specs=pl.BlockSpec(memory_space=pltpu.VMEM),
        out_shape=jax.ShapeDtypeStruct((NH * G, LANES), jnp.float32),
    )(positions, table, lane)


def fold_kernel(pos_ref, sum_ref, lane_ref, out_ref):
    lane = jnp.broadcast_to(lane_ref[...], (NH, LANES))
    keep = lax.broadcasted_iota(jnp.int32, (NH, LANES), 1) < G
    zero = jnp.zeros((NH, LANES), jnp.float32)

    def body(b, total):
        one = sum_ref[pl.ds(b, NH, stride=G), :]
        one = jnp.take_along_axis(one, lane, axis=1, mode="promise_in_bounds")
        one = jnp.concatenate([jnp.where(keep, one, 0.0), zero], axis=1)
        return total + pltpu.roll(one, (G - 1) - pos_ref[b], 1)

    out_ref[...] = lax.fori_loop(0, G, body, jnp.zeros((NH, 2 * LANES), jnp.float32), unroll=4)


def fold(sums, positions):
    inverse = jnp.sum(
        jnp.where(positions[None, :] == jnp.arange(LANES)[:, None], jnp.arange(G)[None, :], 0), axis=1
    ).astype(jnp.int32)[None]
    return pl.pallas_call(
        fold_kernel,
        in_specs=[
            pl.BlockSpec(memory_space=pltpu.SMEM),
            pl.BlockSpec(memory_space=pltpu.VMEM),
            pl.BlockSpec(memory_space=pltpu.VMEM),
        ],
        out_specs=pl.BlockSpec(memory_space=pltpu.VMEM),
        out_shape=jax.ShapeDtypeStruct((NH, 2 * LANES), jnp.float32),
    )(positions, sums, inverse)

def offset_coords():
    delta = jnp.arange(NOFF, dtype=jnp.float32) - (G - 1)
    scaled = delta * (8.0 / (G - 1))
    return jnp.sign(scaled) * jnp.log2(jnp.abs(scaled) + 1.0) / 3.0


def to_tile(flat):
    pad = [(0, 0)] * (flat.ndim - 1) + [(0, 1024 - flat.shape[-1])]
    return jnp.pad(flat, pad).reshape(flat.shape[:-1] + (8, 128))


def from_tile(tiles):
    return tiles.reshape(tiles.shape[:-2] + (1024,))[..., :800]


def gather_units(mlp_in, mlp_bias, mlp_out):
    own = jnp.concatenate([mlp_out, mlp_in[:, None], mlp_bias[:, None]], axis=1)
    tile = to_tile(own.reshape(800))
    got = lax.all_to_all(
        jnp.broadcast_to(tile[None], (GRID, 8, 128)), "grid", 0, 0, tiled=True
    )
    units = from_tile(got).reshape(HM, 50)
    return units[:, :NH], units[:, NH], units[:, NH + 1]


def reduce_units(grad_out, grad_in, grad_bias):
    whole = jnp.concatenate([grad_out, grad_in[:, None], grad_bias[:, None]], axis=1)
    tiles = to_tile(whole.reshape(GRID, 800))
    got = lax.all_to_all(tiles, "grid", 0, 0, tiled=True)
    own = jnp.sum(got, axis=0)
    got = lax.all_to_all(jnp.broadcast_to(own[None], (DP, 8, 128)), "dp", 0, 0, tiled=True)
    own = from_tile(jnp.sum(got, axis=0)).reshape(16, 50)
    return own[:, :NH], own[:, NH], own[:, NH + 1]


def along_x(step, swap):
    return [(i, ((i // 2 + step) % 4) * 2 + ((i % 2) ^ swap)) for i in range(DP)]


def fetch_weight(w_value):
    part = lax.all_to_all(
        jnp.broadcast_to(w_value[None], (GRID,) + w_value.shape), "grid", 0, 0, tiled=True
    ).reshape(D // DP, D)
    mine = [part]
    for step in (1, 2, 3):
        mine.append(lax.ppermute(part, "dp", along_x(step, 0)))
    mine = jnp.stack(mine)
    other = lax.ppermute(mine, "dp", along_x(0, 1))
    both = jnp.stack([mine, other])
    here = lax.axis_index("dp")
    x, core = here // 2, here % 2
    blocks = []
    for target in range(DP):
        tx, tc = target // 2, target % 2
        blocks.append(both[jnp.bitwise_xor(core, tc), (x - tx) % 4])
    return jnp.concatenate(blocks, axis=0)


def shards(
    q_row, k_row, v_row, q_col, k_col, cotangent, w_value,
    row_positions, col_positions, mlp_in, mlp_bias, mlp_out,
):
    images = q_row.shape[0]
    row_count = q_row.shape[1]
    col_count = q_col.shape[2]
    all_out, all_in, all_bias = gather_units(mlp_in, mlp_bias, mlp_out)
    coords = offset_coords()
    pre_act = coords[:, None] * all_in[None, :] + all_bias[None, :]
    hidden_units = jnp.maximum(pre_act, 0.0)
    table_pre = lax.dot_general(all_out, hidden_units, (((0,), (1,)), ((), ())), precision=PRECISE)
    squashed = jax.nn.sigmoid(table_pre)
    table = jnp.pad(squashed * (16.0 * LOG2E), ((0, 0), (0, 2 * LANES - NOFF)))
    whole_weight = fetch_weight(w_value)

    rows = lambda x: x.reshape(images * row_count, G, D)
    cols = lambda x: x.transpose(0, 2, 1, 3).reshape(images * col_count, G, D)
    bias_row = expand(table, col_positions)
    p_row, row_out = attention_forward(rows(q_row), rows(k_row), rows(v_row), bias_row, False)
    col_out = lax.all_to_all(
        row_out.reshape(images, row_count, G, D), "grid", split_axis=2, concat_axis=1, tiled=True
    )

    bias_col = expand(table, row_positions)
    grad_cols = cols(cotangent)
    p_col, d_values = attention_forward(cols(q_col), cols(k_col), grad_cols, bias_col, True)
    d_rows = lax.all_to_all(
        d_values.reshape(images, col_count, G, D), "grid", split_axis=2, concat_axis=1, tiled=True
    )

    value_cols = jnp.dot(
        cols(col_out).reshape(-1, D), whole_weight, preferred_element_type=jnp.float32
    ).astype(jnp.bfloat16).reshape(images * col_count, G, D)
    attended, col_sums = attention_backward(p_col, value_cols, grad_cols, True)
    attended = attended.reshape(images, col_count, G, D).transpose(0, 2, 1, 3)
    col_table = fold(col_sums, row_positions)

    d_flat = lax.dot_general(
        d_rows.transpose(0, 2, 1, 3).reshape(-1, D), whole_weight, NT,
        preferred_element_type=jnp.float32,
    )
    d_row_out = d_flat.astype(jnp.bfloat16).reshape(images * row_count, G, D)
    (row_sums,) = attention_backward(p_row, rows(v_row), d_row_out, False)
    row_table = fold(row_sums, col_positions)

    batch_size = lax.axis_size("dp") * images
    table_grad = (row_table + col_table)[:, :NOFF] / (batch_size * G)
    pre_grad = table_grad * 16.0 * squashed * (1.0 - squashed)
    grad_out = lax.dot_general(
        hidden_units, pre_grad, (((0,), (1,)), ((), ())), precision=PRECISE
    )
    back_units = lax.dot_general(pre_grad, all_out, (((0,), (1,)), ((), ())), precision=PRECISE)
    unit_grad = jnp.where(pre_act > 0, back_units, 0.0)
    grad_in = jnp.sum(unit_grad * coords[:, None], axis=0)
    grad_bias = jnp.sum(unit_grad, axis=0)
    grad_mlp_out, grad_mlp_in, grad_mlp_bias = reduce_units(grad_out, grad_in, grad_bias)
    return (attended, grad_mlp_in, grad_mlp_bias, grad_mlp_out)


def solution(mesh):
    return jax.shard_map(
        shards,
        mesh=mesh,
        in_specs=(
            P("dp", "grid", None, None),
            P("dp", "grid", None, None),
            P("dp", "grid", None, None),
            P("dp", None, "grid", None),
            P("dp", None, "grid", None),
            P("dp", None, "grid", None),
            P(("dp", "grid"), None),
            P(),
            P(),
            P("grid"),
            P("grid"),
            P("grid", None),
        ),
        out_specs=(P("dp", None, "grid", None), P("grid"), P("grid"), P("grid", None)),
        check_vma=False,
    )
```

time: 489 us -> 238 us (0.49); the launches traced: 480 us -> 237 us
  blocking collectives: 224 us -> 48.5 us
  matrix products: 132 us -> 11.4 us
  Pallas kernels: 0 us -> 70 us
  local copies, waits for them, and re-layouts: 92.6 us -> 25.5 us
  waiting for transfers between devices: 0.69 us -> 43 us
  between operations: 14.5 us -> 0.9 us
  starting transfers between devices: 15.2 us -> 26.4 us
  other arithmetic: 0.9 us -> 10.9 us
    psum x2 -> x0, blocking collectives: 224 us -> none  [the longest x1 119 us: shards(): table_pre = lax.psum(partial_table, 'grid')]
    dot_general x14 -> x5, matrix products: 81.5 us -> 11.4 us  [the longest x1 4.07 us: shards(): jnp.dot(cols(col_out).reshape(-1, D), whole_weight, preferred_element_typ...]
    pallas_call x0 -> x8, Pallas kernels: none -> 70 us  [the longest x2 25.2 us: attention_forward(): pl.pallas_call(functools.partial(forward_kernel, transpose=transpose), gr...]
    sub x4 -> x0, matrix products: 50.8 us -> none  [the longest x2 28.2 us: soft_grad(): d_probs - jnp.sum(attn_probs * d_probs, axis=-1, keepdims=True)]
    all_to_all x0 -> x3, blocking collectives: none -> 48.5 us  [the longest x1 21 us: gather_units(): lax.all_to_all(jnp.broadcast_to(tile[None], (GRID, 8, 128)), 'grid', 0, 0...]
    reshape x13 -> x7, local copies, waits for them, and re-layouts: 46.1 us -> 10.6 us  [the longest x1 4.53 us: shards(): d_values.reshape(images, col_count, G, D)]
    unnamed x42 -> x23, local copies, waits for them, and re-layouts: 31.6 us -> 2.16 us
    ppermute x0 -> x4, waiting for transfers between devices: none -> 24 us  [the longest x3 24 us: fetch_weight(): mine.append(lax.ppermute(part, 'dp', along_x(step, 0)))]
  transfers between devices with their start and end apart: 3 -> 7, of which waited for: 0 -> 5; matrix products, arithmetic and copies ran while one was open for 26% -> 10% of each run, Pallas kernels for 0% -> 15%
where the time goes in v1:
time: 238 us; the launch traced here: 237 us
  Pallas kernels  70 us (29%)
  blocking collectives  48.5 us (20%)
  waiting for transfers between devices  43 us (18%)
  starting transfers between devices  26.4 us (11%)
  local copies, waits for them, and re-layouts  25.5 us (11%)
  matrix products  11.4 us (5%)
  other arithmetic  10.9 us (5%)
    pallas_call x2, Pallas kernels, attention_forward(): pl.pallas_call(functools.partial(forward_kernel, transpose=transpose), gr...  25.2 us
    ppermute x3, waiting for transfers between devices, fetch_weight(): mine.append(lax.ppermute(part, 'dp', along_x(step, 0)))  24 us
    all_to_all x1, blocking collectives, gather_units(): lax.all_to_all(jnp.broadcast_to(tile[None], (GRID, 8, 128)), 'grid', 0, 0...  21 us
    pallas_call x2, Pallas kernels, attention_backward(): pl.pallas_call(functools.partial(backward_kernel, attend=attend), grid=(n...  20.4 us
    all_to_all x1, waiting for transfers between devices, shards(): lax.all_to_all(d_values.reshape(images, col_count, G, D), 'grid', split_a...  19 us
    all_to_all x1, blocking collectives, reduce_units(): got = lax.all_to_all(tiles, 'grid', 0, 0, tiled=True)  18.7 us
    pallas_call x2, Pallas kernels, fold(): pl.pallas_call(fold_kernel, in_specs=[pl.BlockSpec(memory_space=pltpu.SME...  14.6 us
    pallas_call x2, Pallas kernels, expand(): pl.pallas_call(expand_kernel, in_specs=[pl.BlockSpec(memory_space=pltpu.S...  9.93 us
  transfers between devices with their start and end apart: 7, of which 5 were waited for; matrix products, arithmetic and copies ran while one was open for 10% of the time, Pallas kernels for 15%

profile of v1, /device:TPU:1, one launch (start us, length us, event | category | flops | bytes accessed | tf_op | source)
XLA Modules:
  0.0 236.7 jit_solution(8097188206689804164)
XLA Ops:
  0.6 0.0 copy-start.8
  0.7 0.7 copy.38
  1.4 0.7 copy.39
  2.1 0.8 pad_maximum_fusion.2
  2.9 0.1 reshape.91
  3.0 21.0 %all_to_all.56 = f32[32,8,128]{2,1,0:T(8,128)S(1)} all-to-all(f32[32,8,128]{2,1,0:T(8,128)S(1)} %broadcast_in_dim.74), channel_id=1, replica_groups=mesh['dp'=8,'grid'=32] {'grid'}, dimensions={0} | all-to-all | bytes 262144 | tf_op jit(solution)/shard_map/all_to_all | solution.py:236
  24.0 1.7 broadcast_in_dim.77
  25.7 3.9 %all-to-all-start.2 = ((bf16[32,6,1536]{2,1,0:T(8,128)(2,1)}), bf16[32,6,1536]{2,1,0:T(8,128)(2,1)S(1)}, u32[]{:S(2)}, u32[]{:S(2)}) async-start(bf16[32,6,1536]{2,1,0:T(8,128)(2,1)} %broadcast_in_dim.77), calls=%async_computation.2 | async-start | bytes 1572864 | tf_op jit(solution)/shard_map/all_to_all | solution.py:258
  29.6 0.5 pad_bitcast_fusion.2
  30.2 0.2 reshape.93
  30.4 0.4 slice_reduce_fusion.1
  30.8 0.6 broadcast_multiply_fusion
  31.4 0.6 pad.20.table_ref
  32.0 5.0 %shard_map.147.bias_ref = f32[4608,128]{1,0:T(8,128)} custom-call(s32[96]{0:T(128)} %pos_ref.7, f32[48,256]{1,0:T(8,128)} %pad.20.table_ref, s32[1,128]{1,0:T(1,128)} %get-tuple-element.27.lane_ref), custom_call_target="tpu_custom_call" | custom-call | tf_op jit(solution)/shard_map/pallas_call | solution.py:177
  37.0 12.6 %shard_map.148 = (bf16[6,4608,96]{2,1,0:T(8,128)(2,1)}, bf16[6,96,1536]{2,1,0:T(8,128)(2,1)}) custom-call(bf16[6,96,1536]{2,1,0:T(8,128)(2,1)} %bitcast.101, bf16[6,96,1536]{2,1,0:T(8,128)(2,1)} %bitcast.102, bf16[6,96,1536]{2,1,0:T(8,128)(2,1)} %bitcast.107, f32[4608,128]{1,0:T(8,128)} %shard_map.147.bias_ref), custom_call_target="tpu_custom_call" | custom-call | flops 5435817984 | bytes 20000000 | tf_op jit(solution)/shard_map/pallas_call | solution.py:133
  49.6 4.5 %copy.44 = bf16[2,3,96,1536]{3,0,1,2:T(2,128)(2,1)} copy(bf16[2,3,96,1536]{3,2,1,0:T(8,128)(2,1)} %bitcast.86) | data formatting | bytes 3538944 | tf_op jit(solution)/shard_map/reshape | solution.py:304
  54.2 9.2 %all-to-all-start.3 = ((bf16[2,3,96,1536]{3,0,1,2:T(2,128)(2,1)}), bf16[2,3,96,1536]{3,0,1,2:T(2,128)(2,1)S(1)}, u32[]{:S(2)}, u32[]{:S(2)}) async-start(bf16[2,3,96,1536]{3,0,1,2:T(2,128)(2,1)} %copy.44), calls=%async_computation.3 | async-start | bytes 3538944 | tf_op jit(solution)/shard_map/all_to_all | solution.py:303
  63.4 4.9 %shard_map.149.bias_ref = f32[4608,128]{1,0:T(8,128)} custom-call(s32[96]{0:T(128)} %pos_ref.6, f32[48,256]{1,0:T(8,128)} %pad.20.table_ref, s32[1,128]{1,0:T(1,128)} %get-tuple-element.26.lane_ref), custom_call_target="tpu_custom_call" | custom-call | tf_op jit(solution)/shard_map/pallas_call | solution.py:177
  68.3 12.6 %shard_map.150 = (bf16[6,4608,96]{2,1,0:T(8,128)(2,1)}, bf16[6,96,1536]{2,1,0:T(8,128)(2,1)}) custom-call(bf16[6,96,1536]{2,1,0:T(8,128)(2,1)} %bitcast.103, bf16[6,96,1536]{2,1,0:T(8,128)(2,1)} %bitcast.104, bf16[6,96,1536]{2,1,0:T(8,128)(2,1)} %bitcast.105, f32[4608,128]{1,0:T(8,128)} %shard_map.149.bias_ref), custom_call_target="tpu_custom_call" | custom-call | flops 5435817984 | bytes 20000000 | tf_op jit(solution)/shard_map/pallas_call | solution.py:133
  80.9 4.5 %copy.40 = bf16[2,3,96,1536]{3,0,1,2:T(2,128)(2,1)} copy(bf16[2,3,96,1536]{3,2,1,0:T(8,128)(2,1)} %bitcast.87) | data formatting | bytes 3538944 | tf_op jit(solution)/shard_map/reshape | solution.py:297
  85.4 19.0 %all-to-all-done.3 = bf16[2,3,96,1536]{3,0,1,2:T(2,128)(2,1)S(1)} async-done(((bf16[2,3,96,1536]{3,0,1,2:T(2,128)(2,1)}), bf16[2,3,96,1536]{3,0,1,2:T(2,128)(2,1)S(1)}, u32[]{:S(2)}, u32[]{:S(2)}) %all-to-all-start.3) | async-done | bytes 1769504 | tf_op jit(solution)/shard_map/all_to_all | solution.py:303
  104.4 6.4 %all-to-all-start.1 = ((bf16[2,3,96,1536]{3,0,1,2:T(2,128)(2,1)}), bf16[2,3,96,1536]{3,0,1,2:T(2,128)(2,1)}, u32[]{:S(2)}, u32[]{:S(2)}) async-start(bf16[2,3,96,1536]{3,0,1,2:T(2,128)(2,1)} %copy.40), calls=%async_computation.1 | async-start | bytes 3538944 | tf_op jit(solution)/shard_map/all_to_all | solution.py:296
  110.8 1.0 reshape.98
  111.9 1.2 collective-permute-start
  113.1 2.4 %collective-permute-start.1 = (bf16[192,1536]{1,0:T(8,128)(2,1)}, bf16[192,1536]{1,0:T(8,128)(2,1)S(1)}, u32[]{:S(2)}, u32[]{:S(2)}) collective-permute-start(bf16[192,1536]{1,0:T(8,128)(2,1)} %reshape.98), channel_id=1, source_target_pairs={{0,128},{32,160},{64,192},{96,224},{128,0},{160,32},{192,64},{224,... | collective-permute-start | bytes 1769480 | tf_op jit(solution)/shard_map/ppermute | solution.py:263
  115.5 1.2 collective-permute-start.2
  116.7 0.2 stack_reshape.3
  116.9 8.6 %collective-permute-done = bf16[192,1536]{1,0:T(8,128)(2,1)} collective-permute-done((bf16[192,1536]{1,0:T(8,128)(2,1)}, bf16[192,1536]{1,0:T(8,128)(2,1)}, u32[]{:S(2)}, u32[]{:S(2)}) %collective-permute-start) | collective-permute-done | bytes 589856 | tf_op jit(solution)/shard_map/ppermute | solution.py:263
  125.5 13.6 %collective-permute-done.1 = bf16[192,1536]{1,0:T(8,128)(2,1)S(1)} collective-permute-done((bf16[192,1536]{1,0:T(8,128)(2,1)}, bf16[192,1536]{1,0:T(8,128)(2,1)S(1)}, u32[]{:S(2)}, u32[]{:S(2)}) %collective-permute-start.1) | collective-permute-done | bytes 589856 | tf_op jit(solution)/shard_map/ppermute | solution.py:263
  139.1 1.7 collective-permute-done.2
  140.8 0.8 copy-done.3
  141.7 2.8 %fusion.33 = (bf16[1,4,192,1536]{3,2,1,0:T(8,128)(2,1)S(1)}, bf16[4,192,1536]{2,1,0:T(8,128)(2,1)}) fusion(bf16[1,192,1536]{2,1,0:T(8,128)(2,1)} %bitcast.89, bf16[1,192,1536]{2,1,0:T(8,128)(2,1)} %bitcast.88, bf16[1,192,1536]{2,1,0:T(8,128)(2,1)} %bitcast.21, bf16[1,192,1536]{2,1,0:T(8,128)(2,1)S(1)} %stack_reshape.3), kind=kLoop, calls=%fused_computation.78 | loop fusion | flops 3538944 | bytes 7077888 | tf_op jit(solution)/shard_map/stack | solution.py:266
  144.5 2.0 collective-permute-start.3
  146.5 0.6 select_reduce_fusion.1
  147.1 0.6 select_reduce_fusion
  147.8 2.7 %copy.46 = bf16[2,32,3,3,1536]{4,0,3,2,1:T(2,128)(2,1)S(1)} copy(bf16[2,32,3,3,1536]{4,0,2,3,1:T(2,128)(2,1)} %bitcast.81) | data formatting | bytes 3538944 | tf_op jit(solution)/shard_map/all_to_all | solution.py:303
  150.4 1.4 copy.47
  151.9 0.1 all-to-all-done.1
  151.9 2.7 %copy.42 = bf16[2,32,3,3,1536]{4,0,3,2,1:T(2,128)(2,1)S(1)} copy(bf16[2,32,3,3,1536]{4,0,2,3,1:T(2,128)(2,1)} %bitcast.17) | data formatting | bytes 3538944 | tf_op jit(solution)/shard_map/all_to_all | solution.py:296
  154.6 0.2 copy.43
  154.8 1.3 bitcast_dynamic-update-slice_fusion.7
  156.1 0.2 bitcast_dynamic-update-slice_fusion.6
  156.4 1.3 bitcast_dynamic-update-slice_fusion.5
  157.7 0.2 bitcast_dynamic-update-slice_fusion.4
  157.9 1.3 bitcast_dynamic-update-slice_fusion.3
  159.2 0.2 bitcast_dynamic-update-slice_fusion.2
  159.4 1.3 bitcast_dynamic-update-slice_fusion.1
  160.7 0.2 bitcast_dynamic-update-slice_fusion
  161.0 1.2 copy-done.1
  162.2 4.1 %convolution_convert_fusion = bf16[576,1536]{1,0:T(8,128)(2,1)} fusion(bf16[576,1536]{1,0:T(8,128)(2,1)S(1)} %bitcast.84, bf16[1536,1536]{1,0:T(8,128)(2,1)S(1)} %bitcast_dynamic-update-slice_fusion), kind=kOutput, calls=%fused_computation.16 | convolution fusion | flops 2718793728 | bytes 8257536 | tf_op jit(solution)/shard_map/dot_general | solution.py:314
  166.3 4.1 %convolution_convert_fusion.1 = bf16[576,1536]{1,0:T(8,128)(2,1)} fusion(bf16[576,1536]{1,0:T(8,128)(2,1)S(1)} %bitcast.85, bf16[1536,1536]{1,0:T(8,128)(2,1)S(1)} %bitcast_dynamic-update-slice_fusion), kind=kOutput, calls=%fused_computation.17 | convolution fusion | flops 2718793728 | bytes 8257536 | tf_op jit(solution)/shard_map/dot_general | solution.py:307
  170.3 9.9 %shard_map.152.sum_ref = f32[4608,128]{1,0:T(8,128)} custom-call(bf16[6,4608,96]{2,1,0:T(8,128)(2,1)} %get-tuple-element.13.p_ref, bf16[6,96,1536]{2,1,0:T(8,128)(2,1)} %bitcast.106, bf16[6,96,1536]{2,1,0:T(8,128)(2,1)} %bitcast.111), custom_call_target="tpu_custom_call" | custom-call | flops 5435817984 | bytes 20000000 | tf_op jit(solution)/shard_map/pallas_call | solution.py:150
  180.2 7.3 %shard_map.153 = f32[48,256]{1,0:T(8,128)} custom-call(s32[96]{0:T(128)} %pos_ref.6, f32[4608,128]{1,0:T(8,128)} %shard_map.152.sum_ref, s32[1,128]{1,0:T(1,128)} %bitcast.98), custom_call_target="tpu_custom_call" | custom-call | tf_op jit(solution)/shard_map/pallas_call | solution.py:207
  187.5 10.4 %shard_map.151 = (bf16[6,96,1536]{2,1,0:T(8,128)(2,1)}, f32[4608,128]{1,0:T(8,128)}) custom-call(bf16[6,4608,96]{2,1,0:T(8,128)(2,1)} %get-tuple-element.10.p_ref, bf16[6,96,1536]{2,1,0:T(8,128)(2,1)} %bitcast.110, bf16[6,96,1536]{2,1,0:T(8,128)(2,1)} %bitcast.108), custom_call_target="tpu_custom_call" | custom-call | flops 5435817984 | bytes 20000000 | tf_op jit(solution)/shard_map/pallas_call | solution.py:150
  198.0 7.3 %shard_map.154 = f32[48,256]{1,0:T(8,128)} custom-call(s32[96]{0:T(128)} %pos_ref.7, f32[4608,128]{1,0:T(8,128)} %get-tuple-element.15.sum_ref, s32[1,128]{1,0:T(1,128)} %bitcast.97), custom_call_target="tpu_custom_call" | custom-call | tf_op jit(solution)/shard_map/pallas_call | solution.py:207
  205.3 1.3 fusion.13
  206.6 1.4 multiply_reduce_fusion
  208.0 0.1 copy.48
  208.1 0.1 reshape.104
  208.3 18.7 %all_to_all.57 = f32[32,8,128]{2,1,0:T(8,128)S(1)} all-to-all(f32[32,8,128]{2,1,0:T(8,128)S(1)} %bitcast.91), channel_id=1, replica_groups=mesh['dp'=8,'grid'=32] {'grid'}, dimensions={0} | all-to-all | bytes 262144 | tf_op jit(solution)/shard_map/all_to_all | solution.py:246
  227.0 8.8 %all_to_all.58 = f32[8,8,128]{2,1,0:T(8,128)S(1)} all-to-all(f32[8,8,128]{2,1,0:T(8,128)S(1)} %broadcast_in_dim.85), channel_id=1, replica_groups=mesh['dp'=8,'grid'=32] {'dp'}, dimensions={0} | all-to-all | bytes 65536 | tf_op jit(solution)/shard_map/all_to_all | solution.py:248
  235.9 0.1 reshape.107
  235.9 0.0 copy-start.4
  236.0 0.7 slice_reduce_fusion.2
  (29 shorter events, 0.2 us)
Async XLA Ops:
  0.6 29.0 %copy-start.8 = (s32[96]{0:T(128)S(1)}, s32[96]{0:T(128)}, u32[]{:S(2)}) copy-start(s32[96]{0:T(128)} %pos_ref.7) | copy-start | bytes 1156
  0.6 29.0 %copy-start.6 = (s32[96]{0:T(128)S(1)}, s32[96]{0:T(128)}, u32[]{:S(2)}) copy-start(s32[96]{0:T(128)} %pos_ref.6) | copy-start | bytes 1156
  25.7 28.5 %all-to-all-start.2 = ((bf16[32,6,1536]{2,1,0:T(8,128)(2,1)}), bf16[32,6,1536]{2,1,0:T(8,128)(2,1)S(1)}, u32[]{:S(2)}, u32[]{:S(2)}) async-start(bf16[32,6,1536]{2,1,0:T(8,128)(2,1)} %broadcast_in_dim.77), calls=%async_computation.2 | async-start | bytes 1572864 | tf_op jit(solution)/shard_map/all_to_all | solution.py:258
  54.2 50.2 %all-to-all-start.3 = ((bf16[2,3,96,1536]{3,0,1,2:T(2,128)(2,1)}), bf16[2,3,96,1536]{3,0,1,2:T(2,128)(2,1)S(1)}, u32[]{:S(2)}, u32[]{:S(2)}) async-start(bf16[2,3,96,1536]{3,0,1,2:T(2,128)(2,1)} %copy.44), calls=%async_computation.3 | async-start | bytes 3538944 | tf_op jit(solution)/shard_map/all_to_all | solution.py:303
  104.4 7.5 %copy-start = (bf16[2,3,96,1536]{3,0,1,2:T(2,128)(2,1)}, bf16[2,3,96,1536]{3,0,1,2:T(2,128)(2,1)S(1)}, u32[]{:S(2)}) copy-start(bf16[2,3,96,1536]{3,0,1,2:T(2,128)(2,1)S(1)} %all-to-all-done.3) | copy-start | bytes 5308420
  104.4 47.5 %all-to-all-start.1 = ((bf16[2,3,96,1536]{3,0,1,2:T(2,128)(2,1)}), bf16[2,3,96,1536]{3,0,1,2:T(2,128)(2,1)}, u32[]{:S(2)}, u32[]{:S(2)}) async-start(bf16[2,3,96,1536]{3,0,1,2:T(2,128)(2,1)} %copy.40), calls=%async_computation.1 | async-start | bytes 3538944 | tf_op jit(solution)/shard_map/all_to_all | solution.py:296
  111.9 13.6 %collective-permute-start = (bf16[192,1536]{1,0:T(8,128)(2,1)}, bf16[192,1536]{1,0:T(8,128)(2,1)}, u32[]{:S(2)}, u32[]{:S(2)}) collective-permute-start(bf16[192,1536]{1,0:T(8,128)(2,1)} %reshape.98), channel_id=1, source_target_pairs={{0,64},{32,96},{64,128},{96,160},{128,192},{160,224},{192,0},{224,... | collective-permute-start | bytes 1769480 | tf_op jit(solution)/shard_map/ppermute | solution.py:263
  113.1 26.0 %collective-permute-start.1 = (bf16[192,1536]{1,0:T(8,128)(2,1)}, bf16[192,1536]{1,0:T(8,128)(2,1)S(1)}, u32[]{:S(2)}, u32[]{:S(2)}) collective-permute-start(bf16[192,1536]{1,0:T(8,128)(2,1)} %reshape.98), channel_id=1, source_target_pairs={{0,128},{32,160},{64,192},{96,224},{128,0},{160,32},{192,64},{224,... | collective-permute-start | bytes 1769480 | tf_op jit(solution)/shard_map/ppermute | solution.py:263
  115.5 25.3 %collective-permute-start.2 = (bf16[192,1536]{1,0:T(8,128)(2,1)}, bf16[192,1536]{1,0:T(8,128)(2,1)S(1)}, u32[]{:S(2)}, u32[]{:S(2)}) collective-permute-start(bf16[192,1536]{1,0:T(8,128)(2,1)} %reshape.98), channel_id=1, source_target_pairs={{0,192},{32,224},{64,0},{96,32},{128,64},{160,96},{192,128},{224,1... | collective-permute-start | bytes 1769480 | tf_op jit(solution)/shard_map/ppermute | solution.py:263
  139.1 1.7 copy-start.2
  140.8 0.8 copy-start.3
  141.7 4.9 %copy-start.7 = (s32[96]{0:T(128)S(1)}, s32[96]{0:T(128)}, u32[]{:S(2)}) copy-start(s32[96]{0:T(128)} %pos_ref.6) | copy-start | bytes 1156
  141.7 5.5 %copy-start.9 = (s32[96]{0:T(128)S(1)}, s32[96]{0:T(128)}, u32[]{:S(2)}) copy-start(s32[96]{0:T(128)} %pos_ref.7) | copy-start | bytes 1156
  144.5 10.3 %collective-permute-start.3 = (bf16[4,192,1536]{2,1,0:T(8,128)(2,1)}, bf16[4,192,1536]{2,1,0:T(8,128)(2,1)}, u32[]{:S(2)}, u32[]{:S(2)}) collective-permute-start(bf16[4,192,1536]{2,1,0:T(8,128)(2,1)} %get-tuple-element.23), channel_id=1, source_target_pairs={{0,32},{32,0},{64,96},{96,64},{128,160},{160,128},{192,224},{224,1... | collective-permute-start | bytes 7077896 | tf_op jit(solution)/shard_map/ppermute | solution.py:265
  160.7 1.5 copy-start.1
  198.0 7.3 %copy-start.5 = (f32[48,256]{1,0:T(8,128)S(1)}, f32[48,256]{1,0:T(8,128)}, u32[]{:S(2)}) copy-start(f32[48,256]{1,0:T(8,128)} %shard_map.153) | copy-start | bytes 147460
  235.9 0.7 copy-start.4

commit v2 on v1

--- a/solution.py
+++ b/solution.py
@@ -2,11 +2,11 @@
 
 import jax
 import jax.numpy as jnp
-import numpy as np
 from jax import lax
 from jax.experimental import pallas as pl
 from jax.experimental.pallas import tpu as pltpu
 from jax.sharding import PartitionSpec as P
+
 
 G = 96
 D = 1536
@@ -58,8 +58,29 @@
     return p.reshape(STACK * G, G).astype(jnp.bfloat16)
 
 
-def forward_kernel(q_ref, k_ref, x_ref, bias_ref, p_ref, o_ref, *, transpose):
+def pick(row, index):
+    return jnp.take_along_axis(row, index, axis=1, mode="promise_in_bounds")
+
+
+def forward_kernel(q_ref, k_ref, x_ref, table_ref, level_ref, p_ref, o_ref, bias_ref, *, transpose):
     masks = head_masks()
+
+    @pl.when(pl.program_id(0) == 0)
+    def _():
+        level = level_ref[...]
+        index = jnp.bitwise_and(level, LANES - 1)
+        high = level >= LANES
+
+        def spread(block, carry):
+            table = table_ref[pl.ds(pl.multiple_of(block * 8, 8), 8), :]
+            for j in range(8):
+                low = jnp.broadcast_to(table[j:j + 1, :LANES], (G, LANES))
+                up = jnp.broadcast_to(table[j:j + 1, LANES:], (G, LANES))
+                rows = pl.ds(pl.multiple_of((block * 8 + j) * G, G), G)
+                bias_ref[rows, :] = jnp.where(high, pick(up, index), pick(low, index))
+            return carry
+
+        lax.fori_loop(0, NH // 8, spread, 0)
 
     def body(g, carry):
         sl = lane_group(g)
@@ -85,8 +106,8 @@
     lax.fori_loop(0, GROUPS, body, 0, unroll=UNROLL)
 
 
-def backward_kernel(p_ref, v_ref, g_ref, *outs, attend):
-    sum_ref = outs[-1]
+def backward_kernel(p_ref, v_ref, g_ref, index_ref, *outs, attend):
+    fold_ref, sum_ref = outs[-2:]
     masks = head_masks()
 
     @pl.when(pl.program_id(0) == 0)
@@ -115,6 +136,23 @@
 
     lax.fori_loop(0, GROUPS, body, 0, unroll=UNROLL)
 
+    @pl.when(pl.program_id(0) == pl.num_programs(0) - 1)
+    def _():
+        low, high = index_ref[:, :LANES], index_ref[:, LANES:]
+
+        def gather(block, carry):
+            lows, highs = [], []
+            for j in range(8):
+                own = sum_ref[pl.ds(pl.multiple_of((block * 8 + j) * G, G), G), :]
+                lows.append(jnp.sum(pick(own, low), axis=0, keepdims=True))
+                highs.append(jnp.sum(pick(own, high), axis=0, keepdims=True))
+            rows = pl.ds(pl.multiple_of(block * 8, 8), 8)
+            fold_ref[rows, :LANES] = jnp.concatenate(lows, axis=0)
+            fold_ref[rows, LANES:] = jnp.concatenate(highs, axis=0)
+            return carry
+
+        lax.fori_loop(0, NH // 8, gather, 0)
+
 
 BLOCK = (1, G, D)
 PSHAPE = (1, NH * G, G)
@@ -128,92 +166,69 @@
     return pl.BlockSpec(shape, lambda i: (0,) * len(shape))
 
 
-def attention_forward(q, k, x, bias, transpose):
+def attention_forward(q, k, x, table, level, transpose):
     n = q.shape[0]
     return pl.pallas_call(
         functools.partial(forward_kernel, transpose=transpose),
         grid=(n,),
-        in_specs=[each(BLOCK)] * 3 + [whole((NH * G, LANES))],
+        in_specs=[each(BLOCK)] * 3 + [whole((NH, 2 * LANES)), whole((G, LANES))],
         out_specs=[each(PSHAPE), each(BLOCK)],
         out_shape=[
             jax.ShapeDtypeStruct((n, NH * G, G), jnp.bfloat16),
             jax.ShapeDtypeStruct((n, G, D), jnp.bfloat16),
         ],
-        cost_estimate=pl.CostEstimate(flops=n * NH * 16 * G * G * LANES, transcendentals=n * NH * G * G, bytes_accessed=20_000_000),
-    )(q, k, x, bias)
-
-
-def attention_backward(p, v, g, attend):
+        scratch_shapes=[pltpu.VMEM((NH * G, LANES), jnp.float32)],
+        cost_estimate=pl.CostEstimate(
+            flops=n * NH * 16 * G * G * LANES, transcendentals=n * NH * G * G, bytes_accessed=20_000_000
+        ),
+    )(q, k, x, table, level)
+
+
+def attention_backward(p, v, g, index, attend):
     n = p.shape[0]
     specs = [each(BLOCK)] if attend else []
     shapes = [jax.ShapeDtypeStruct((n, G, D), jnp.bfloat16)] if attend else []
     return pl.pallas_call(
         functools.partial(backward_kernel, attend=attend),
         grid=(n,),
-        in_specs=[each(PSHAPE), each(BLOCK), each(BLOCK)],
-        out_specs=specs + [whole((NH * G, LANES))],
-        out_shape=shapes + [jax.ShapeDtypeStruct((NH * G, LANES), jnp.float32)],
-        cost_estimate=pl.CostEstimate(flops=n * NH * 16 * G * G * LANES, transcendentals=0, bytes_accessed=20_000_000),
-    )(p, v, g)
-
-
-def expand_kernel(pos_ref, table_ref, lane_ref, out_ref):
-    low, high = table_ref[:, :LANES], table_ref[:, LANES:]
-    lane = jnp.broadcast_to(lane_ref[...], (NH, LANES)) + (G - 1)
-
-    def body(b, carry):
-        level = lane - pos_ref[b]
-        index = jnp.bitwise_and(level, LANES - 1)
-        x = jnp.take_along_axis(low, index, axis=1, mode="promise_in_bounds")
-        y = jnp.take_along_axis(high, index, axis=1, mode="promise_in_bounds")
-        out_ref[pl.ds(b, NH, stride=G), :] = jnp.where(level >= LANES, y, x)
-        return carry
-
-    lax.fori_loop(0, G, body, 0, unroll=16)
-
-
-def expand(table, positions):
-    lane = jnp.pad(positions, (0, LANES - G))[None]
+        in_specs=[each(PSHAPE), each(BLOCK), each(BLOCK), whole((G, 2 * LANES))],
+        out_specs=specs + [whole((NH, 2 * LANES))],
+        out_shape=shapes + [jax.ShapeDtypeStruct((NH, 2 * LANES), jnp.float32)],
+        scratch_shapes=[pltpu.VMEM((NH * G, LANES), jnp.float32)],
+        cost_estimate=pl.CostEstimate(
+            flops=n * NH * 16 * G * G * LANES, transcendentals=0, bytes_accessed=20_000_000
+        ),
+    )(p, v, g, index)
+
+
+def levels(positions):
+    level = positions[None, :] - positions[:, None] + (G - 1)
+    return jnp.pad(level, ((0, 0), (0, LANES - G)))
+
+
+def fold_index(positions):
+    level = positions[None, :] - positions[:, None] + (G - 1)
+    hit = level[:, :, None] == jnp.arange(2 * LANES)[None, None, :]
+    spot = jnp.arange(G, dtype=jnp.int32)[None, :, None] - (LANES - 1)
+    return jnp.sum(jnp.where(hit, spot, 0), axis=1) + (LANES - 1)
+
+
+def assemble_kernel(start_ref, *refs):
+    out_ref = refs[-1]
+    for j in range(DP):
+        first = pl.multiple_of(start_ref[j], D // DP)
+        out_ref[pl.ds(first, D // DP), :] = refs[j][...]
+
+
+def assemble(parts, starts):
     return pl.pallas_call(
-        expand_kernel,
-        in_specs=[
-            pl.BlockSpec(memory_space=pltpu.SMEM),
-            pl.BlockSpec(memory_space=pltpu.VMEM),
-            pl.BlockSpec(memory_space=pltpu.VMEM),
-        ],
+        assemble_kernel,
+        in_specs=[pl.BlockSpec(memory_space=pltpu.SMEM)] + [pl.BlockSpec(memory_space=pltpu.VMEM)] * DP,
         out_specs=pl.BlockSpec(memory_space=pltpu.VMEM),
-        out_shape=jax.ShapeDtypeStruct((NH * G, LANES), jnp.float32),
-    )(positions, table, lane)
-
-
-def fold_kernel(pos_ref, sum_ref, lane_ref, out_ref):
-    lane = jnp.broadcast_to(lane_ref[...], (NH, LANES))
-    keep = lax.broadcasted_iota(jnp.int32, (NH, LANES), 1) < G
-    zero = jnp.zeros((NH, LANES), jnp.float32)
-
-    def body(b, total):
-        one = sum_ref[pl.ds(b, NH, stride=G), :]
-        one = jnp.take_along_axis(one, lane, axis=1, mode="promise_in_bounds")
-        one = jnp.concatenate([jnp.where(keep, one, 0.0), zero], axis=1)
-        return total + pltpu.roll(one, (G - 1) - pos_ref[b], 1)
-
-    out_ref[...] = lax.fori_loop(0, G, body, jnp.zeros((NH, 2 * LANES), jnp.float32), unroll=4)
-
-
-def fold(sums, positions):
-    inverse = jnp.sum(
-        jnp.where(positions[None, :] == jnp.arange(LANES)[:, None], jnp.arange(G)[None, :], 0), axis=1
-    ).astype(jnp.int32)[None]
-    return pl.pallas_call(
-        fold_kernel,
-        in_specs=[
-            pl.BlockSpec(memory_space=pltpu.SMEM),
-            pl.BlockSpec(memory_space=pltpu.VMEM),
-            pl.BlockSpec(memory_space=pltpu.VMEM),
-        ],
-        out_specs=pl.BlockSpec(memory_space=pltpu.VMEM),
-        out_shape=jax.ShapeDtypeStruct((NH, 2 * LANES), jnp.float32),
-    )(positions, sums, inverse)
+        out_shape=jax.ShapeDtypeStruct((D, D), jnp.bfloat16),
+        cost_estimate=pl.CostEstimate(flops=0, transcendentals=0, bytes_accessed=2 * D * D * 2),
+    )(starts, *parts)
+
 
 def offset_coords():
     delta = jnp.arange(NOFF, dtype=jnp.float32) - (G - 1)
@@ -261,16 +276,14 @@
     mine = [part]
     for step in (1, 2, 3):
         mine.append(lax.ppermute(part, "dp", along_x(step, 0)))
-    mine = jnp.stack(mine)
-    other = lax.ppermute(mine, "dp", along_x(0, 1))
-    both = jnp.stack([mine, other])
+    other = []
+    for step in range(4):
+        other.append(lax.ppermute(mine[step], "dp", along_x(0, 1)))
     here = lax.axis_index("dp")
     x, core = here // 2, here % 2
-    blocks = []
-    for target in range(DP):
-        tx, tc = target // 2, target % 2
-        blocks.append(both[jnp.bitwise_xor(core, tc), (x - tx) % 4])
-    return jnp.concatenate(blocks, axis=0)
+    order = (x - jnp.arange(4)) % 4 * 2
+    starts = jnp.concatenate([order + core, order + (1 - core)]) * (D // DP)
+    return assemble(mine + other, starts.astype(jnp.int32))
 
 
 def shards(
@@ -291,15 +304,17 @@
 
     rows = lambda x: x.reshape(images * row_count, G, D)
     cols = lambda x: x.transpose(0, 2, 1, 3).reshape(images * col_count, G, D)
-    bias_row = expand(table, col_positions)
-    p_row, row_out = attention_forward(rows(q_row), rows(k_row), rows(v_row), bias_row, False)
+    p_row, row_out = attention_forward(
+        rows(q_row), rows(k_row), rows(v_row), table, levels(col_positions), False
+    )
     col_out = lax.all_to_all(
         row_out.reshape(images, row_count, G, D), "grid", split_axis=2, concat_axis=1, tiled=True
     )
 
-    bias_col = expand(table, row_positions)
     grad_cols = cols(cotangent)
-    p_col, d_values = attention_forward(cols(q_col), cols(k_col), grad_cols, bias_col, True)
+    p_col, d_values = attention_forward(
+        cols(q_col), cols(k_col), grad_cols, table, levels(row_positions), True
+    )
     d_rows = lax.all_to_all(
         d_values.reshape(images, col_count, G, D), "grid", split_axis=2, concat_axis=1, tiled=True
     )
@@ -307,17 +322,19 @@
     value_cols = jnp.dot(
         cols(col_out).reshape(-1, D), whole_weight, preferred_element_type=jnp.float32
     ).astype(jnp.bfloat16).reshape(images * col_count, G, D)
-    attended, col_sums = attention_backward(p_col, value_cols, grad_cols, True)
+    attended, col_table = attention_backward(
+        p_col, value_cols, grad_cols, fold_index(row_positions), True
+    )
     attended = attended.reshape(images, col_count, G, D).transpose(0, 2, 1, 3)
-    col_table = fold(col_sums, row_positions)
 
     d_flat = lax.dot_general(
         d_rows.transpose(0, 2, 1, 3).reshape(-1, D), whole_weight, NT,
         preferred_element_type=jnp.float32,
     )
     d_row_out = d_flat.astype(jnp.bfloat16).reshape(images * row_count, G, D)
-    (row_sums,) = attention_backward(p_row, rows(v_row), d_row_out, False)
-    row_table = fold(row_sums, col_positions)
+    (row_table,) = attention_backward(
+        p_row, rows(v_row), d_row_out, fold_index(col_positions), False
+    )
 
     batch_size = lax.axis_size("dp") * images
     table_grad = (row_table + col_table)[:, :NOFF] / (batch_size * G)

time: 238 us -> 228 us (0.958)
  starting transfers between devices: 26.4 us -> 37.4 us
  waiting for transfers between devices: 43 us -> 32.1 us
  Pallas kernels: 70 us -> 61.9 us
    pallas_call x4 -> x1, Pallas kernels: 24.5 us -> 4.74 us  [assemble(): pl.pallas_call(assemble_kernel, in_specs=[pl.BlockSpec(memory_space=pltpu...]
    ppermute x3, waiting for transfers between devices: 24 us -> 12.3 us  [fetch_weight(): mine.append(lax.ppermute(part, 'dp', along_x(step, 0)))]
    ppermute x1 -> x4, starting transfers between devices: 2.04 us -> 13.2 us  [fetch_weight(): other.append(lax.ppermute(mine[step], 'dp', along_x(0, 1)))]
    reduce_sum x2 -> x1, other arithmetic: 1.21 us -> 7.48 us  [fold_index(): return jnp.sum(jnp.where(hit, spot, 0), axis=1) + (LANES - 1)]
    pallas_call x2, Pallas kernels: 20.4 us -> 26.5 us  [attention_backward(): pl.pallas_call(functools.partial(backward_kernel, attend=attend), grid=(n...]
    unnamed x7 -> x0, other arithmetic: 5.84 us -> none
    pallas_call x2, Pallas kernels: 25.2 us -> 30.7 us  [attention_forward(): pl.pallas_call(functools.partial(forward_kernel, transpose=transpose), gr...]
    another operation x1 -> x0, other arithmetic: 2.82 us -> none  [fetch_weight(): both = jnp.stack([mine, other])]
  transfers between devices with their start and end apart: 7 -> 10, of which waited for: 5 -> 3; matrix products, arithmetic and copies ran while one was open for 10% -> 11% of each run, Pallas kernels for 15% -> 16%
where the time goes in v2:
time: 228 us; the launch traced here: 227 us
  Pallas kernels  61.9 us (27%)
  blocking collectives  49.8 us (22%)
  starting transfers between devices  37.4 us (16%)
  waiting for transfers between devices  32.1 us (14%)
  local copies, waits for them, and re-layouts  23.2 us (10%)
  matrix products  12 us (5%)
  other arithmetic  9.79 us (4%)
    pallas_call x2, Pallas kernels, attention_forward(): pl.pallas_call(functools.partial(forward_kernel, transpose=transpose), gr...  30.7 us
    pallas_call x2, Pallas kernels, attention_backward(): pl.pallas_call(functools.partial(backward_kernel, attend=attend), grid=(n...  26.5 us
    all_to_all x1, blocking collectives, gather_units(): lax.all_to_all(jnp.broadcast_to(tile[None], (GRID, 8, 128)), 'grid', 0, 0...  21 us
    all_to_all x1, waiting for transfers between devices, shards(): lax.all_to_all(d_values.reshape(images, col_count, G, D), 'grid', split_a...  19.8 us
    all_to_all x1, blocking collectives, reduce_units(): got = lax.all_to_all(tiles, 'grid', 0, 0, tiled=True)  18.2 us
    ppermute x4, starting transfers between devices, fetch_weight(): other.append(lax.ppermute(mine[step], 'dp', along_x(0, 1)))  13.2 us
    ppermute x3, waiting for transfers between devices, fetch_weight(): mine.append(lax.ppermute(part, 'dp', along_x(step, 0)))  12.3 us
    all_to_all x1, blocking collectives, reduce_units(): lax.all_to_all(jnp.broadcast_to(own[None], (DP, 8, 128)), 'dp', 0, 0, til...  10.6 us
  transfers between devices with their start and end apart: 10, of which 3 were waited for; matrix products, arithmetic and copies ran while one was open for 11% of the time, Pallas kernels for 16%

profile of v2, /device:TPU:1, one launch (start us, length us, event | category | flops | bytes accessed | tf_op | source)
XLA Modules:
  0.0 227.3 jit_solution(18219710236528537868)
XLA Ops:
  0.6 0.7 copy.38
  1.4 0.7 copy.39
  2.1 0.8 pad_maximum_fusion.1
  2.9 0.1 reshape.146
  3.0 21.0 %all_to_all.56 = f32[32,8,128]{2,1,0:T(8,128)S(1)} all-to-all(f32[32,8,128]{2,1,0:T(8,128)S(1)} %broadcast_in_dim.39), channel_id=1, replica_groups=mesh['dp'=8,'grid'=32] {'grid'}, dimensions={0} | all-to-all | bytes 262144 | tf_op jit(solution)/shard_map/all_to_all | solution.py:251
  24.0 1.7 broadcast_in_dim.40
  25.6 3.9 %all-to-all-start.2 = ((bf16[32,6,1536]{2,1,0:T(8,128)(2,1)}), bf16[32,6,1536]{2,1,0:T(8,128)(2,1)S(1)}, u32[]{:S(2)}, u32[]{:S(2)}) async-start(bf16[32,6,1536]{2,1,0:T(8,128)(2,1)} %broadcast_in_dim.40), calls=%async_computation.2 | async-start | bytes 1572864 | tf_op jit(solution)/shard_map/all_to_all | solution.py:273
  29.6 0.1 subtract_add_fusion.1
  29.7 0.0 copy-start.4
  29.7 0.6 pad.21.level_ref
  30.4 0.2 reshape.148
  30.6 0.4 slice_reduce_fusion.1
  31.0 1.3 broadcast_multiply_fusion
  32.2 0.6 pad.20.table_ref
  32.9 15.3 %shard_map.147 = (bf16[6,4608,96]{2,1,0:T(8,128)(2,1)}, bf16[6,96,1536]{2,1,0:T(8,128)(2,1)}) custom-call(bf16[6,96,1536]{2,1,0:T(8,128)(2,1)} %bitcast.70, bf16[6,96,1536]{2,1,0:T(8,128)(2,1)} %bitcast.71, bf16[6,96,1536]{2,1,0:T(8,128)(2,1)} %bitcast.76, f32[48,256]{1,0:T(8,128)} %pad.20.table_ref, s32[96,128]{1,0:T(8,128)} %pad.21.level_ref), custom_call_target="tpu_custom_call" | custom-call | flops 5435817984 | bytes 20000000 | tf_op jit(solution)/shard_map/pallas_call | solution.py:171
  48.2 4.5 %copy.44 = bf16[2,3,96,1536]{3,0,1,2:T(2,128)(2,1)} copy(bf16[2,3,96,1536]{3,2,1,0:T(8,128)(2,1)} %bitcast.60) | data formatting | bytes 3538944 | tf_op jit(solution)/shard_map/reshape | solution.py:319
  52.7 0.0 all-to-all-done.2
  52.7 0.9 copy-done.1
  53.6 9.2 %all-to-all-start.3 = ((bf16[2,3,96,1536]{3,0,1,2:T(2,128)(2,1)}), bf16[2,3,96,1536]{3,0,1,2:T(2,128)(2,1)S(1)}, u32[]{:S(2)}, u32[]{:S(2)}) async-start(bf16[2,3,96,1536]{3,0,1,2:T(2,128)(2,1)} %copy.44), calls=%async_computation.3 | async-start | bytes 3538944 | tf_op jit(solution)/shard_map/all_to_all | solution.py:318
  62.8 0.1 subtract_add_fusion
  62.9 0.6 copy-done.5
  63.5 0.6 pad.22.level_ref
  64.1 15.4 %shard_map.148 = (bf16[6,4608,96]{2,1,0:T(8,128)(2,1)}, bf16[6,96,1536]{2,1,0:T(8,128)(2,1)}) custom-call(bf16[6,96,1536]{2,1,0:T(8,128)(2,1)} %bitcast.72, bf16[6,96,1536]{2,1,0:T(8,128)(2,1)} %bitcast.73, bf16[6,96,1536]{2,1,0:T(8,128)(2,1)} %bitcast.74, f32[48,256]{1,0:T(8,128)} %pad.20.table_ref, s32[96,128]{1,0:T(8,128)} %pad.22.level_ref), custom_call_target="tpu_custom_call" | custom-call | flops 5435817984 | bytes 20000000 | tf_op jit(solution)/shard_map/pallas_call | solution.py:171
  79.5 4.5 %copy.40 = bf16[2,3,96,1536]{3,0,1,2:T(2,128)(2,1)} copy(bf16[2,3,96,1536]{3,2,1,0:T(8,128)(2,1)} %bitcast.58) | data formatting | bytes 3538944 | tf_op jit(solution)/shard_map/reshape | solution.py:311
  84.0 19.8 %all-to-all-done.3 = bf16[2,3,96,1536]{3,0,1,2:T(2,128)(2,1)S(1)} async-done(((bf16[2,3,96,1536]{3,0,1,2:T(2,128)(2,1)}), bf16[2,3,96,1536]{3,0,1,2:T(2,128)(2,1)S(1)}, u32[]{:S(2)}, u32[]{:S(2)}) %all-to-all-start.3) | async-done | bytes 1769504 | tf_op jit(solution)/shard_map/all_to_all | solution.py:318
  103.8 6.3 %all-to-all-start.1 = ((bf16[2,3,96,1536]{3,0,1,2:T(2,128)(2,1)}), bf16[2,3,96,1536]{3,0,1,2:T(2,128)(2,1)S(1)}, u32[]{:S(2)}, u32[]{:S(2)}) async-start(bf16[2,3,96,1536]{3,0,1,2:T(2,128)(2,1)} %copy.40), calls=%async_computation.1 | async-start | bytes 3538944 | tf_op jit(solution)/shard_map/all_to_all | solution.py:310
  110.1 2.1 reshape.153.refs_0_
  112.2 1.2 collective-permute-start
  113.4 2.4 %collective-permute-start.1 = (bf16[192,1536]{1,0:T(8,128)(2,1)}, bf16[192,1536]{1,0:T(8,128)(2,1)}, u32[]{:S(2)}, u32[]{:S(2)}) collective-permute-start(bf16[192,1536]{1,0:T(8,128)(2,1)} %reshape.153.refs_0_), channel_id=1, source_target_pairs={{0,128},{32,160},{64,192},{96,224},{128,0},{160,32},{192,64},{224,... | collective-permute-start | bytes 1769480 | tf_op jit(solution)/shard_map/ppermute | solution.py:278
  115.9 1.2 collective-permute-start.2
  117.1 0.6 add_multiply_fusion.start_ref
  117.7 3.6 %collective-permute-start.3 = (bf16[192,1536]{1,0:T(8,128)(2,1)}, bf16[192,1536]{1,0:T(8,128)(2,1)}, u32[]{:S(2)}, u32[]{:S(2)}) collective-permute-start(bf16[192,1536]{1,0:T(8,128)(2,1)} %reshape.153.refs_0_), channel_id=1, source_target_pairs={{0,32},{32,0},{64,96},{96,64},{128,160},{160,128},{192,224},{224,1... | collective-permute-start | bytes 1769480 | tf_op jit(solution)/shard_map/ppermute | solution.py:281
  121.3 4.6 %collective-permute-done.refs_1_ = bf16[192,1536]{1,0:T(8,128)(2,1)} collective-permute-done((bf16[192,1536]{1,0:T(8,128)(2,1)}, bf16[192,1536]{1,0:T(8,128)(2,1)}, u32[]{:S(2)}, u32[]{:S(2)}) %collective-permute-start) | collective-permute-done | bytes 589856 | tf_op jit(solution)/shard_map/ppermute | solution.py:278
  125.9 5.9 %collective-permute-start.4 = (bf16[192,1536]{1,0:T(8,128)(2,1)}, bf16[192,1536]{1,0:T(8,128)(2,1)}, u32[]{:S(2)}, u32[]{:S(2)}) collective-permute-start(bf16[192,1536]{1,0:T(8,128)(2,1)} %collective-permute-done.refs_1_), channel_id=1, source_target_pairs={{0,32},{32,0},{64,96},{96,64},{128,160},{160,128},{192,224},{224,1... | collective-permute-start | bytes 1769480 | tf_op jit(solution)/shard_map/ppermute | solution.py:281
  131.8 7.7 %collective-permute-done.1.refs_2_ = bf16[192,1536]{1,0:T(8,128)(2,1)} collective-permute-done((bf16[192,1536]{1,0:T(8,128)(2,1)}, bf16[192,1536]{1,0:T(8,128)(2,1)}, u32[]{:S(2)}, u32[]{:S(2)}) %collective-permute-start.1) | collective-permute-done | bytes 589856 | tf_op jit(solution)/shard_map/ppermute | solution.py:278
  139.5 3.6 %collective-permute-start.5 = (bf16[192,1536]{1,0:T(8,128)(2,1)}, bf16[192,1536]{1,0:T(8,128)(2,1)}, u32[]{:S(2)}, u32[]{:S(2)}) collective-permute-start(bf16[192,1536]{1,0:T(8,128)(2,1)} %collective-permute-done.1.refs_2_), channel_id=1, source_target_pairs={{0,32},{32,0},{64,96},{96,64},{128,160},{160,128},{192,224},{224,1... | collective-permute-start | bytes 1769480 | tf_op jit(solution)/shard_map/ppermute | solution.py:281
  143.1 0.0 collective-permute-done.2.refs_3_
  143.1 0.0 collective-permute-start.6
  143.1 7.5 %select_reduce_fusion = (s32[96,256]{1,0:T(8,128)S(1)}, s32[96,256]{1,0:T(8,128)S(1)}) fusion(s32[96,96]{1,0:T(8,128)} %copy-done.5, s32[96]{0:T(128)S(1)} %iota_add_fusion, s32[96,96]{1,0:T(8,128)} %copy-done.4), kind=kLoop, calls=%fused_computation | loop fusion | flops 14106624 | bytes 270720 | tf_op jit(solution)/shard_map/reduce_sum | solution.py:213
  150.6 0.7 broadcast_add_fusion
  151.3 0.0 collective-permute-done.3.refs_4_
  151.3 0.0 collective-permute-done.4.refs_5_
  151.3 0.0 collective-permute-done.5.refs_6_
  151.3 0.0 collective-permute-done.6.refs_7_
  151.4 4.7 %shard_map.149 = bf16[1536,1536]{1,0:T(8,128)(2,1)} custom-call(s32[8]{0:T(128)} %add_multiply_fusion.start_ref, bf16[192,1536]{1,0:T(8,128)(2,1)} %reshape.153.refs_0_, bf16[192,1536]{1,0:T(8,128)(2,1)} %collective-permute-done.refs_1_, bf16[192,1536]{1,0:T(8,128)(2,1)} %collective-permute-done.1.refs_2_, bf16[192,1536]{1,0:T(8,128)(2,1)} %collective-permute-done.2.refs_3_, ...), custom_call_target="tpu_custom_call" | custom-call | bytes 9437184 | tf_op jit(solution)/shard_map/pallas_call | solution.py:224
  156.1 1.2 copy.46
  157.3 0.2 copy.47
  157.5 0.0 all-to-all-done.1
  157.5 1.2 copy.42
  158.8 0.2 copy.43
  159.0 0.9 copy-done
  159.9 4.1 %convolution_convert_fusion = bf16[576,1536]{1,0:T(8,128)(2,1)} fusion(bf16[576,1536]{1,0:T(8,128)(2,1)S(1)} %bitcast.57, bf16[1536,1536]{1,0:T(8,128)(2,1)S(1)} %copy-done), kind=kOutput, calls=%fused_computation.4 | convolution fusion | flops 2718793728 | bytes 8257536 | tf_op jit(solution)/shard_map/dot_general | solution.py:330
  163.9 4.1 %convolution_convert_fusion.1 = bf16[576,1536]{1,0:T(8,128)(2,1)} fusion(bf16[576,1536]{1,0:T(8,128)(2,1)S(1)} %bitcast.59, bf16[1536,1536]{1,0:T(8,128)(2,1)S(1)} %copy-done), kind=kOutput, calls=%fused_computation.5 | convolution fusion | flops 2718793728 | bytes 8257536 | tf_op jit(solution)/shard_map/dot_general | solution.py:322
  168.0 12.9 %shard_map.151 = f32[48,256]{1,0:T(8,128)} custom-call(bf16[6,4608,96]{2,1,0:T(8,128)(2,1)} %get-tuple-element.13.p_ref, bf16[6,96,1536]{2,1,0:T(8,128)(2,1)} %bitcast.75, bf16[6,96,1536]{2,1,0:T(8,128)(2,1)} %bitcast.80, s32[96,256]{1,0:T(8,128)} %get-tuple-element.28.index_ref), custom_call_target="tpu_custom_call" | custom-call | flops 5435817984 | bytes 20000000 | tf_op jit(solution)/shard_map/pallas_call | solution.py:191
  180.9 13.6 %shard_map.150 = (bf16[6,96,1536]{2,1,0:T(8,128)(2,1)}, f32[48,256]{1,0:T(8,128)}) custom-call(bf16[6,4608,96]{2,1,0:T(8,128)(2,1)} %get-tuple-element.10.p_ref, bf16[6,96,1536]{2,1,0:T(8,128)(2,1)} %bitcast.79, bf16[6,96,1536]{2,1,0:T(8,128)(2,1)} %bitcast.77, s32[96,256]{1,0:T(8,128)} %get-tuple-element.29.index_ref), custom_call_target="tpu_custom_call" | custom-call | flops 5435817984 | bytes 20000000 | tf_op jit(solution)/shard_map/pallas_call | solution.py:191
  194.5 1.3 fusion.5
  195.8 1.4 multiply_reduce_fusion
  197.2 0.1 copy.48
  197.4 0.1 reshape.159
  197.6 18.2 %all_to_all.57 = f32[32,8,128]{2,1,0:T(8,128)S(1)} all-to-all(f32[32,8,128]{2,1,0:T(8,128)S(1)} %bitcast.62), channel_id=1, replica_groups=mesh['dp'=8,'grid'=32] {'grid'}, dimensions={0} | all-to-all | bytes 262144 | tf_op jit(solution)/shard_map/all_to_all | solution.py:261
  215.8 10.6 %all_to_all.58 = f32[8,8,128]{2,1,0:T(8,128)S(1)} all-to-all(f32[8,8,128]{2,1,0:T(8,128)S(1)} %broadcast_in_dim.76), channel_id=1, replica_groups=mesh['dp'=8,'grid'=32] {'dp'}, dimensions={0} | all-to-all | bytes 65536 | tf_op jit(solution)/shard_map/all_to_all | solution.py:263
  226.5 0.1 reshape.162
  226.5 0.0 copy-start.6
  226.6 0.7 slice_reduce_fusion.2
  (30 shorter events, 0.2 us)
Async XLA Ops:
  0.6 28.9 %copy-start.7 = (s32[96]{0:T(128)S(1)}, s32[96]{0:T(128)}, u32[]{:S(2)}) copy-start(s32[96]{0:T(128)} %param.19) | copy-start | bytes 1156
  25.6 27.0 %all-to-all-start.2 = ((bf16[32,6,1536]{2,1,0:T(8,128)(2,1)}), bf16[32,6,1536]{2,1,0:T(8,128)(2,1)S(1)}, u32[]{:S(2)}, u32[]{:S(2)}) async-start(bf16[32,6,1536]{2,1,0:T(8,128)(2,1)} %broadcast_in_dim.40), calls=%async_computation.2 | async-start | bytes 1572864 | tf_op jit(solution)/shard_map/all_to_all | solution.py:273
  29.7 0.7 copy-start.4
  30.6 17.6 %copy-start.2 = (f32[512,50]{1,0:T(8,128)}, f32[512,50]{1,0:T(8,128)S(1)}, u32[]{:S(2)}) copy-start(f32[512,50]{1,0:T(8,128)S(1)} %reshape.148) | copy-start | bytes 307204
  52.7 10.2 %copy-start.8 = (s32[96]{0:T(128)S(1)}, s32[96]{0:T(128)}, u32[]{:S(2)}) copy-start(s32[96]{0:T(128)} %param.20) | copy-start | bytes 1156
  52.7 0.9 copy-start.1
  53.6 50.2 %all-to-all-start.3 = ((bf16[2,3,96,1536]{3,0,1,2:T(2,128)(2,1)}), bf16[2,3,96,1536]{3,0,1,2:T(2,128)(2,1)S(1)}, u32[]{:S(2)}, u32[]{:S(2)}) async-start(bf16[2,3,96,1536]{3,0,1,2:T(2,128)(2,1)} %copy.44), calls=%async_computation.3 | async-start | bytes 3538944 | tf_op jit(solution)/shard_map/all_to_all | solution.py:318
  62.9 0.6 copy-start.5
  103.8 53.7 %all-to-all-start.1 = ((bf16[2,3,96,1536]{3,0,1,2:T(2,128)(2,1)}), bf16[2,3,96,1536]{3,0,1,2:T(2,128)(2,1)S(1)}, u32[]{:S(2)}, u32[]{:S(2)}) async-start(bf16[2,3,96,1536]{3,0,1,2:T(2,128)(2,1)} %copy.40), calls=%async_computation.1 | async-start | bytes 3538944 | tf_op jit(solution)/shard_map/all_to_all | solution.py:310
  112.2 13.6 %collective-permute-start = (bf16[192,1536]{1,0:T(8,128)(2,1)}, bf16[192,1536]{1,0:T(8,128)(2,1)}, u32[]{:S(2)}, u32[]{:S(2)}) collective-permute-start(bf16[192,1536]{1,0:T(8,128)(2,1)} %reshape.153.refs_0_), channel_id=1, source_target_pairs={{0,64},{32,96},{64,128},{96,160},{128,192},{160,224},{192,0},{224,... | collective-permute-start | bytes 1769480 | tf_op jit(solution)/shard_map/ppermute | solution.py:278
  113.4 26.0 %collective-permute-start.1 = (bf16[192,1536]{1,0:T(8,128)(2,1)}, bf16[192,1536]{1,0:T(8,128)(2,1)}, u32[]{:S(2)}, u32[]{:S(2)}) collective-permute-start(bf16[192,1536]{1,0:T(8,128)(2,1)} %reshape.153.refs_0_), channel_id=1, source_target_pairs={{0,128},{32,160},{64,192},{96,224},{128,0},{160,32},{192,64},{224,... | collective-permute-start | bytes 1769480 | tf_op jit(solution)/shard_map/ppermute | solution.py:278
  115.9 27.2 %collective-permute-start.2 = (bf16[192,1536]{1,0:T(8,128)(2,1)}, bf16[192,1536]{1,0:T(8,128)(2,1)}, u32[]{:S(2)}, u32[]{:S(2)}) collective-permute-start(bf16[192,1536]{1,0:T(8,128)(2,1)} %reshape.153.refs_0_), channel_id=1, source_target_pairs={{0,192},{32,224},{64,0},{96,32},{128,64},{160,96},{192,128},{224,1... | collective-permute-start | bytes 1769480 | tf_op jit(solution)/shard_map/ppermute | solution.py:278
  117.7 33.7 %collective-permute-start.3 = (bf16[192,1536]{1,0:T(8,128)(2,1)}, bf16[192,1536]{1,0:T(8,128)(2,1)}, u32[]{:S(2)}, u32[]{:S(2)}) collective-permute-start(bf16[192,1536]{1,0:T(8,128)(2,1)} %reshape.153.refs_0_), channel_id=1, source_target_pairs={{0,32},{32,0},{64,96},{96,64},{128,160},{160,128},{192,224},{224,1... | collective-permute-start | bytes 1769480 | tf_op jit(solution)/shard_map/ppermute | solution.py:281
  125.9 25.5 %collective-permute-start.4 = (bf16[192,1536]{1,0:T(8,128)(2,1)}, bf16[192,1536]{1,0:T(8,128)(2,1)}, u32[]{:S(2)}, u32[]{:S(2)}) collective-permute-start(bf16[192,1536]{1,0:T(8,128)(2,1)} %collective-permute-done.refs_1_), channel_id=1, source_target_pairs={{0,32},{32,0},{64,96},{96,64},{128,160},{160,128},{192,224},{224,1... | collective-permute-start | bytes 1769480 | tf_op jit(solution)/shard_map/ppermute | solution.py:281
  139.5 11.9 %collective-permute-start.5 = (bf16[192,1536]{1,0:T(8,128)(2,1)}, bf16[192,1536]{1,0:T(8,128)(2,1)}, u32[]{:S(2)}, u32[]{:S(2)}) collective-permute-start(bf16[192,1536]{1,0:T(8,128)(2,1)} %collective-permute-done.1.refs_2_), channel_id=1, source_target_pairs={{0,32},{32,0},{64,96},{96,64},{128,160},{160,128},{192,224},{224,1... | collective-permute-start | bytes 1769480 | tf_op jit(solution)/shard_map/ppermute | solution.py:281
  143.1 8.2 %collective-permute-start.6 = (bf16[192,1536]{1,0:T(8,128)(2,1)}, bf16[192,1536]{1,0:T(8,128)(2,1)}, u32[]{:S(2)}, u32[]{:S(2)}) collective-permute-start(bf16[192,1536]{1,0:T(8,128)(2,1)} %collective-permute-done.2.refs_3_), channel_id=1, source_target_pairs={{0,32},{32,0},{64,96},{96,64},{128,160},{160,128},{192,224},{224,1... | collective-permute-start | bytes 1769480 | tf_op jit(solution)/shard_map/ppermute | solution.py:281
  157.5 2.3 %copy-start = (bf16[1536,1536]{1,0:T(8,128)(2,1)S(1)}, bf16[1536,1536]{1,0:T(8,128)(2,1)}, u32[]{:S(2)}) copy-start(bf16[1536,1536]{1,0:T(8,128)(2,1)} %shard_map.149) | copy-start | bytes 14155780
  180.9 13.6 %copy-start.9 = (f32[48,191]{1,0:T(8,128)S(1)}, f32[48,191]{1,0:T(8,128)}, u32[]{:S(2)}) copy-start(f32[48,191]{1,0:T(8,128)} %get-tuple-element.25) | copy-start | bytes 110020
  180.9 13.6 %copy-start.10 = (f32[48,256]{1,0:T(8,128)S(1)}, f32[48,256]{1,0:T(8,128)}, u32[]{:S(2)}) copy-start(f32[48,256]{1,0:T(8,128)} %shard_map.151) | copy-start | bytes 147460
  180.9 14.9 %copy-start.3 = (f32[512,50]{1,0:T(8,128)S(1)}, f32[512,50]{1,0:T(8,128)}, u32[]{:S(2)}) copy-start(f32[512,50]{1,0:T(8,128)} %copy-done.2) | copy-start | bytes 307204
  226.5 0.7 copy-start.6

commit v3 on v2

--- a/solution.py
+++ b/solution.py
@@ -20,7 +20,9 @@
 PACK = LANES // HD
 GROUPS = D // LANES
 ROWS = PACK * G
+MESSAGE = 6 * 3 * GROUPS
 LOG2E = 1.4426950408889634
+GRANT = 28 << 20
 
 PRECISE = lax.Precision.HIGHEST
 NT = (((1,), (1,)), ((), ()))
@@ -62,7 +64,9 @@
     return jnp.take_along_axis(row, index, axis=1, mode="promise_in_bounds")
 
 
-def forward_kernel(q_ref, k_ref, x_ref, table_ref, level_ref, p_ref, o_ref, bias_ref, *, transpose):
+def forward_kernel(
+    q_ref, k_ref, x_ref, table_ref, level_ref, p_ref, o_ref, bias_ref, sent_ref, *, transpose
+):
     masks = head_masks()
 
     @pl.when(pl.program_id(0) == 0)
@@ -100,10 +104,26 @@
                     p, stack_heads(x, own), TN, preferred_element_type=jnp.float32
                 )
                 o = r if o is None else o + r
-        o_ref[0, :, sl] = o.astype(jnp.bfloat16)
+        if sent_ref is None:
+            o_ref[0, :, sl] = o.astype(jnp.bfloat16)
+        else:
+            first = pl.program_id(0) * GROUPS + g
+            sent_ref[pl.ds(first, G, stride=MESSAGE // 3), :] = o
         return carry
 
     lax.fori_loop(0, GROUPS, body, 0, unroll=UNROLL)
+
+    if sent_ref is not None:
+
+        @pl.when(pl.program_id(0) == pl.num_programs(0) - 1)
+        def _():
+            def flush(j, carry):
+                rows = pl.ds(pl.multiple_of(j * 4 * MESSAGE, 4 * MESSAGE), 4 * MESSAGE)
+                out = pl.ds(pl.multiple_of(j * 4, 4), 4)
+                o_ref[out] = sent_ref[rows, :].astype(jnp.bfloat16).reshape(4, MESSAGE, LANES)
+                return carry
+
+            lax.fori_loop(0, GRID // 4, flush, 0)
 
 
 def backward_kernel(p_ref, v_ref, g_ref, index_ref, *outs, attend):
@@ -168,16 +188,25 @@
 
 def attention_forward(q, k, x, table, level, transpose):
     n = q.shape[0]
+    scratch = [pltpu.VMEM((NH * G, LANES), jnp.float32)]
+    kernel = functools.partial(forward_kernel, transpose=transpose)
+    if transpose:
+        kernel = functools.partial(kernel, sent_ref=None)
+        spec, shape = each(BLOCK), (n, G, D)
+    else:
+        scratch.append(pltpu.VMEM((GRID * MESSAGE, LANES), jnp.float32))
+        spec, shape = whole((GRID, MESSAGE, LANES)), (GRID, MESSAGE, LANES)
     return pl.pallas_call(
-        functools.partial(forward_kernel, transpose=transpose),
+        kernel,
         grid=(n,),
+        compiler_params=pltpu.CompilerParams(vmem_limit_bytes=GRANT),
         in_specs=[each(BLOCK)] * 3 + [whole((NH, 2 * LANES)), whole((G, LANES))],
-        out_specs=[each(PSHAPE), each(BLOCK)],
+        out_specs=[each(PSHAPE), spec],
         out_shape=[
             jax.ShapeDtypeStruct((n, NH * G, G), jnp.bfloat16),
-            jax.ShapeDtypeStruct((n, G, D), jnp.bfloat16),
+            jax.ShapeDtypeStruct(shape, jnp.bfloat16),
         ],
-        scratch_shapes=[pltpu.VMEM((NH * G, LANES), jnp.float32)],
+        scratch_shapes=scratch,
         cost_estimate=pl.CostEstimate(
             flops=n * NH * 16 * G * G * LANES, transcendentals=n * NH * G * G, bytes_accessed=20_000_000
         ),
@@ -191,6 +220,7 @@
     return pl.pallas_call(
         functools.partial(backward_kernel, attend=attend),
         grid=(n,),
+        compiler_params=pltpu.CompilerParams(vmem_limit_bytes=GRANT),
         in_specs=[each(PSHAPE), each(BLOCK), each(BLOCK), whole((G, 2 * LANES))],
         out_specs=specs + [whole((NH, 2 * LANES))],
         out_shape=shapes + [jax.ShapeDtypeStruct((NH, 2 * LANES), jnp.float32)],
@@ -226,6 +256,7 @@
         in_specs=[pl.BlockSpec(memory_space=pltpu.SMEM)] + [pl.BlockSpec(memory_space=pltpu.VMEM)] * DP,
         out_specs=pl.BlockSpec(memory_space=pltpu.VMEM),
         out_shape=jax.ShapeDtypeStruct((D, D), jnp.bfloat16),
+        compiler_params=pltpu.CompilerParams(vmem_limit_bytes=GRANT),
         cost_estimate=pl.CostEstimate(flops=0, transcendentals=0, bytes_accessed=2 * D * D * 2),
     )(starts, *parts)
 
@@ -236,43 +267,135 @@
     return jnp.sign(scaled) * jnp.log2(jnp.abs(scaled) + 1.0) / 3.0
 
 
-def to_tile(flat):
-    pad = [(0, 0)] * (flat.ndim - 1) + [(0, 1024 - flat.shape[-1])]
-    return jnp.pad(flat, pad).reshape(flat.shape[:-1] + (8, 128))
-
-
-def from_tile(tiles):
-    return tiles.reshape(tiles.shape[:-2] + (1024,))[..., :800]
+UNITS = HM // GRID
+HALF = UNITS // 2
+WIDE = LANES // 2
+
+
+def column(row):
+    n = row.shape[1]
+    i = lax.broadcasted_iota(jnp.int32, (n, n), 0)
+    j = lax.broadcasted_iota(jnp.int32, (n, n), 1)
+    return jnp.sum(jnp.where(i == j, jnp.broadcast_to(row, (n, n)), 0.0), axis=1, keepdims=True)
+
+
+def pack_kernel(in_ref, bias_ref, out_ref, tile_ref):
+    rest = jnp.zeros((UNITS, WIDE - NH - 2), jnp.float32)
+    rows = jnp.concatenate([out_ref[...], column(in_ref[...]), column(bias_ref[...]), rest], axis=1)
+    tile = jnp.concatenate([rows[:HALF], rows[HALF:]], axis=1)
+    tile_ref[...] = jnp.broadcast_to(tile[None], (GRID, HALF, LANES))
+
+
+def halves(tiles):
+    return jnp.concatenate([tiles[:, :WIDE], tiles[:, WIDE:]], axis=0)
+
+
+def table_kernel(unit_ref, coord_ref, table_ref, squashed_ref):
+    units = halves(unit_ref[...])
+    pre_act = units[:, NH:NH + 1] * coord_ref[...] + units[:, NH + 1:NH + 2]
+    hidden = jnp.maximum(pre_act, 0.0)
+    pre = lax.dot_general(
+        units[:, :NH], hidden, TN, precision=PRECISE, preferred_element_type=jnp.float32
+    )
+    squashed = 1.0 / (1.0 + jnp.exp(-pre))
+    squashed_ref[...] = squashed
+    table_ref[...] = squashed * (16.0 * LOG2E)
+
+
+def grad_kernel(unit_ref, coord_ref, squashed_ref, row_ref, col_ref, out_ref, *, scale):
+    units = halves(unit_ref[...])
+    coords = coord_ref[...]
+    pre_act = units[:, NH:NH + 1] * coords + units[:, NH + 1:NH + 2]
+    hidden = jnp.maximum(pre_act, 0.0)
+    squashed = squashed_ref[...]
+    pre_grad = (row_ref[...] + col_ref[...]) * scale * 16.0 * squashed * (1.0 - squashed)
+    grad_out = lax.dot_general(
+        hidden, pre_grad, NT, precision=PRECISE, preferred_element_type=jnp.float32
+    )
+    back = lax.dot_general(
+        units[:, :NH], pre_grad, NN, precision=PRECISE, preferred_element_type=jnp.float32
+    )
+    unit_grad = jnp.where(pre_act > 0, back, 0.0)
+    grad_in = jnp.sum(unit_grad * coords, axis=1, keepdims=True)
+    grad_bias = jnp.sum(unit_grad, axis=1, keepdims=True)
+    rest = jnp.zeros((HM, WIDE - NH - 2), jnp.float32)
+    rows = jnp.concatenate([grad_out, grad_in, grad_bias, rest], axis=1)
+    out_ref[...] = jnp.concatenate([rows[:HM // 2], rows[HM // 2:]], axis=1)
+
+
+def unpack_kernel(got_ref, out_ref, in_ref, bias_ref):
+    units = halves(jnp.sum(got_ref[...], axis=0))
+    out_ref[...] = units[:, :NH]
+    i = lax.broadcasted_iota(jnp.int32, (UNITS, UNITS), 0)
+    j = lax.broadcasted_iota(jnp.int32, (UNITS, UNITS), 1)
+    for lane, ref in ((NH, in_ref), (NH + 1, bias_ref)):
+        spread = jnp.broadcast_to(units[:, lane:lane + 1], (UNITS, UNITS))
+        ref[...] = jnp.sum(jnp.where(i == j, spread, 0.0), axis=0, keepdims=True)
 
 
 def gather_units(mlp_in, mlp_bias, mlp_out):
-    own = jnp.concatenate([mlp_out, mlp_in[:, None], mlp_bias[:, None]], axis=1)
-    tile = to_tile(own.reshape(800))
-    got = lax.all_to_all(
-        jnp.broadcast_to(tile[None], (GRID, 8, 128)), "grid", 0, 0, tiled=True
-    )
-    units = from_tile(got).reshape(HM, 50)
-    return units[:, :NH], units[:, NH], units[:, NH + 1]
-
-
-def reduce_units(grad_out, grad_in, grad_bias):
-    whole = jnp.concatenate([grad_out, grad_in[:, None], grad_bias[:, None]], axis=1)
-    tiles = to_tile(whole.reshape(GRID, 800))
+    tiles = pl.pallas_call(
+        pack_kernel, out_shape=jax.ShapeDtypeStruct((GRID, HALF, LANES), jnp.float32)
+    )(mlp_in[None], mlp_bias[None], mlp_out)
     got = lax.all_to_all(tiles, "grid", 0, 0, tiled=True)
-    own = jnp.sum(got, axis=0)
-    got = lax.all_to_all(jnp.broadcast_to(own[None], (DP, 8, 128)), "dp", 0, 0, tiled=True)
-    own = from_tile(jnp.sum(got, axis=0)).reshape(16, 50)
-    return own[:, :NH], own[:, NH], own[:, NH + 1]
+    return got.reshape(HM // 2, LANES)
+
+
+def bias_tables(units, coords):
+    shape = jax.ShapeDtypeStruct((NH, 2 * LANES), jnp.float32)
+    return pl.pallas_call(table_kernel, out_shape=[shape, shape])(units, coords)
+
+
+def unit_grads(units, coords, squashed, row_table, col_table, scale):
+    return pl.pallas_call(
+        functools.partial(grad_kernel, scale=scale),
+        out_shape=jax.ShapeDtypeStruct((HM // 2, LANES), jnp.float32),
+    )(units, coords, squashed, row_table, col_table)
+
+
+def reduce_units(grads):
+    got = lax.all_to_all(grads.reshape(GRID, HALF, LANES), "grid", 0, 0, tiled=True)
+    own = jnp.broadcast_to(jnp.sum(got, axis=0)[None], (DP, HALF, LANES))
+    got = lax.all_to_all(own, "dp", 0, 0, tiled=True)
+    row = jax.ShapeDtypeStruct((1, UNITS), jnp.float32)
+    grad_out, grad_in, grad_bias = pl.pallas_call(
+        unpack_kernel, out_shape=[jax.ShapeDtypeStruct((UNITS, NH), jnp.float32), row, row]
+    )(got)
+    return grad_out, grad_in[0], grad_bias[0]
 
 
 def along_x(step, swap):
     return [(i, ((i // 2 + step) % 4) * 2 + ((i % 2) ^ swap)) for i in range(DP)]
 
 
+def order_kernel(swap_ref, mine_ref, other_ref, out_ref):
+    half = mine_ref.shape[0]
+    for first, (a_ref, b_ref) in ((0, (mine_ref, other_ref)), (1, (other_ref, mine_ref))):
+
+        @pl.when(swap_ref[0] == first)
+        def _():
+            out_ref[:half] = a_ref[...]
+            out_ref[half:] = b_ref[...]
+
+
+def in_order(mine, other, swap):
+    rows = mine.shape[0]
+    return pl.pallas_call(
+        order_kernel,
+        in_specs=[pl.BlockSpec(memory_space=pltpu.SMEM)] + [pl.BlockSpec(memory_space=pltpu.VMEM)] * 2,
+        out_specs=pl.BlockSpec(memory_space=pltpu.VMEM),
+        out_shape=jax.ShapeDtypeStruct((2 * rows, D), jnp.bfloat16),
+        compiler_params=pltpu.CompilerParams(vmem_limit_bytes=8 << 20),
+        cost_estimate=pl.CostEstimate(flops=0, transcendentals=0, bytes_accessed=8 * rows * D),
+    )(swap[None].astype(jnp.int32), mine, other)
+
+
 def fetch_weight(w_value):
-    part = lax.all_to_all(
-        jnp.broadcast_to(w_value[None], (GRID,) + w_value.shape), "grid", 0, 0, tiled=True
-    ).reshape(D // DP, D)
+    here = lax.axis_index("grid")
+    part = w_value
+    for bit in range(5):
+        other = lax.ppermute(part, "grid", [(g, g ^ (1 << bit)) for g in range(GRID)])
+        part = in_order(part, other, (here >> bit) & 1)
     mine = [part]
     for step in (1, 2, 3):
         mine.append(lax.ppermute(part, "dp", along_x(step, 0)))
@@ -293,13 +416,9 @@
     images = q_row.shape[0]
     row_count = q_row.shape[1]
     col_count = q_col.shape[2]
-    all_out, all_in, all_bias = gather_units(mlp_in, mlp_bias, mlp_out)
-    coords = offset_coords()
-    pre_act = coords[:, None] * all_in[None, :] + all_bias[None, :]
-    hidden_units = jnp.maximum(pre_act, 0.0)
-    table_pre = lax.dot_general(all_out, hidden_units, (((0,), (1,)), ((), ())), precision=PRECISE)
-    squashed = jax.nn.sigmoid(table_pre)
-    table = jnp.pad(squashed * (16.0 * LOG2E), ((0, 0), (0, 2 * LANES - NOFF)))
+    units = gather_units(mlp_in, mlp_bias, mlp_out)
+    coords = jnp.pad(offset_coords(), (0, 2 * LANES - NOFF))[None]
+    table, squashed = bias_tables(units, coords)
     whole_weight = fetch_weight(w_value)
 
     rows = lambda x: x.reshape(images * row_count, G, D)
@@ -307,9 +426,7 @@
     p_row, row_out = attention_forward(
         rows(q_row), rows(k_row), rows(v_row), table, levels(col_positions), False
     )
-    col_out = lax.all_to_all(
-        row_out.reshape(images, row_count, G, D), "grid", split_axis=2, concat_axis=1, tiled=True
-    )
+    col_out = lax.all_to_all(row_out, "grid", split_axis=0, concat_axis=0, tiled=True)
 
     grad_cols = cols(cotangent)
     p_col, d_values = attention_forward(
@@ -319,8 +436,9 @@
         d_values.reshape(images, col_count, G, D), "grid", split_axis=2, concat_axis=1, tiled=True
     )
 
+    col_tokens = col_out.reshape(GRID, col_count, images, row_count, D).transpose(2, 1, 0, 3, 4)
     value_cols = jnp.dot(
-        cols(col_out).reshape(-1, D), whole_weight, preferred_element_type=jnp.float32
+        col_tokens.reshape(-1, D), whole_weight, preferred_element_type=jnp.float32
     ).astype(jnp.bfloat16).reshape(images * col_count, G, D)
     attended, col_table = attention_backward(
         p_col, value_cols, grad_cols, fold_index(row_positions), True
@@ -337,16 +455,8 @@
     )
 
     batch_size = lax.axis_size("dp") * images
-    table_grad = (row_table + col_table)[:, :NOFF] / (batch_size * G)
-    pre_grad = table_grad * 16.0 * squashed * (1.0 - squashed)
-    grad_out = lax.dot_general(
-        hidden_units, pre_grad, (((0,), (1,)), ((), ())), precision=PRECISE
-    )
-    back_units = lax.dot_general(pre_grad, all_out, (((0,), (1,)), ((), ())), precision=PRECISE)
-    unit_grad = jnp.where(pre_act > 0, back_units, 0.0)
-    grad_in = jnp.sum(unit_grad * coords[:, None], axis=0)
-    grad_bias = jnp.sum(unit_grad, axis=0)
-    grad_mlp_out, grad_mlp_in, grad_mlp_bias = reduce_units(grad_out, grad_in, grad_bias)
+    grads = unit_grads(units, coords, squashed, row_table, col_table, 1.0 / (batch_size * G))
+    grad_mlp_out, grad_mlp_in, grad_mlp_bias = reduce_units(grads)
     return (attended, grad_mlp_in, grad_mlp_bias, grad_mlp_out)
 
 

time: 228 us -> 281 us (1.23)
  waiting for transfers between devices: 32.1 us -> 89.1 us
  blocking collectives: 49.8 us -> 26.9 us
  starting transfers between devices: 37.4 us -> 52.8 us
  local copies, waits for them, and re-layouts: 23.2 us -> 36.9 us
  Pallas kernels: 61.9 us -> 57 us
  matrix products: 12 us -> 8.32 us
    ppermute x0 -> x5, waiting for transfers between devices: none -> 53.9 us  [fetch_weight(): other = lax.ppermute(part, 'grid', [(g, g ^ 1 << bit) for g in range(GRID)])]
    all_to_all x3 -> x2, blocking collectives: 49.8 us -> 26.9 us  [the longest x1 16.3 us: reduce_units(): lax.all_to_all(grads.reshape(GRID, HALF, LANES), 'grid', 0, 0, tiled=True)]
    unnamed x25 -> x56, local copies, waits for them, and re-layouts: 2.52 us -> 17.3 us
    ppermute x0 -> x5, starting transfers between devices: none -> 10.4 us  [fetch_weight(): other = lax.ppermute(part, 'grid', [(g, g ^ 1 << bit) for g in range(GRID)])]
    all_to_all x2, starting transfers between devices: 10.2 us -> 19.9 us  [the longest x1 12 us: gather_units(): got = lax.all_to_all(tiles, 'grid', 0, 0, tiled=True)]
    all_to_all x2, waiting for transfers between devices: 0.01 us -> 6.52 us  [the longest x1 6.51 us: gather_units(): got = lax.all_to_all(tiles, 'grid', 0, 0, tiled=True)]
    ppermute x3, waiting for transfers between devices: 12.3 us -> 6.13 us  [fetch_weight(): mine.append(lax.ppermute(part, 'dp', along_x(step, 0)))]
    pallas_call x2, Pallas kernels: 26.5 us -> 20.5 us  [attention_backward(): pl.pallas_call(functools.partial(backward_kernel, attend=attend), grid=(n...]
  transfers between devices with their start and end apart: 10 -> 15, of which waited for: 3 -> 10; matrix products, arithmetic and copies ran while one was open for 11% -> 5% of each run, Pallas kernels for 16% -> 6%
where the time goes in v3:
time: 281 us; the launch traced here: 280 us
  waiting for transfers between devices  89.1 us (32%)
  Pallas kernels  57 us (20%)
  starting transfers between devices  52.8 us (19%)
  local copies, waits for them, and re-layouts  36.9 us (13%)
  blocking collectives  26.9 us (10%)
  matrix products  8.32 us (3%)
  other arithmetic  8.05 us (3%)
    ppermute x5, waiting for transfers between devices, fetch_weight(): other = lax.ppermute(part, 'grid', [(g, g ^ 1 << bit) for g in range(GRID)])  53.9 us
    pallas_call x2, Pallas kernels, attention_forward(): pl.pallas_call(kernel, grid=(n,), compiler_params=pltpu.CompilerParams(vm...  27.6 us
    pallas_call x2, Pallas kernels, attention_backward(): pl.pallas_call(functools.partial(backward_kernel, attend=attend), grid=(n...  20.5 us
    all_to_all x1, waiting for transfers between devices, shards(): lax.all_to_all(d_values.reshape(images, col_count, G, D), 'grid', split_a...  20.3 us
    unnamed x56, local copies, waits for them, and re-layouts  17.3 us
    all_to_all x1, blocking collectives, reduce_units(): lax.all_to_all(grads.reshape(GRID, HALF, LANES), 'grid', 0, 0, tiled=True)  16.3 us
    ppermute x4, starting transfers between devices, fetch_weight(): other.append(lax.ppermute(mine[step], 'dp', along_x(0, 1)))  13.2 us
    all_to_all x1, starting transfers between devices, gather_units(): got = lax.all_to_all(tiles, 'grid', 0, 0, tiled=True)  12 us
  transfers between devices with their start and end apart: 15, of which 10 were waited for; matrix products, arithmetic and copies ran while one was open for 5% of the time, Pallas kernels for 6%

profile of v3, /device:TPU:1, one launch (start us, length us, event | category | flops | bytes accessed | tf_op | source)
XLA Modules:
  0.0 280.1 jit_solution(18386287853474517745)
XLA Ops:
  0.6 1.5 shard_map.147
  2.2 12.0 %all-to-all-start = ((f32[32,8,128]{2,1,0:T(8,128)}), f32[32,8,128]{2,1,0:T(8,128)S(1)}, u32[]{:S(2)}, u32[]{:S(2)}) async-start(f32[32,8,128]{2,1,0:T(8,128)} %shard_map.147), calls=%async_computation | async-start | bytes 262144 | tf_op jit(solution)/shard_map/all_to_all | solution.py:340
  14.2 0.6 pad.11
  14.8 1.4 subtract_add_fusion
  16.2 0.6 copy-done.20
  16.8 6.5 %all-to-all-done = f32[32,8,128]{2,1,0:T(8,128)S(1)} async-done(((f32[32,8,128]{2,1,0:T(8,128)}), f32[32,8,128]{2,1,0:T(8,128)S(1)}, u32[]{:S(2)}, u32[]{:S(2)}) %all-to-all-start) | async-done | bytes 131104 | tf_op jit(solution)/shard_map/all_to_all | solution.py:340
  23.4 0.6 copy-done.18
  24.0 2.2 shard_map.148
  26.2 1.5 copy-done.4
  27.7 1.5 copy-done.5
  29.2 1.5 copy-done.10
  30.7 0.8 copy-done.12
  31.5 13.0 %shard_map.149 = (bf16[6,4608,96]{2,1,0:T(8,128)(2,1)S(1)}, bf16[6,96,1536]{2,1,0:T(8,128)(2,1)S(1)}) custom-call(bf16[6,96,1536]{2,1,0:T(8,128)(2,1)S(1)} %bitcast.45, bf16[6,96,1536]{2,1,0:T(8,128)(2,1)S(1)} %bitcast.46, bf16[6,96,1536]{2,1,0:T(8,128)(2,1)S(1)} %bitcast.51, f32[48,256]{1,0:T(8,128)S(1)} %copy-done.12, s32[96,128]{1,0:T(8,128)S(1)} %pad.12.level_ref), custom_call_target="tpu_custom_call" | custom-call | flops 5435817984 | bytes 20000000 | tf_op jit(solution)/shard_map/pallas_call | solution.py:199
  44.5 2.8 %copy-done.15 = bf16[6,4608,96]{2,1,0:T(8,128)(2,1)} copy-done((bf16[6,4608,96]{2,1,0:T(8,128)(2,1)}, bf16[6,4608,96]{2,1,0:T(8,128)(2,1)S(1)}, u32[]{:S(2)}) %copy-start.15) | copy-done | bytes 5308440
  47.3 3.0 %copy.26 = bf16[2,3,96,1536]{3,0,1,2:T(2,128)(2,1)} copy(bf16[2,3,96,1536]{3,2,1,0:T(8,128)(2,1)S(1)} %bitcast.44) | data formatting | bytes 3538944 | tf_op jit(solution)/shard_map/reshape | solution.py:436
  50.3 5.0 %all-to-all-start.2 = ((bf16[2,3,96,1536]{3,0,1,2:T(2,128)(2,1)}), bf16[2,3,96,1536]{3,0,1,2:T(2,128)(2,1)}, u32[]{:S(2)}, u32[]{:S(2)}) async-start(bf16[2,3,96,1536]{3,0,1,2:T(2,128)(2,1)} %copy.26), calls=%async_computation.2 | async-start | bytes 3538944 | tf_op jit(solution)/shard_map/all_to_all | solution.py:435
  55.3 0.8 pad.13.level_ref
  56.1 0.0 copy-start.8
  56.1 1.5 copy-done.8
  57.6 0.8 copy-done.13
  58.4 14.6 %shard_map.150 = (bf16[6,4608,96]{2,1,0:T(8,128)(2,1)S(1)}, bf16[32,216,128]{2,1,0:T(8,128)(2,1)}) custom-call(bf16[6,96,1536]{2,1,0:T(8,128)(2,1)S(1)} %bitcast.47, bf16[6,96,1536]{2,1,0:T(8,128)(2,1)S(1)} %bitcast.48, bf16[6,96,1536]{2,1,0:T(8,128)(2,1)S(1)} %bitcast.49, f32[48,256]{1,0:T(8,128)S(1)} %copy-done.13, s32[96,128]{1,0:T(8,128)S(1)} %pad.13.level_ref), custom_call_target="tpu_custom_call" | custom-call | flops 5435817984 | bytes 20000000 | tf_op jit(solution)/shard_map/pallas_call | solution.py:199
  73.0 2.9 %copy-done.14 = bf16[6,4608,96]{2,1,0:T(8,128)(2,1)} copy-done((bf16[6,4608,96]{2,1,0:T(8,128)(2,1)}, bf16[6,4608,96]{2,1,0:T(8,128)(2,1)S(1)}, u32[]{:S(2)}) %copy-start.14) | copy-done | bytes 5308440
  75.9 20.3 %all-to-all-done.2 = bf16[2,3,96,1536]{3,0,1,2:T(2,128)(2,1)} async-done(((bf16[2,3,96,1536]{3,0,1,2:T(2,128)(2,1)}), bf16[2,3,96,1536]{3,0,1,2:T(2,128)(2,1)}, u32[]{:S(2)}, u32[]{:S(2)}) %all-to-all-start.2) | async-done | bytes 1769504 | tf_op jit(solution)/shard_map/all_to_all | solution.py:435
  96.2 7.9 %all-to-all-start.1 = ((bf16[32,216,128]{2,1,0:T(8,128)(2,1)}), bf16[32,216,128]{2,1,0:T(8,128)(2,1)}, u32[]{:S(2)}, u32[]{:S(2)}) async-start(bf16[32,216,128]{2,1,0:T(8,128)(2,1)} %get-tuple-element.17), calls=%async_computation.1 | async-start | bytes 3538944 | tf_op jit(solution)/shard_map/all_to_all | solution.py:429
  104.1 1.3 collective-permute-start
  105.3 38.8 %collective-permute-done.other_ref = bf16[6,1536]{1,0:T(8,128)(2,1)S(1)} collective-permute-done((bf16[6,1536]{1,0:T(8,128)(2,1)S(1)}, bf16[6,1536]{1,0:T(8,128)(2,1)S(1)}, u32[]{:S(2)}, u32[]{:S(2)}) %collective-permute-start) | collective-permute-done | bytes 18464 | tf_op jit(solution)/shard_map/ppermute | solution.py:397
  144.1 0.7 collective-permute-start.1
  144.9 3.5 %collective-permute-done.1.other_ref = bf16[12,1536]{1,0:T(8,128)(2,1)S(1)} collective-permute-done((bf16[12,1536]{1,0:T(8,128)(2,1)S(1)}, bf16[12,1536]{1,0:T(8,128)(2,1)S(1)}, u32[]{:S(2)}, u32[]{:S(2)}) %collective-permute-start.1) | collective-permute-done | bytes 36896 | tf_op jit(solution)/shard_map/ppermute | solution.py:397
  148.4 4.9 %collective-permute-start.2 = (bf16[24,1536]{1,0:T(8,128)(2,1)S(1)}, bf16[24,1536]{1,0:T(8,128)(2,1)S(1)}, u32[]{:S(2)}, u32[]{:S(2)}) collective-permute-start(bf16[24,1536]{1,0:T(8,128)(2,1)S(1)} %shard_map.152.mine_ref), channel_id=1, source_target_pairs={{0,4},{1,5},{2,6},{3,7},{4,0},{5,1},{6,2},{7,3},{8,12},{9,13},{10,... | collective-permute-start | bytes 221192 | tf_op jit(solution)/shard_map/ppermute | solution.py:397
  153.3 2.3 collective-permute-done.2.other_ref
  155.6 1.0 collective-permute-start.3
  156.6 3.1 %collective-permute-done.3.other_ref = bf16[48,1536]{1,0:T(8,128)(2,1)S(1)} collective-permute-done((bf16[48,1536]{1,0:T(8,128)(2,1)S(1)}, bf16[48,1536]{1,0:T(8,128)(2,1)S(1)}, u32[]{:S(2)}, u32[]{:S(2)}) %collective-permute-start.3) | collective-permute-done | bytes 147488 | tf_op jit(solution)/shard_map/ppermute | solution.py:397
  159.7 2.5 collective-permute-start.4
  162.2 6.3 %collective-permute-done.4.other_ref = bf16[96,1536]{1,0:T(8,128)(2,1)S(1)} collective-permute-done((bf16[96,1536]{1,0:T(8,128)(2,1)S(1)}, bf16[96,1536]{1,0:T(8,128)(2,1)S(1)}, u32[]{:S(2)}, u32[]{:S(2)}) %collective-permute-start.4) | collective-permute-done | bytes 294944 | tf_op jit(solution)/shard_map/ppermute | solution.py:397
  168.5 2.8 %collective-permute-start.6 = (bf16[192,1536]{1,0:T(8,128)(2,1)S(1)}, bf16[192,1536]{1,0:T(8,128)(2,1)S(1)}, u32[]{:S(2)}, u32[]{:S(2)}) collective-permute-start(bf16[192,1536]{1,0:T(8,128)(2,1)S(1)} %shard_map.155.refs_0_), channel_id=1, source_target_pairs={{0,128},{32,160},{64,192},{96,224},{128,0},{160,32},{192,64},{224,... | collective-permute-start | bytes 1769480 | tf_op jit(solution)/shard_map/ppermute | solution.py:401
  171.3 0.9 collective-permute-start.7
  172.2 0.6 collective-permute-start.5
  172.8 6.4 %select_reduce_fusion = (s32[96,256]{1,0:T(8,128)S(1)}, s32[96,256]{1,0:T(8,128)S(1)}) fusion(s32[96,96]{1,0:T(8,128)S(1)} %copy-done.19, s32[96]{0:T(128)S(1)} %iota_add_fusion, s32[96,96]{1,0:T(8,128)S(1)} %copy-done.21), kind=kLoop, calls=%fused_computation | loop fusion | flops 14106624 | bytes 270720 | tf_op jit(solution)/shard_map/reduce_sum | solution.py:243
  179.3 5.5 %collective-permute-start.8 = (bf16[192,1536]{1,0:T(8,128)(2,1)S(1)}, bf16[192,1536]{1,0:T(8,128)(2,1)S(1)}, u32[]{:S(2)}, u32[]{:S(2)}) collective-permute-start(bf16[192,1536]{1,0:T(8,128)(2,1)S(1)} %shard_map.155.refs_0_), channel_id=1, source_target_pairs={{0,32},{32,0},{64,96},{96,64},{128,160},{160,128},{192,224},{224,1... | collective-permute-start | bytes 1769480 | tf_op jit(solution)/shard_map/ppermute | solution.py:404
  184.8 6.1 %collective-permute-start.10 = (bf16[192,1536]{1,0:T(8,128)(2,1)S(1)}, bf16[192,1536]{1,0:T(8,128)(2,1)S(1)}, u32[]{:S(2)}, u32[]{:S(2)}) collective-permute-start(bf16[192,1536]{1,0:T(8,128)(2,1)S(1)} %collective-permute-done.6.refs_2_), channel_id=1, source_target_pairs={{0,32},{32,0},{64,96},{96,64},{128,160},{160,128},{192,224},{224,1... | collective-permute-start | bytes 1769480 | tf_op jit(solution)/shard_map/ppermute | solution.py:404
  190.9 6.1 %collective-permute-done.7.refs_3_ = bf16[192,1536]{1,0:T(8,128)(2,1)S(1)} collective-permute-done((bf16[192,1536]{1,0:T(8,128)(2,1)S(1)}, bf16[192,1536]{1,0:T(8,128)(2,1)S(1)}, u32[]{:S(2)}, u32[]{:S(2)}) %collective-permute-start.7) | collective-permute-done | bytes 589856 | tf_op jit(solution)/shard_map/ppermute | solution.py:401
  197.1 1.6 collective-permute-start.11
  198.6 0.0 collective-permute-start.9
  198.6 0.1 add_multiply_fusion.start_ref
  198.8 1.5 collective-permute-done.11.refs_7_
  200.3 0.8 collective-permute-done.9.refs_5_
  201.1 0.8 shard_map.156
  202.0 2.1 copy-done
  204.1 2.7 copy.28
  206.8 1.4 copy.29
  208.2 3.3 %reshape.119 = bf16[32,3,2,3,1536]{4,3,2,1,0:T(4,128)(2,1)S(1)} reshape(bf16[32,216,128]{2,1,0:T(8,128)(2,1)} %all-to-all-done.1) | data formatting | bytes 3538944 | tf_op jit(solution)/shard_map/reshape | solution.py:439
  211.6 2.2 copy.25
  213.8 5.5 %reshape.120 = bf16[576,1536]{1,0:T(8,128)(2,1)} reshape(bf16[2,3,32,3,1536]{4,3,2,1,0:T(4,128)(2,1)} %copy.25) | data formatting | bytes 3538944 | tf_op jit(solution)/shard_map/reshape | solution.py:441
  219.3 5.4 %convolution_convert_fusion = bf16[576,1536]{1,0:T(8,128)(2,1)S(1)} fusion(bf16[576,1536]{1,0:T(8,128)(2,1)S(1)} %bitcast.61, bf16[1536,1536]{1,0:T(8,128)(2,1)} %copy-done), kind=kOutput, calls=%fused_computation.4 | convolution fusion | flops 2718793728 | bytes 8257536 | tf_op jit(solution)/shard_map/dot_general | solution.py:448
  224.8 0.0 copy-start.9
  224.8 2.9 %convolution_convert_fusion.1 = bf16[576,1536]{1,0:T(8,128)(2,1)S(1)} fusion(bf16[576,1536]{1,0:T(8,128)(2,1)S(1)} %copy-done.17, bf16[1536,1536]{1,0:T(8,128)(2,1)S(1)} %bitcast.43), kind=kOutput, calls=%fused_computation.5 | convolution fusion | flops 2718793728 | bytes 8257536 | tf_op jit(solution)/shard_map/dot_general | solution.py:440
  227.8 0.0 copy-start.11
  227.8 9.7 %shard_map.158.row_ref = f32[48,256]{1,0:T(8,128)S(1)} custom-call(bf16[6,4608,96]{2,1,0:T(8,128)(2,1)S(1)} %bitcast.56, bf16[6,96,1536]{2,1,0:T(8,128)(2,1)S(1)} %bitcast.50, bf16[6,96,1536]{2,1,0:T(8,128)(2,1)S(1)} %bitcast.54, s32[96,256]{1,0:T(8,128)S(1)} %broadcast_add_fusion.index_ref), custom_call_target="tpu_custom_call" | custom-call | flops 5435817984 | bytes 20000000 | tf_op jit(solution)/shard_map/pallas_call | solution.py:220
  237.5 10.8 %shard_map.157 = (bf16[6,96,1536]{2,1,0:T(8,128)(2,1)}, f32[48,256]{1,0:T(8,128)S(1)}) custom-call(bf16[6,4608,96]{2,1,0:T(8,128)(2,1)S(1)} %bitcast.58, bf16[6,96,1536]{2,1,0:T(8,128)(2,1)S(1)} %bitcast.53, bf16[6,96,1536]{2,1,0:T(8,128)(2,1)S(1)} %bitcast.52, s32[96,256]{1,0:T(8,128)S(1)} %broadcast_add_fusion.1.index_ref), custom_call_target="tpu_custom_call" | custom-call | flops 5435817984 | bytes 20000000 | tf_op jit(solution)/shard_map/pallas_call | solution.py:220
  248.3 0.6 copy-done.2
  248.9 2.8 shard_map.159
  251.7 16.3 %all_to_all.38 = f32[32,8,128]{2,1,0:T(8,128)S(1)} all-to-all(f32[32,8,128]{2,1,0:T(8,128)} %bitcast.64), channel_id=1, replica_groups=mesh['dp'=8,'grid'=32] {'grid'}, dimensions={0} | all-to-all | bytes 262144 | tf_op jit(solution)/shard_map/all_to_all | solution.py:357
  268.1 10.6 %all_to_all.39.got_ref = f32[8,8,128]{2,1,0:T(8,128)} all-to-all(f32[8,8,128]{2,1,0:T(8,128)S(1)} %broadcast_in_dim.72), channel_id=1, replica_groups=mesh['dp'=8,'grid'=32] {'dp'}, dimensions={0} | all-to-all | bytes 65536 | tf_op jit(solution)/shard_map/all_to_all | solution.py:359
  278.7 1.4 shard_map.160
  (63 shorter events, 0.3 us)
Async XLA Ops:
  2.2 21.2 %all-to-all-start = ((f32[32,8,128]{2,1,0:T(8,128)}), f32[32,8,128]{2,1,0:T(8,128)S(1)}, u32[]{:S(2)}, u32[]{:S(2)}) async-start(f32[32,8,128]{2,1,0:T(8,128)} %shard_map.147), calls=%async_computation | async-start | bytes 262144 | tf_op jit(solution)/shard_map/all_to_all | solution.py:340
  16.2 0.6 copy-start.20
  23.4 0.6 copy-start.18
  26.2 1.5 copy-start.4
  27.7 1.5 copy-start.5
  29.2 1.5 copy-start.10
  30.7 0.8 copy-start.12
  44.5 2.8 %copy-start.15 = (bf16[6,4608,96]{2,1,0:T(8,128)(2,1)}, bf16[6,4608,96]{2,1,0:T(8,128)(2,1)S(1)}, u32[]{:S(2)}) copy-start(bf16[6,4608,96]{2,1,0:T(8,128)(2,1)S(1)} %get-tuple-element.16.p_ref) | copy-start | bytes 15925252
  50.3 5.8 %copy-start.6 = (bf16[2,3,96,1536]{3,2,1,0:T(8,128)(2,1)S(1)}, bf16[2,3,96,1536]{3,2,1,0:T(8,128)(2,1)}, u32[]{:S(2)}) copy-start(bf16[2,3,96,1536]{3,2,1,0:T(8,128)(2,1)} %param.12) | copy-start | bytes 5308420
  50.3 5.8 %copy-start.7 = (bf16[2,3,96,1536]{3,2,1,0:T(8,128)(2,1)S(1)}, bf16[2,3,96,1536]{3,2,1,0:T(8,128)(2,1)}, u32[]{:S(2)}) copy-start(bf16[2,3,96,1536]{3,2,1,0:T(8,128)(2,1)} %param.13) | copy-start | bytes 5308420
  50.3 45.9 %all-to-all-start.2 = ((bf16[2,3,96,1536]{3,0,1,2:T(2,128)(2,1)}), bf16[2,3,96,1536]{3,0,1,2:T(2,128)(2,1)}, u32[]{:S(2)}, u32[]{:S(2)}) async-start(bf16[2,3,96,1536]{3,0,1,2:T(2,128)(2,1)} %copy.26), calls=%async_computation.2 | async-start | bytes 3538944 | tf_op jit(solution)/shard_map/all_to_all | solution.py:435
  56.1 1.5 copy-start.8
  57.6 0.8 copy-start.13
  73.0 2.9 %copy-start.14 = (bf16[6,4608,96]{2,1,0:T(8,128)(2,1)}, bf16[6,4608,96]{2,1,0:T(8,128)(2,1)S(1)}, u32[]{:S(2)}) copy-start(bf16[6,4608,96]{2,1,0:T(8,128)(2,1)S(1)} %get-tuple-element.20.p_ref) | copy-start | bytes 15925252
  96.2 7.9 %copy-start.3 = (bf16[6,1536]{1,0:T(8,128)(2,1)S(1)}, bf16[6,1536]{1,0:T(8,128)(2,1)}, u32[]{:S(2)}) copy-start(bf16[6,1536]{1,0:T(8,128)(2,1)} %mine_ref.1) | copy-start | bytes 55300
  96.2 112.0 %all-to-all-start.1 = ((bf16[32,216,128]{2,1,0:T(8,128)(2,1)}), bf16[32,216,128]{2,1,0:T(8,128)(2,1)}, u32[]{:S(2)}, u32[]{:S(2)}) async-start(bf16[32,216,128]{2,1,0:T(8,128)(2,1)} %get-tuple-element.17), calls=%async_computation.1 | async-start | bytes 3538944 | tf_op jit(solution)/shard_map/all_to_all | solution.py:429
  104.1 68.7 %copy-start.19 = (s32[96,96]{1,0:T(8,128)S(1)}, s32[96,96]{1,0:T(8,128)}, u32[]{:S(2)}) copy-start(s32[96,96]{1,0:T(8,128)} %get-tuple-element.28) | copy-start | bytes 110596
  104.1 68.7 %copy-start.21 = (s32[96,96]{1,0:T(8,128)S(1)}, s32[96,96]{1,0:T(8,128)}, u32[]{:S(2)}) copy-start(s32[96,96]{1,0:T(8,128)} %copy-done.20) | copy-start | bytes 110596
  104.1 40.0 %collective-permute-start = (bf16[6,1536]{1,0:T(8,128)(2,1)S(1)}, bf16[6,1536]{1,0:T(8,128)(2,1)S(1)}, u32[]{:S(2)}, u32[]{:S(2)}) collective-permute-start(bf16[6,1536]{1,0:T(8,128)(2,1)S(1)} %copy-done.3), channel_id=1, source_target_pairs={{0,1},{1,0},{2,3},{3,2},{4,5},{5,4},{6,7},{7,6},{8,9},{9,8},{10,11... | collective-permute-start | bytes 55304 | tf_op jit(solution)/shard_map/ppermute | solution.py:397
  144.1 4.2 %collective-permute-start.1 = (bf16[12,1536]{1,0:T(8,128)(2,1)S(1)}, bf16[12,1536]{1,0:T(8,128)(2,1)S(1)}, u32[]{:S(2)}, u32[]{:S(2)}) collective-permute-start(bf16[12,1536]{1,0:T(8,128)(2,1)S(1)} %shard_map.151.mine_ref), channel_id=1, source_target_pairs={{0,2},{1,3},{2,0},{3,1},{4,6},{5,7},{6,4},{7,5},{8,10},{9,11},{10,... | collective-permute-start | bytes 110600 | tf_op jit(solution)/shard_map/ppermute | solution.py:397
  148.4 7.2 %collective-permute-start.2 = (bf16[24,1536]{1,0:T(8,128)(2,1)S(1)}, bf16[24,1536]{1,0:T(8,128)(2,1)S(1)}, u32[]{:S(2)}, u32[]{:S(2)}) collective-permute-start(bf16[24,1536]{1,0:T(8,128)(2,1)S(1)} %shard_map.152.mine_ref), channel_id=1, source_target_pairs={{0,4},{1,5},{2,6},{3,7},{4,0},{5,1},{6,2},{7,3},{8,12},{9,13},{10,... | collective-permute-start | bytes 221192 | tf_op jit(solution)/shard_map/ppermute | solution.py:397
  155.6 4.1 %collective-permute-start.3 = (bf16[48,1536]{1,0:T(8,128)(2,1)S(1)}, bf16[48,1536]{1,0:T(8,128)(2,1)S(1)}, u32[]{:S(2)}, u32[]{:S(2)}) collective-permute-start(bf16[48,1536]{1,0:T(8,128)(2,1)S(1)} %shard_map.153.mine_ref), channel_id=1, source_target_pairs={{0,8},{1,9},{2,10},{3,11},{4,12},{5,13},{6,14},{7,15},{8,0},{9,1},... | collective-permute-start | bytes 442376 | tf_op jit(solution)/shard_map/ppermute | solution.py:397
  159.7 8.7 %collective-permute-start.4 = (bf16[96,1536]{1,0:T(8,128)(2,1)S(1)}, bf16[96,1536]{1,0:T(8,128)(2,1)S(1)}, u32[]{:S(2)}, u32[]{:S(2)}) collective-permute-start(bf16[96,1536]{1,0:T(8,128)(2,1)S(1)} %shard_map.154.mine_ref), channel_id=1, source_target_pairs={{0,16},{1,17},{2,18},{3,19},{4,20},{5,21},{6,22},{7,23},{8,24},{9,... | collective-permute-start | bytes 884744 | tf_op jit(solution)/shard_map/ppermute | solution.py:397
  168.5 16.3 %collective-permute-start.6 = (bf16[192,1536]{1,0:T(8,128)(2,1)S(1)}, bf16[192,1536]{1,0:T(8,128)(2,1)S(1)}, u32[]{:S(2)}, u32[]{:S(2)}) collective-permute-start(bf16[192,1536]{1,0:T(8,128)(2,1)S(1)} %shard_map.155.refs_0_), channel_id=1, source_target_pairs={{0,128},{32,160},{64,192},{96,224},{128,0},{160,32},{192,64},{224,... | collective-permute-start | bytes 1769480 | tf_op jit(solution)/shard_map/ppermute | solution.py:401
  171.3 25.7 %collective-permute-start.7 = (bf16[192,1536]{1,0:T(8,128)(2,1)S(1)}, bf16[192,1536]{1,0:T(8,128)(2,1)S(1)}, u32[]{:S(2)}, u32[]{:S(2)}) collective-permute-start(bf16[192,1536]{1,0:T(8,128)(2,1)S(1)} %shard_map.155.refs_0_), channel_id=1, source_target_pairs={{0,192},{32,224},{64,0},{96,32},{128,64},{160,96},{192,128},{224,1... | collective-permute-start | bytes 1769480 | tf_op jit(solution)/shard_map/ppermute | solution.py:401
  172.2 26.4 %collective-permute-start.5 = (bf16[192,1536]{1,0:T(8,128)(2,1)S(1)}, bf16[192,1536]{1,0:T(8,128)(2,1)S(1)}, u32[]{:S(2)}, u32[]{:S(2)}) collective-permute-start(bf16[192,1536]{1,0:T(8,128)(2,1)S(1)} %shard_map.155.refs_0_), channel_id=1, source_target_pairs={{0,64},{32,96},{64,128},{96,160},{128,192},{160,224},{192,0},{224,... | collective-permute-start | bytes 1769480 | tf_op jit(solution)/shard_map/ppermute | solution.py:401
  179.3 19.5 %collective-permute-start.8 = (bf16[192,1536]{1,0:T(8,128)(2,1)S(1)}, bf16[192,1536]{1,0:T(8,128)(2,1)S(1)}, u32[]{:S(2)}, u32[]{:S(2)}) collective-permute-start(bf16[192,1536]{1,0:T(8,128)(2,1)S(1)} %shard_map.155.refs_0_), channel_id=1, source_target_pairs={{0,32},{32,0},{64,96},{96,64},{128,160},{160,128},{192,224},{224,1... | collective-permute-start | bytes 1769480 | tf_op jit(solution)/shard_map/ppermute | solution.py:404
  184.8 13.9 %collective-permute-start.10 = (bf16[192,1536]{1,0:T(8,128)(2,1)S(1)}, bf16[192,1536]{1,0:T(8,128)(2,1)S(1)}, u32[]{:S(2)}, u32[]{:S(2)}) collective-permute-start(bf16[192,1536]{1,0:T(8,128)(2,1)S(1)} %collective-permute-done.6.refs_2_), channel_id=1, source_target_pairs={{0,32},{32,0},{64,96},{96,64},{128,160},{160,128},{192,224},{224,1... | collective-permute-start | bytes 1769480 | tf_op jit(solution)/shard_map/ppermute | solution.py:404
  197.1 3.2 %collective-permute-start.11 = (bf16[192,1536]{1,0:T(8,128)(2,1)S(1)}, bf16[192,1536]{1,0:T(8,128)(2,1)S(1)}, u32[]{:S(2)}, u32[]{:S(2)}) collective-permute-start(bf16[192,1536]{1,0:T(8,128)(2,1)S(1)} %collective-permute-done.7.refs_3_), channel_id=1, source_target_pairs={{0,32},{32,0},{64,96},{96,64},{128,160},{160,128},{192,224},{224,1... | collective-permute-start | bytes 1769480 | tf_op jit(solution)/shard_map/ppermute | solution.py:404
  198.6 2.5 collective-permute-start.9
  201.9 2.1 copy-start
  213.8 5.5 %copy-start.16 = (bf16[2,3,96,1536]{3,2,1,0:T(8,128)(2,1)S(1)}, bf16[2,3,96,1536]{3,2,1,0:T(8,128)(2,1)}, u32[]{:S(2)}) copy-start(bf16[2,3,96,1536]{3,2,1,0:T(8,128)(2,1)} %copy.29) | copy-start | bytes 5308420
  213.8 10.9 %slice-start = ((s8[4718592]{0:T(1024)(128)(4,1)}), s8[524288]{0:T(1024)(128)(4,1)S(1)}, s32[]{:S(2)}) async-start(s8[4718592]{0:T(1024)(128)(4,1)} %bitcast.42), calls=%async_computation.5 | async-start | bytes 1048576
  219.3 5.5 %slice-start.1 = ((s8[4718592]{0:T(1024)(128)(4,1)}), s8[4194304]{0:T(1024)(128)(4,1)S(1)}, s32[]{:S(2)}) async-start(s8[4718592]{0:T(1024)(128)(4,1)} %bitcast.42), calls=%async_computation.6 | async-start | bytes 8388608
  219.3 5.5 %copy-start.17 = (bf16[576,1536]{1,0:T(8,128)(2,1)S(1)}, bf16[576,1536]{1,0:T(8,128)(2,1)}, u32[]{:S(2)}) copy-start(bf16[576,1536]{1,0:T(8,128)(2,1)} %reshape.120) | copy-start | bytes 5308420
  219.3 8.4 %slice-start.2 = ((s8[7077888]{0:T(1024)(128)(4,1)}), s8[2883584]{0:T(1024)(128)(4,1)S(1)}, s32[]{:S(2)}) async-start(s8[7077888]{0:T(1024)(128)(4,1)} %bitcast.55), calls=%async_computation.7 | async-start | bytes 5767168
  219.3 18.2 %slice-start.4 = ((s8[7077888]{0:T(1024)(128)(4,1)}), s8[4194304]{0:T(1024)(128)(4,1)S(1)}, s32[]{:S(2)}) async-start(s8[7077888]{0:T(1024)(128)(4,1)} %bitcast.57), calls=%async_computation.9 | async-start | bytes 8388608
  224.8 3.0 %copy-start.9 = (bf16[2,3,96,1536]{3,2,1,0:T(8,128)(2,1)S(1)}, bf16[2,3,96,1536]{3,2,1,0:T(8,128)(2,1)}, u32[]{:S(2)}) copy-start(bf16[2,3,96,1536]{3,2,1,0:T(8,128)(2,1)} %param.14) | copy-start | bytes 5308420
  224.8 2.9 %slice-start.3 = ((s8[7077888]{0:T(1024)(128)(4,1)}), s8[4194304]{0:T(1024)(128)(4,1)S(1)}, s32[]{:S(2)}) async-start(s8[7077888]{0:T(1024)(128)(4,1)} %bitcast.55), calls=%async_computation.8 | async-start | bytes 8388608
  224.8 12.7 %slice-start.5 = ((s8[7077888]{0:T(1024)(128)(4,1)}), s8[2883584]{0:T(1024)(128)(4,1)S(1)}, s32[]{:S(2)}) async-start(s8[7077888]{0:T(1024)(128)(4,1)} %bitcast.57), calls=%async_computation.10 | async-start | bytes 5767168
  227.8 9.8 %copy-start.11 = (bf16[2,96,3,1536]{3,1,2,0:T(8,128)(2,1)S(1)}, bf16[2,96,3,1536]{3,1,2,0:T(8,128)(2,1)}, u32[]{:S(2)}) copy-start(bf16[2,96,3,1536]{3,1,2,0:T(8,128)(2,1)} %param.17) | copy-start | bytes 5308420
  237.5 10.8 %copy-start.1 = (f32[48,256]{1,0:T(8,128)}, f32[48,256]{1,0:T(8,128)S(1)}, u32[]{:S(2)}) copy-start(f32[48,256]{1,0:T(8,128)S(1)} %shard_map.158.row_ref) | copy-start | bytes 147460
  248.3 0.6 copy-start.2

commit v4 on v3

--- a/solution.py
+++ b/solution.py
@@ -158,7 +158,18 @@
 
     @pl.when(pl.program_id(0) == pl.num_programs(0) - 1)
     def _():
-        low, high = index_ref[:, :LANES], index_ref[:, LANES:]
+        lane = lax.broadcasted_iota(jnp.int32, (G, LANES), 1)
+        spot = lax.broadcasted_iota(jnp.int32, (G, LANES), 0)
+        position = jnp.broadcast_to(index_ref[...], (G, LANES))
+        inverse = jnp.sum(jnp.where(position == lane, spot, 0), axis=0, keepdims=True)
+        inverse = jnp.broadcast_to(inverse, (G, LANES))
+
+        def at(offset):
+            place = offset + position - (G - 1)
+            found = pick(inverse, jnp.bitwise_and(place, LANES - 1))
+            return jnp.where((place >= 0) & (place < G), found, LANES - 1)
+
+        low, high = at(lane), at(lane + LANES)
 
         def gather(block, carry):
             lows, highs = [], []
@@ -199,7 +210,6 @@
     return pl.pallas_call(
         kernel,
         grid=(n,),
-        compiler_params=pltpu.CompilerParams(vmem_limit_bytes=GRANT),
         in_specs=[each(BLOCK)] * 3 + [whole((NH, 2 * LANES)), whole((G, LANES))],
         out_specs=[each(PSHAPE), spec],
         out_shape=[
@@ -221,7 +231,7 @@
         functools.partial(backward_kernel, attend=attend),
         grid=(n,),
         compiler_params=pltpu.CompilerParams(vmem_limit_bytes=GRANT),
-        in_specs=[each(PSHAPE), each(BLOCK), each(BLOCK), whole((G, 2 * LANES))],
+        in_specs=[each(PSHAPE), each(BLOCK), each(BLOCK), whole((G, 1))],
         out_specs=specs + [whole((NH, 2 * LANES))],
         out_shape=shapes + [jax.ShapeDtypeStruct((NH, 2 * LANES), jnp.float32)],
         scratch_shapes=[pltpu.VMEM((NH * G, LANES), jnp.float32)],
@@ -234,13 +244,6 @@
 def levels(positions):
     level = positions[None, :] - positions[:, None] + (G - 1)
     return jnp.pad(level, ((0, 0), (0, LANES - G)))
-
-
-def fold_index(positions):
-    level = positions[None, :] - positions[:, None] + (G - 1)
-    hit = level[:, :, None] == jnp.arange(2 * LANES)[None, None, :]
-    spot = jnp.arange(G, dtype=jnp.int32)[None, :, None] - (LANES - 1)
-    return jnp.sum(jnp.where(hit, spot, 0), axis=1) + (LANES - 1)
 
 
 def assemble_kernel(start_ref, *refs):
@@ -432,16 +435,16 @@
     p_col, d_values = attention_forward(
         cols(q_col), cols(k_col), grad_cols, table, levels(row_positions), True
     )
-    d_rows = lax.all_to_all(
-        d_values.reshape(images, col_count, G, D), "grid", split_axis=2, concat_axis=1, tiled=True
-    )
+    d_values = d_values.reshape(images, col_count, G, D)
+    d_rows = lax.all_to_all(d_values, "grid", split_axis=2, concat_axis=1, tiled=True)
 
     col_tokens = col_out.reshape(GRID, col_count, images, row_count, D).transpose(2, 1, 0, 3, 4)
+    col_tokens = col_tokens.reshape(-1, D)
     value_cols = jnp.dot(
-        col_tokens.reshape(-1, D), whole_weight, preferred_element_type=jnp.float32
+        col_tokens, whole_weight, preferred_element_type=jnp.float32
     ).astype(jnp.bfloat16).reshape(images * col_count, G, D)
     attended, col_table = attention_backward(
-        p_col, value_cols, grad_cols, fold_index(row_positions), True
+        p_col, value_cols, grad_cols, row_positions[:, None], True
     )
     attended = attended.reshape(images, col_count, G, D).transpose(0, 2, 1, 3)
 
@@ -450,9 +453,7 @@
         preferred_element_type=jnp.float32,
     )
     d_row_out = d_flat.astype(jnp.bfloat16).reshape(images * row_count, G, D)
-    (row_table,) = attention_backward(
-        p_row, rows(v_row), d_row_out, fold_index(col_positions), False
-    )
+    (row_table,) = attention_backward(p_row, rows(v_row), d_row_out, col_positions[:, None], False)
 
     batch_size = lax.axis_size("dp") * images
     grads = unit_grads(units, coords, squashed, row_table, col_table, 1.0 / (batch_size * G))

time: 281 us -> 278 us (0.989)
  local copies, waits for them, and re-layouts: 36.9 us -> 26.8 us
  other arithmetic: 8.05 us -> 1.04 us
  Pallas kernels: 57 us -> 62.7 us
  waiting for transfers between devices: 89.1 us -> 94.1 us
  starting transfers between devices: 52.8 us -> 56.2 us
    unnamed x56 -> x42, local copies, waits for them, and re-layouts: 17.3 us -> 5.27 us
    reduce_sum x1 -> x0, other arithmetic: 6.44 us -> none  [fold_index(): return jnp.sum(jnp.where(hit, spot, 0), axis=1) + (LANES - 1)]
    ppermute x4, starting transfers between devices: 13.2 us -> 17.5 us  [fetch_weight(): other.append(lax.ppermute(mine[step], 'dp', along_x(0, 1)))]
    pallas_call x2, Pallas kernels: 27.6 us -> 31.7 us  [attention_forward(): pl.pallas_call(kernel, grid=(n,), in_specs=[each(BLOCK)] * 3 + [whole((NH...]
    all_to_all x1, waiting for transfers between devices: 20.3 us -> 23.8 us  [shards(): lax.all_to_all(d_values, 'grid', split_axis=2, concat_axis=1, tiled=True)]
  transfers between devices with their start and end apart: 15 -> 15, of which waited for: 10 -> 11; matrix products, arithmetic and copies ran while one was open for 5% -> 3% of each run, Pallas kernels for 6% -> 7%
where the time goes in v4:
time: 278 us; the launch traced here: 277 us
  waiting for transfers between devices  94.1 us (34%)
  Pallas kernels  62.7 us (23%)
  starting transfers between devices  56.2 us (20%)
  local copies, waits for them, and re-layouts  26.8 us (10%)
  blocking collectives  26.8 us (10%)
  matrix products  8.33 us (3%)
    ppermute x5, waiting for transfers between devices, fetch_weight(): other = lax.ppermute(part, 'grid', [(g, g ^ 1 << bit) for g in range(GRID)])  53.9 us
    pallas_call x2, Pallas kernels, attention_forward(): pl.pallas_call(kernel, grid=(n,), in_specs=[each(BLOCK)] * 3 + [whole((NH...  31.7 us
    all_to_all x1, waiting for transfers between devices, shards(): lax.all_to_all(d_values, 'grid', split_axis=2, concat_axis=1, tiled=True)  23.8 us
    pallas_call x2, Pallas kernels, attention_backward(): pl.pallas_call(functools.partial(backward_kernel, attend=attend), grid=(n...  21.4 us
    ppermute x4, starting transfers between devices, fetch_weight(): other.append(lax.ppermute(mine[step], 'dp', along_x(0, 1)))  17.5 us
    all_to_all x1, blocking collectives, reduce_units(): lax.all_to_all(grads.reshape(GRID, HALF, LANES), 'grid', 0, 0, tiled=True)  16.2 us
    all_to_all x1, starting transfers between devices, gather_units(): got = lax.all_to_all(tiles, 'grid', 0, 0, tiled=True)  12 us
    all_to_all x1, blocking collectives, reduce_units(): got = lax.all_to_all(own, 'dp', 0, 0, tiled=True)  10.5 us
  transfers between devices with their start and end apart: 15, of which 11 were waited for; matrix products, arithmetic and copies ran while one was open for 3% of the time, Pallas kernels for 7%

profile of v4, /device:TPU:1, one launch (start us, length us, event | category | flops | bytes accessed | tf_op | source)
XLA Modules:
  0.0 277.1 jit_solution(4332643644077551094)
XLA Ops:
  0.6 1.5 shard_map.147
  2.2 12.0 %all-to-all-start = ((f32[32,8,128]{2,1,0:T(8,128)}), f32[32,8,128]{2,1,0:T(8,128)S(1)}, u32[]{:S(2)}, u32[]{:S(2)}) async-start(f32[32,8,128]{2,1,0:T(8,128)} %shard_map.147), calls=%async_computation | async-start | bytes 262144 | tf_op jit(solution)/shard_map/all_to_all | solution.py:343
  14.2 0.6 pad.11
  14.8 0.8 subtract_add_fusion.1
  15.6 0.6 pad.12.level_ref
  16.2 7.1 %all-to-all-done = f32[32,8,128]{2,1,0:T(8,128)S(1)} async-done(((f32[32,8,128]{2,1,0:T(8,128)}), f32[32,8,128]{2,1,0:T(8,128)S(1)}, u32[]{:S(2)}, u32[]{:S(2)}) %all-to-all-start) | async-done | bytes 131104 | tf_op jit(solution)/shard_map/all_to_all | solution.py:343
  23.4 0.6 copy-done.12
  24.0 2.2 shard_map.148
  26.2 15.3 %shard_map.149 = (bf16[6,4608,96]{2,1,0:T(8,128)(2,1)}, bf16[6,96,1536]{2,1,0:T(8,128)(2,1)}) custom-call(bf16[6,96,1536]{2,1,0:T(8,128)(2,1)} %bitcast.70, bf16[6,96,1536]{2,1,0:T(8,128)(2,1)} %bitcast.71, bf16[6,96,1536]{2,1,0:T(8,128)(2,1)} %bitcast.48, f32[48,256]{1,0:T(8,128)} %get-tuple-element.15.table_ref, s32[96,128]{1,0:T(8,128)} %pad.12.level_ref), custom_call_target="tpu_custom_call" | custom-call | flops 5435817984 | bytes 20000000 | tf_op jit(solution)/shard_map/pallas_call | solution.py:210
  41.5 4.5 %copy.26 = bf16[2,3,96,1536]{3,0,1,2:T(2,128)(2,1)} copy(bf16[2,3,96,1536]{3,2,1,0:T(8,128)(2,1)} %bitcast.60) | data formatting | bytes 3538944 | tf_op jit(solution)/shard_map/reshape | solution.py:438
  46.1 4.1 %all-to-all-start.2 = ((bf16[2,3,96,1536]{3,0,1,2:T(2,128)(2,1)}), bf16[2,3,96,1536]{3,0,1,2:T(2,128)(2,1)S(1)}, u32[]{:S(2)}, u32[]{:S(2)}) async-start(bf16[2,3,96,1536]{3,0,1,2:T(2,128)(2,1)} %copy.26), calls=%async_computation.2 | async-start | bytes 3538944 | tf_op jit(solution)/shard_map/all_to_all | solution.py:439
  50.2 0.1 subtract_add_fusion
  50.3 0.6 pad.13.level_ref
  50.9 16.4 %shard_map.150 = (bf16[6,4608,96]{2,1,0:T(8,128)(2,1)}, bf16[32,216,128]{2,1,0:T(8,128)(2,1)}) custom-call(bf16[6,96,1536]{2,1,0:T(8,128)(2,1)} %bitcast.72, bf16[6,96,1536]{2,1,0:T(8,128)(2,1)} %bitcast.73, bf16[6,96,1536]{2,1,0:T(8,128)(2,1)} %bitcast.46, f32[48,256]{1,0:T(8,128)} %get-tuple-element.15.table_ref, s32[96,128]{1,0:T(8,128)} %pad.13.level_ref), custom_call_target="tpu_custom_call" | custom-call | flops 5435817984 | bytes 20000000 | tf_op jit(solution)/shard_map/pallas_call | solution.py:210
  67.3 23.8 %all-to-all-done.2 = bf16[2,3,96,1536]{3,0,1,2:T(2,128)(2,1)S(1)} async-done(((bf16[2,3,96,1536]{3,0,1,2:T(2,128)(2,1)}), bf16[2,3,96,1536]{3,0,1,2:T(2,128)(2,1)S(1)}, u32[]{:S(2)}, u32[]{:S(2)}) %all-to-all-start.2) | async-done | bytes 1769504 | tf_op jit(solution)/shard_map/all_to_all | solution.py:439
  91.1 1.2 copy-done.8
  92.3 7.9 %all-to-all-start.1 = ((bf16[32,216,128]{2,1,0:T(8,128)(2,1)}), bf16[32,216,128]{2,1,0:T(8,128)(2,1)}, u32[]{:S(2)}, u32[]{:S(2)}) async-start(bf16[32,216,128]{2,1,0:T(8,128)(2,1)} %get-tuple-element.17), calls=%async_computation.1 | async-start | bytes 3538944 | tf_op jit(solution)/shard_map/all_to_all | solution.py:432
  100.2 0.0 copy-start.14
  100.2 1.3 collective-permute-start
  101.5 38.8 %collective-permute-done.other_ref = bf16[6,1536]{1,0:T(8,128)(2,1)S(1)} collective-permute-done((bf16[6,1536]{1,0:T(8,128)(2,1)S(1)}, bf16[6,1536]{1,0:T(8,128)(2,1)S(1)}, u32[]{:S(2)}, u32[]{:S(2)}) %collective-permute-start) | collective-permute-done | bytes 18464 | tf_op jit(solution)/shard_map/ppermute | solution.py:400
  140.3 0.7 collective-permute-start.1
  141.0 3.5 %collective-permute-done.1.other_ref = bf16[12,1536]{1,0:T(8,128)(2,1)S(1)} collective-permute-done((bf16[12,1536]{1,0:T(8,128)(2,1)S(1)}, bf16[12,1536]{1,0:T(8,128)(2,1)S(1)}, u32[]{:S(2)}, u32[]{:S(2)}) %collective-permute-start.1) | collective-permute-done | bytes 36896 | tf_op jit(solution)/shard_map/ppermute | solution.py:400
  144.5 4.9 %collective-permute-start.2 = (bf16[24,1536]{1,0:T(8,128)(2,1)S(1)}, bf16[24,1536]{1,0:T(8,128)(2,1)S(1)}, u32[]{:S(2)}, u32[]{:S(2)}) collective-permute-start(bf16[24,1536]{1,0:T(8,128)(2,1)S(1)} %shard_map.152.mine_ref), channel_id=1, source_target_pairs={{0,4},{1,5},{2,6},{3,7},{4,0},{5,1},{6,2},{7,3},{8,12},{9,13},{10,... | collective-permute-start | bytes 221192 | tf_op jit(solution)/shard_map/ppermute | solution.py:400
  149.4 2.3 collective-permute-done.2.other_ref
  151.7 1.0 collective-permute-start.3
  152.7 3.1 %collective-permute-done.3.other_ref = bf16[48,1536]{1,0:T(8,128)(2,1)S(1)} collective-permute-done((bf16[48,1536]{1,0:T(8,128)(2,1)S(1)}, bf16[48,1536]{1,0:T(8,128)(2,1)S(1)}, u32[]{:S(2)}, u32[]{:S(2)}) %collective-permute-start.3) | collective-permute-done | bytes 147488 | tf_op jit(solution)/shard_map/ppermute | solution.py:400
  155.8 2.5 collective-permute-start.4
  158.3 6.3 %collective-permute-done.4.other_ref = bf16[96,1536]{1,0:T(8,128)(2,1)S(1)} collective-permute-done((bf16[96,1536]{1,0:T(8,128)(2,1)S(1)}, bf16[96,1536]{1,0:T(8,128)(2,1)S(1)}, u32[]{:S(2)}, u32[]{:S(2)}) %collective-permute-start.4) | collective-permute-done | bytes 294944 | tf_op jit(solution)/shard_map/ppermute | solution.py:400
  164.6 2.8 %collective-permute-start.6 = (bf16[192,1536]{1,0:T(8,128)(2,1)S(1)}, bf16[192,1536]{1,0:T(8,128)(2,1)S(1)}, u32[]{:S(2)}, u32[]{:S(2)}) collective-permute-start(bf16[192,1536]{1,0:T(8,128)(2,1)S(1)} %shard_map.155.refs_0_), channel_id=1, source_target_pairs={{0,128},{32,160},{64,192},{96,224},{128,0},{160,32},{192,64},{224,... | collective-permute-start | bytes 1769480 | tf_op jit(solution)/shard_map/ppermute | solution.py:404
  167.5 0.9 collective-permute-start.7
  168.3 0.6 collective-permute-start.5
  169.0 5.5 %collective-permute-start.8 = (bf16[192,1536]{1,0:T(8,128)(2,1)S(1)}, bf16[192,1536]{1,0:T(8,128)(2,1)S(1)}, u32[]{:S(2)}, u32[]{:S(2)}) collective-permute-start(bf16[192,1536]{1,0:T(8,128)(2,1)S(1)} %shard_map.155.refs_0_), channel_id=1, source_target_pairs={{0,32},{32,0},{64,96},{96,64},{128,160},{160,128},{192,224},{224,1... | collective-permute-start | bytes 1769480 | tf_op jit(solution)/shard_map/ppermute | solution.py:407
  174.4 2.1 collective-permute-done.6.refs_2_
  176.6 10.5 %collective-permute-start.10 = (bf16[192,1536]{1,0:T(8,128)(2,1)S(1)}, bf16[192,1536]{1,0:T(8,128)(2,1)S(1)}, u32[]{:S(2)}, u32[]{:S(2)}) collective-permute-start(bf16[192,1536]{1,0:T(8,128)(2,1)S(1)} %collective-permute-done.6.refs_2_), channel_id=1, source_target_pairs={{0,32},{32,0},{64,96},{96,64},{128,160},{160,128},{192,224},{224,1... | collective-permute-start | bytes 1769480 | tf_op jit(solution)/shard_map/ppermute | solution.py:407
  187.1 6.1 %collective-permute-done.7.refs_3_ = bf16[192,1536]{1,0:T(8,128)(2,1)S(1)} collective-permute-done((bf16[192,1536]{1,0:T(8,128)(2,1)S(1)}, bf16[192,1536]{1,0:T(8,128)(2,1)S(1)}, u32[]{:S(2)}, u32[]{:S(2)}) %collective-permute-start.7) | collective-permute-done | bytes 589856 | tf_op jit(solution)/shard_map/ppermute | solution.py:404
  193.2 1.6 collective-permute-start.11
  194.8 0.0 collective-permute-done.5.refs_1_
  194.8 0.0 collective-permute-start.9
  194.8 0.7 copy.30.index_ref
  195.5 0.7 copy.25.index_ref
  196.2 0.1 add_multiply_fusion.start_ref
  196.3 0.2 collective-permute-done.11.refs_7_
  196.5 0.8 collective-permute-done.9.refs_5_
  197.4 1.6 shard_map.156
  198.9 2.1 copy-done
  201.1 1.2 copy.28
  202.3 1.5 copy.29
  203.8 3.3 %reshape.66 = bf16[32,3,2,3,1536]{4,3,2,1,0:T(4,128)(2,1)S(1)} reshape(bf16[32,216,128]{2,1,0:T(8,128)(2,1)} %all-to-all-done.1) | data formatting | bytes 3538944 | tf_op jit(solution)/shard_map/reshape | solution.py:441
  207.1 2.3 copy.24
  209.4 5.5 %reshape.67 = bf16[576,1536]{1,0:T(8,128)(2,1)} reshape(bf16[2,3,32,3,1536]{4,3,2,1,0:T(4,128)(2,1)} %copy.24) | data formatting | bytes 3538944 | tf_op jit(solution)/shard_map/reshape | solution.py:442
  214.9 0.0 slice-start.4
  214.9 5.4 %convolution_convert_fusion = bf16[576,1536]{1,0:T(8,128)(2,1)S(1)} fusion(bf16[576,1536]{1,0:T(8,128)(2,1)S(1)} %bitcast.59, bf16[1536,1536]{1,0:T(8,128)(2,1)} %copy-done), kind=kOutput, calls=%fused_computation | convolution fusion | flops 2718793728 | bytes 8257536 | tf_op jit(solution)/shard_map/dot_general | solution.py:451
  220.4 0.0 copy-start.6
  220.4 0.0 slice-start.5
  220.4 2.9 %convolution_convert_fusion.1 = bf16[576,1536]{1,0:T(8,128)(2,1)S(1)} fusion(bf16[576,1536]{1,0:T(8,128)(2,1)S(1)} %copy-done.11, bf16[1536,1536]{1,0:T(8,128)(2,1)S(1)} %bitcast.45), kind=kOutput, calls=%fused_computation.1 | convolution fusion | flops 2718793728 | bytes 8257536 | tf_op jit(solution)/shard_map/dot_general | solution.py:443
  223.4 0.0 copy-start.7
  223.4 10.2 %shard_map.158.row_ref = f32[48,256]{1,0:T(8,128)S(1)} custom-call(bf16[6,4608,96]{2,1,0:T(8,128)(2,1)S(1)} %bitcast.53, bf16[6,96,1536]{2,1,0:T(8,128)(2,1)S(1)} %bitcast.47, bf16[6,96,1536]{2,1,0:T(8,128)(2,1)S(1)} %bitcast.51, s32[96,1]{1,0:T(8,128)S(1)} %copy-done.4), custom_call_target="tpu_custom_call" | custom-call | flops 5435817984 | bytes 20000000 | tf_op jit(solution)/shard_map/pallas_call | solution.py:230
  233.6 0.6 copy-done.1
  234.2 11.2 %shard_map.157 = (bf16[6,96,1536]{2,1,0:T(8,128)(2,1)}, f32[48,256]{1,0:T(8,128)S(1)}) custom-call(bf16[6,4608,96]{2,1,0:T(8,128)(2,1)S(1)} %bitcast.55, bf16[6,96,1536]{2,1,0:T(8,128)(2,1)S(1)} %bitcast.50, bf16[6,96,1536]{2,1,0:T(8,128)(2,1)S(1)} %bitcast.49, s32[96,1]{1,0:T(8,128)S(1)} %copy-done.3), custom_call_target="tpu_custom_call" | custom-call | flops 5435817984 | bytes 20000000 | tf_op jit(solution)/shard_map/pallas_call | solution.py:230
  245.4 0.6 copy-done.2
  246.1 2.8 %shard_map.159 = f32[256,128]{1,0:T(8,128)} custom-call(f32[256,128]{1,0:T(8,128)} %bitcast.62, f32[1,256]{1,0:T(1,128)} %bitcast.65, f32[48,256]{1,0:T(8,128)} %get-tuple-element.19.squashed_ref, f32[48,256]{1,0:T(8,128)} %copy-done.1, f32[48,256]{1,0:T(8,128)} %copy-done.2), custom_call_target="tpu_custom_call" | custom-call | tf_op jit(solution)/shard_map/pallas_call | solution.py:353
  248.8 16.2 %all_to_all.38 = f32[32,8,128]{2,1,0:T(8,128)S(1)} all-to-all(f32[32,8,128]{2,1,0:T(8,128)} %bitcast.63), channel_id=1, replica_groups=mesh['dp'=8,'grid'=32] {'grid'}, dimensions={0} | all-to-all | bytes 262144 | tf_op jit(solution)/shard_map/all_to_all | solution.py:360
  265.1 10.5 %all_to_all.39.got_ref = f32[8,8,128]{2,1,0:T(8,128)} all-to-all(f32[8,8,128]{2,1,0:T(8,128)S(1)} %broadcast_in_dim.50), channel_id=1, replica_groups=mesh['dp'=8,'grid'=32] {'dp'}, dimensions={0} | all-to-all | bytes 65536 | tf_op jit(solution)/shard_map/all_to_all | solution.py:362
  275.7 1.4 shard_map.160
  (48 shorter events, 0.3 us)
Async XLA Ops:
  2.2 21.2 %all-to-all-start = ((f32[32,8,128]{2,1,0:T(8,128)}), f32[32,8,128]{2,1,0:T(8,128)S(1)}, u32[]{:S(2)}, u32[]{:S(2)}) async-start(f32[32,8,128]{2,1,0:T(8,128)} %shard_map.147), calls=%async_computation | async-start | bytes 262144 | tf_op jit(solution)/shard_map/all_to_all | solution.py:343
  23.4 0.6 copy-start.12
  46.1 4.1 %copy-start.13 = (s32[96]{0:T(128)S(1)}, s32[96]{0:T(128)}, u32[]{:S(2)}) copy-start(s32[96]{0:T(128)} %param.20) | copy-start | bytes 1156
  46.1 45.0 %all-to-all-start.2 = ((bf16[2,3,96,1536]{3,0,1,2:T(2,128)(2,1)}), bf16[2,3,96,1536]{3,0,1,2:T(2,128)(2,1)S(1)}, u32[]{:S(2)}, u32[]{:S(2)}) async-start(bf16[2,3,96,1536]{3,0,1,2:T(2,128)(2,1)} %copy.26), calls=%async_computation.2 | async-start | bytes 3538944 | tf_op jit(solution)/shard_map/all_to_all | solution.py:439
  91.1 1.2 copy-start.8
  92.3 7.9 %copy-start.5 = (bf16[6,1536]{1,0:T(8,128)(2,1)S(1)}, bf16[6,1536]{1,0:T(8,128)(2,1)}, u32[]{:S(2)}) copy-start(bf16[6,1536]{1,0:T(8,128)(2,1)} %mine_ref.1) | copy-start | bytes 55300
  92.3 111.4 %all-to-all-start.1 = ((bf16[32,216,128]{2,1,0:T(8,128)(2,1)}), bf16[32,216,128]{2,1,0:T(8,128)(2,1)}, u32[]{:S(2)}, u32[]{:S(2)}) async-start(bf16[32,216,128]{2,1,0:T(8,128)(2,1)} %get-tuple-element.17), calls=%async_computation.1 | async-start | bytes 3538944 | tf_op jit(solution)/shard_map/all_to_all | solution.py:432
  100.2 95.3 %copy-start.14 = (s32[96]{0:T(128)S(1)}, s32[96]{0:T(128)}, u32[]{:S(2)}) copy-start(s32[96]{0:T(128)} %param.19) | copy-start | bytes 1156
  100.2 40.0 %collective-permute-start = (bf16[6,1536]{1,0:T(8,128)(2,1)S(1)}, bf16[6,1536]{1,0:T(8,128)(2,1)S(1)}, u32[]{:S(2)}, u32[]{:S(2)}) collective-permute-start(bf16[6,1536]{1,0:T(8,128)(2,1)S(1)} %copy-done.5), channel_id=1, source_target_pairs={{0,1},{1,0},{2,3},{3,2},{4,5},{5,4},{6,7},{7,6},{8,9},{9,8},{10,11... | collective-permute-start | bytes 55304 | tf_op jit(solution)/shard_map/ppermute | solution.py:400
  140.3 4.2 %collective-permute-start.1 = (bf16[12,1536]{1,0:T(8,128)(2,1)S(1)}, bf16[12,1536]{1,0:T(8,128)(2,1)S(1)}, u32[]{:S(2)}, u32[]{:S(2)}) collective-permute-start(bf16[12,1536]{1,0:T(8,128)(2,1)S(1)} %shard_map.151.mine_ref), channel_id=1, source_target_pairs={{0,2},{1,3},{2,0},{3,1},{4,6},{5,7},{6,4},{7,5},{8,10},{9,11},{10,... | collective-permute-start | bytes 110600 | tf_op jit(solution)/shard_map/ppermute | solution.py:400
  144.5 7.2 %collective-permute-start.2 = (bf16[24,1536]{1,0:T(8,128)(2,1)S(1)}, bf16[24,1536]{1,0:T(8,128)(2,1)S(1)}, u32[]{:S(2)}, u32[]{:S(2)}) collective-permute-start(bf16[24,1536]{1,0:T(8,128)(2,1)S(1)} %shard_map.152.mine_ref), channel_id=1, source_target_pairs={{0,4},{1,5},{2,6},{3,7},{4,0},{5,1},{6,2},{7,3},{8,12},{9,13},{10,... | collective-permute-start | bytes 221192 | tf_op jit(solution)/shard_map/ppermute | solution.py:400
  151.7 4.1 %collective-permute-start.3 = (bf16[48,1536]{1,0:T(8,128)(2,1)S(1)}, bf16[48,1536]{1,0:T(8,128)(2,1)S(1)}, u32[]{:S(2)}, u32[]{:S(2)}) collective-permute-start(bf16[48,1536]{1,0:T(8,128)(2,1)S(1)} %shard_map.153.mine_ref), channel_id=1, source_target_pairs={{0,8},{1,9},{2,10},{3,11},{4,12},{5,13},{6,14},{7,15},{8,0},{9,1},... | collective-permute-start | bytes 442376 | tf_op jit(solution)/shard_map/ppermute | solution.py:400
  155.8 8.7 %collective-permute-start.4 = (bf16[96,1536]{1,0:T(8,128)(2,1)S(1)}, bf16[96,1536]{1,0:T(8,128)(2,1)S(1)}, u32[]{:S(2)}, u32[]{:S(2)}) collective-permute-start(bf16[96,1536]{1,0:T(8,128)(2,1)S(1)} %shard_map.154.mine_ref), channel_id=1, source_target_pairs={{0,16},{1,17},{2,18},{3,19},{4,20},{5,21},{6,22},{7,23},{8,24},{9,... | collective-permute-start | bytes 884744 | tf_op jit(solution)/shard_map/ppermute | solution.py:400
  164.6 11.9 %collective-permute-start.6 = (bf16[192,1536]{1,0:T(8,128)(2,1)S(1)}, bf16[192,1536]{1,0:T(8,128)(2,1)S(1)}, u32[]{:S(2)}, u32[]{:S(2)}) collective-permute-start(bf16[192,1536]{1,0:T(8,128)(2,1)S(1)} %shard_map.155.refs_0_), channel_id=1, source_target_pairs={{0,128},{32,160},{64,192},{96,224},{128,0},{160,32},{192,64},{224,... | collective-permute-start | bytes 1769480 | tf_op jit(solution)/shard_map/ppermute | solution.py:404
  167.5 25.7 %collective-permute-start.7 = (bf16[192,1536]{1,0:T(8,128)(2,1)S(1)}, bf16[192,1536]{1,0:T(8,128)(2,1)S(1)}, u32[]{:S(2)}, u32[]{:S(2)}) collective-permute-start(bf16[192,1536]{1,0:T(8,128)(2,1)S(1)} %shard_map.155.refs_0_), channel_id=1, source_target_pairs={{0,192},{32,224},{64,0},{96,32},{128,64},{160,96},{192,128},{224,1... | collective-permute-start | bytes 1769480 | tf_op jit(solution)/shard_map/ppermute | solution.py:404
  168.3 26.4 %collective-permute-start.5 = (bf16[192,1536]{1,0:T(8,128)(2,1)S(1)}, bf16[192,1536]{1,0:T(8,128)(2,1)S(1)}, u32[]{:S(2)}, u32[]{:S(2)}) collective-permute-start(bf16[192,1536]{1,0:T(8,128)(2,1)S(1)} %shard_map.155.refs_0_), channel_id=1, source_target_pairs={{0,64},{32,96},{64,128},{96,160},{128,192},{160,224},{192,0},{224,... | collective-permute-start | bytes 1769480 | tf_op jit(solution)/shard_map/ppermute | solution.py:404
  169.0 27.4 %collective-permute-start.8 = (bf16[192,1536]{1,0:T(8,128)(2,1)S(1)}, bf16[192,1536]{1,0:T(8,128)(2,1)S(1)}, u32[]{:S(2)}, u32[]{:S(2)}) collective-permute-start(bf16[192,1536]{1,0:T(8,128)(2,1)S(1)} %shard_map.155.refs_0_), channel_id=1, source_target_pairs={{0,32},{32,0},{64,96},{96,64},{128,160},{160,128},{192,224},{224,1... | collective-permute-start | bytes 1769480 | tf_op jit(solution)/shard_map/ppermute | solution.py:407
  176.6 19.8 %collective-permute-start.10 = (bf16[192,1536]{1,0:T(8,128)(2,1)S(1)}, bf16[192,1536]{1,0:T(8,128)(2,1)S(1)}, u32[]{:S(2)}, u32[]{:S(2)}) collective-permute-start(bf16[192,1536]{1,0:T(8,128)(2,1)S(1)} %collective-permute-done.6.refs_2_), channel_id=1, source_target_pairs={{0,32},{32,0},{64,96},{96,64},{128,160},{160,128},{192,224},{224,1... | collective-permute-start | bytes 1769480 | tf_op jit(solution)/shard_map/ppermute | solution.py:407
  193.2 3.3 %collective-permute-start.11 = (bf16[192,1536]{1,0:T(8,128)(2,1)S(1)}, bf16[192,1536]{1,0:T(8,128)(2,1)}, u32[]{:S(2)}, u32[]{:S(2)}) collective-permute-start(bf16[192,1536]{1,0:T(8,128)(2,1)S(1)} %collective-permute-done.7.refs_3_), channel_id=1, source_target_pairs={{0,32},{32,0},{64,96},{96,64},{128,160},{160,128},{192,224},{224,1... | collective-permute-start | bytes 1769480 | tf_op jit(solution)/shard_map/ppermute | solution.py:407
  194.8 2.6 collective-permute-start.9
  196.3 4.7 %copy-start.9 = (bf16[2,3,96,1536]{3,0,1,2:T(2,128)(2,1)S(1)}, bf16[2,3,96,1536]{3,0,1,2:T(2,128)(2,1)}, u32[]{:S(2)}) copy-start(bf16[2,3,96,1536]{3,0,1,2:T(2,128)(2,1)} %copy-done.8) | copy-start | bytes 5308420
  198.9 2.1 copy-start
  209.4 5.5 %copy-start.10 = (bf16[2,3,96,1536]{3,2,1,0:T(8,128)(2,1)S(1)}, bf16[2,3,96,1536]{3,2,1,0:T(8,128)(2,1)}, u32[]{:S(2)}) copy-start(bf16[2,3,96,1536]{3,2,1,0:T(8,128)(2,1)} %copy.29) | copy-start | bytes 5308420
  209.4 10.9 %slice-start = ((s8[4718592]{0:T(1024)(128)(4,1)}), s8[524288]{0:T(1024)(128)(4,1)S(1)}, s32[]{:S(2)}) async-start(s8[4718592]{0:T(1024)(128)(4,1)} %bitcast.44), calls=%async_computation.5 | async-start | bytes 1048576
  214.9 5.5 %slice-start.1 = ((s8[4718592]{0:T(1024)(128)(4,1)}), s8[4194304]{0:T(1024)(128)(4,1)S(1)}, s32[]{:S(2)}) async-start(s8[4718592]{0:T(1024)(128)(4,1)} %bitcast.44), calls=%async_computation.6 | async-start | bytes 8388608
  214.9 5.5 %copy-start.11 = (bf16[576,1536]{1,0:T(8,128)(2,1)S(1)}, bf16[576,1536]{1,0:T(8,128)(2,1)}, u32[]{:S(2)}) copy-start(bf16[576,1536]{1,0:T(8,128)(2,1)} %reshape.67) | copy-start | bytes 5308420
  214.9 8.5 %slice-start.2 = ((s8[7077888]{0:T(1024)(128)(4,1)}), s8[2883584]{0:T(1024)(128)(4,1)S(1)}, s32[]{:S(2)}) async-start(s8[7077888]{0:T(1024)(128)(4,1)} %bitcast.52), calls=%async_computation.7 | async-start | bytes 5767168
  214.9 19.3 %slice-start.4 = ((s8[7077888]{0:T(1024)(128)(4,1)}), s8[4194304]{0:T(1024)(128)(4,1)S(1)}, s32[]{:S(2)}) async-start(s8[7077888]{0:T(1024)(128)(4,1)} %bitcast.54), calls=%async_computation.9 | async-start | bytes 8388608
  220.3 3.0 %copy-start.4 = (s32[96,1]{1,0:T(8,128)S(1)}, s32[96,1]{1,0:T(8,128)}, u32[]{:S(2)}) copy-start(s32[96,1]{1,0:T(8,128)} %copy.30.index_ref) | copy-start | bytes 1156
  220.4 3.0 %copy-start.6 = (bf16[2,3,96,1536]{3,2,1,0:T(8,128)(2,1)S(1)}, bf16[2,3,96,1536]{3,2,1,0:T(8,128)(2,1)}, u32[]{:S(2)}) copy-start(bf16[2,3,96,1536]{3,2,1,0:T(8,128)(2,1)} %param.14) | copy-start | bytes 5308420
  220.4 3.0 %slice-start.3 = ((s8[7077888]{0:T(1024)(128)(4,1)}), s8[4194304]{0:T(1024)(128)(4,1)S(1)}, s32[]{:S(2)}) async-start(s8[7077888]{0:T(1024)(128)(4,1)} %bitcast.52), calls=%async_computation.8 | async-start | bytes 8388608
  220.4 13.8 %slice-start.5 = ((s8[7077888]{0:T(1024)(128)(4,1)}), s8[2883584]{0:T(1024)(128)(4,1)S(1)}, s32[]{:S(2)}) async-start(s8[7077888]{0:T(1024)(128)(4,1)} %bitcast.54), calls=%async_computation.10 | async-start | bytes 5767168
  223.4 10.8 %copy-start.3 = (s32[96,1]{1,0:T(8,128)S(1)}, s32[96,1]{1,0:T(8,128)}, u32[]{:S(2)}) copy-start(s32[96,1]{1,0:T(8,128)} %copy.25.index_ref) | copy-start | bytes 1156
  223.4 10.8 %copy-start.7 = (bf16[2,96,3,1536]{3,1,2,0:T(8,128)(2,1)S(1)}, bf16[2,96,3,1536]{3,1,2,0:T(8,128)(2,1)}, u32[]{:S(2)}) copy-start(bf16[2,96,3,1536]{3,1,2,0:T(8,128)(2,1)} %param.17) | copy-start | bytes 5308420
  233.6 0.6 copy-start.1
  245.4 0.6 copy-start.2

commit v5 on v4

--- a/solution.py
+++ b/solution.py
@@ -60,18 +60,28 @@
     return p.reshape(STACK * G, G).astype(jnp.bfloat16)
 
 
+def both_ways(row):
+    i = lax.broadcasted_iota(jnp.int32, (G, G), 0)
+    j = lax.broadcasted_iota(jnp.int32, (G, G), 1)
+    spread = jnp.broadcast_to(row.astype(jnp.float32), (G, G))
+    down = jnp.sum(jnp.where(i == j, spread, 0.0), axis=1, keepdims=True).astype(jnp.int32)
+    across = jnp.concatenate([row, jnp.zeros((1, LANES - G), jnp.int32)], axis=1)
+    return jnp.broadcast_to(across, (G, LANES)), jnp.broadcast_to(down, (G, LANES))
+
+
 def pick(row, index):
     return jnp.take_along_axis(row, index, axis=1, mode="promise_in_bounds")
 
 
 def forward_kernel(
-    q_ref, k_ref, x_ref, table_ref, level_ref, p_ref, o_ref, bias_ref, sent_ref, *, transpose
+    q_ref, k_ref, x_ref, table_ref, pos_ref, p_ref, o_ref, bias_ref, sent_ref, *, transpose
 ):
     masks = head_masks()
 
     @pl.when(pl.program_id(0) == 0)
     def _():
-        level = level_ref[...]
+        across, down = both_ways(pos_ref[...])
+        level = across - down + (G - 1)
         index = jnp.bitwise_and(level, LANES - 1)
         high = level >= LANES
 
@@ -160,7 +170,7 @@
     def _():
         lane = lax.broadcasted_iota(jnp.int32, (G, LANES), 1)
         spot = lax.broadcasted_iota(jnp.int32, (G, LANES), 0)
-        position = jnp.broadcast_to(index_ref[...], (G, LANES))
+        position = both_ways(index_ref[...])[1]
         inverse = jnp.sum(jnp.where(position == lane, spot, 0), axis=0, keepdims=True)
         inverse = jnp.broadcast_to(inverse, (G, LANES))
 
@@ -197,30 +207,62 @@
     return pl.BlockSpec(shape, lambda i: (0,) * len(shape))
 
 
-def attention_forward(q, k, x, table, level, transpose):
+def row_forward_kernel(
+    q_ref, k_ref, x_ref, unit_ref, coord_ref, pos_ref,
+    p_ref, o_ref, table_ref, squashed_ref, bias_ref, sent_ref,
+):
+    @pl.when(pl.program_id(0) == 0)
+    def _():
+        table_kernel(unit_ref, coord_ref, table_ref, squashed_ref)
+
+    forward_kernel(
+        q_ref, k_ref, x_ref, table_ref, pos_ref, p_ref, o_ref, bias_ref, sent_ref, transpose=False
+    )
+
+
+def forward_cost(n):
+    return pl.CostEstimate(
+        flops=n * NH * 16 * G * G * LANES, transcendentals=n * NH * G * G, bytes_accessed=20_000_000
+    )
+
+
+def row_forward(q, k, v, units, coords, positions):
     n = q.shape[0]
-    scratch = [pltpu.VMEM((NH * G, LANES), jnp.float32)]
-    kernel = functools.partial(forward_kernel, transpose=transpose)
-    if transpose:
-        kernel = functools.partial(kernel, sent_ref=None)
-        spec, shape = each(BLOCK), (n, G, D)
-    else:
-        scratch.append(pltpu.VMEM((GRID * MESSAGE, LANES), jnp.float32))
-        spec, shape = whole((GRID, MESSAGE, LANES)), (GRID, MESSAGE, LANES)
+    table = (NH, 2 * LANES)
     return pl.pallas_call(
-        kernel,
+        row_forward_kernel,
         grid=(n,),
-        in_specs=[each(BLOCK)] * 3 + [whole((NH, 2 * LANES)), whole((G, LANES))],
-        out_specs=[each(PSHAPE), spec],
+        in_specs=[each(BLOCK)] * 3
+        + [whole((HM // 2, LANES)), whole((1, 2 * LANES)), whole((1, G))],
+        out_specs=[each(PSHAPE), whole((GRID, MESSAGE, LANES)), whole(table), whole(table)],
         out_shape=[
             jax.ShapeDtypeStruct((n, NH * G, G), jnp.bfloat16),
-            jax.ShapeDtypeStruct(shape, jnp.bfloat16),
+            jax.ShapeDtypeStruct((GRID, MESSAGE, LANES), jnp.bfloat16),
+            jax.ShapeDtypeStruct(table, jnp.float32),
+            jax.ShapeDtypeStruct(table, jnp.float32),
         ],
-        scratch_shapes=scratch,
-        cost_estimate=pl.CostEstimate(
-            flops=n * NH * 16 * G * G * LANES, transcendentals=n * NH * G * G, bytes_accessed=20_000_000
-        ),
-    )(q, k, x, table, level)
+        scratch_shapes=[
+            pltpu.VMEM((NH * G, LANES), jnp.float32),
+            pltpu.VMEM((GRID * MESSAGE, LANES), jnp.float32),
+        ],
+        cost_estimate=forward_cost(n),
+    )(q, k, v, units, coords, positions)
+
+
+def col_forward(q, k, g, table, positions):
+    n = q.shape[0]
+    return pl.pallas_call(
+        functools.partial(forward_kernel, sent_ref=None, transpose=True),
+        grid=(n,),
+        in_specs=[each(BLOCK)] * 3 + [whole((NH, 2 * LANES)), whole((1, G))],
+        out_specs=[each(PSHAPE), each(BLOCK)],
+        out_shape=[
+            jax.ShapeDtypeStruct((n, NH * G, G), jnp.bfloat16),
+            jax.ShapeDtypeStruct((n, G, D), jnp.bfloat16),
+        ],
+        scratch_shapes=[pltpu.VMEM((NH * G, LANES), jnp.float32)],
+        cost_estimate=forward_cost(n),
+    )(q, k, g, table, positions)
 
 
 def attention_backward(p, v, g, index, attend):
@@ -231,7 +273,7 @@
         functools.partial(backward_kernel, attend=attend),
         grid=(n,),
         compiler_params=pltpu.CompilerParams(vmem_limit_bytes=GRANT),
-        in_specs=[each(PSHAPE), each(BLOCK), each(BLOCK), whole((G, 1))],
+        in_specs=[each(PSHAPE), each(BLOCK), each(BLOCK), whole((1, G))],
         out_specs=specs + [whole((NH, 2 * LANES))],
         out_shape=shapes + [jax.ShapeDtypeStruct((NH, 2 * LANES), jnp.float32)],
         scratch_shapes=[pltpu.VMEM((NH * G, LANES), jnp.float32)],
@@ -239,11 +281,6 @@
             flops=n * NH * 16 * G * G * LANES, transcendentals=0, bytes_accessed=20_000_000
         ),
     )(p, v, g, index)
-
-
-def levels(positions):
-    level = positions[None, :] - positions[:, None] + (G - 1)
-    return jnp.pad(level, ((0, 0), (0, LANES - G)))
 
 
 def assemble_kernel(start_ref, *refs):
@@ -344,11 +381,6 @@
     return got.reshape(HM // 2, LANES)
 
 
-def bias_tables(units, coords):
-    shape = jax.ShapeDtypeStruct((NH, 2 * LANES), jnp.float32)
-    return pl.pallas_call(table_kernel, out_shape=[shape, shape])(units, coords)
-
-
 def unit_grads(units, coords, squashed, row_table, col_table, scale):
     return pl.pallas_call(
         functools.partial(grad_kernel, scale=scale),
@@ -371,20 +403,22 @@
     return [(i, ((i // 2 + step) % 4) * 2 + ((i % 2) ^ swap)) for i in range(DP)]
 
 
-def order_kernel(swap_ref, mine_ref, other_ref, out_ref):
-    half = mine_ref.shape[0]
+def order_kernel(swap_ref, mine_ref, other_ref, out_ref, *, parts):
+    size = mine_ref.shape[0] // parts
     for first, (a_ref, b_ref) in ((0, (mine_ref, other_ref)), (1, (other_ref, mine_ref))):
 
         @pl.when(swap_ref[0] == first)
         def _():
-            out_ref[:half] = a_ref[...]
-            out_ref[half:] = b_ref[...]
-
-
-def in_order(mine, other, swap):
+            for j in range(parts):
+                own = slice(j * size, (j + 1) * size)
+                out_ref[2 * j * size:(2 * j + 1) * size] = a_ref[own]
+                out_ref[(2 * j + 1) * size:(2 * j + 2) * size] = b_ref[own]
+
+
+def in_order(mine, other, swap, parts):
     rows = mine.shape[0]
     return pl.pallas_call(
-        order_kernel,
+        functools.partial(order_kernel, parts=parts),
         in_specs=[pl.BlockSpec(memory_space=pltpu.SMEM)] + [pl.BlockSpec(memory_space=pltpu.VMEM)] * 2,
         out_specs=pl.BlockSpec(memory_space=pltpu.VMEM),
         out_shape=jax.ShapeDtypeStruct((2 * rows, D), jnp.bfloat16),
@@ -396,9 +430,9 @@
 def fetch_weight(w_value):
     here = lax.axis_index("grid")
     part = w_value
-    for bit in range(5):
+    for bit, parts in ((2, 1), (0, 2), (1, 2), (3, 1), (4, 1)):
         other = lax.ppermute(part, "grid", [(g, g ^ (1 << bit)) for g in range(GRID)])
-        part = in_order(part, other, (here >> bit) & 1)
+        part = in_order(part, other, (here >> bit) & 1, parts)
     mine = [part]
     for step in (1, 2, 3):
         mine.append(lax.ppermute(part, "dp", along_x(step, 0)))
@@ -421,20 +455,17 @@
     col_count = q_col.shape[2]
     units = gather_units(mlp_in, mlp_bias, mlp_out)
     coords = jnp.pad(offset_coords(), (0, 2 * LANES - NOFF))[None]
-    table, squashed = bias_tables(units, coords)
     whole_weight = fetch_weight(w_value)
 
     rows = lambda x: x.reshape(images * row_count, G, D)
     cols = lambda x: x.transpose(0, 2, 1, 3).reshape(images * col_count, G, D)
-    p_row, row_out = attention_forward(
-        rows(q_row), rows(k_row), rows(v_row), table, levels(col_positions), False
+    p_row, row_out, table, squashed = row_forward(
+        rows(q_row), rows(k_row), rows(v_row), units, coords, col_positions[None]
     )
     col_out = lax.all_to_all(row_out, "grid", split_axis=0, concat_axis=0, tiled=True)
 
     grad_cols = cols(cotangent)
-    p_col, d_values = attention_forward(
-        cols(q_col), cols(k_col), grad_cols, table, levels(row_positions), True
-    )
+    p_col, d_values = col_forward(cols(q_col), cols(k_col), grad_cols, table, row_positions[None])
     d_values = d_values.reshape(images, col_count, G, D)
     d_rows = lax.all_to_all(d_values, "grid", split_axis=2, concat_axis=1, tiled=True)
 
@@ -444,7 +475,7 @@
         col_tokens, whole_weight, preferred_element_type=jnp.float32
     ).astype(jnp.bfloat16).reshape(images * col_count, G, D)
     attended, col_table = attention_backward(
-        p_col, value_cols, grad_cols, row_positions[:, None], True
+        p_col, value_cols, grad_cols, row_positions[None], True
     )
     attended = attended.reshape(images, col_count, G, D).transpose(0, 2, 1, 3)
 
@@ -453,7 +484,9 @@
         preferred_element_type=jnp.float32,
     )
     d_row_out = d_flat.astype(jnp.bfloat16).reshape(images * row_count, G, D)
-    (row_table,) = attention_backward(p_row, rows(v_row), d_row_out, col_positions[:, None], False)
+    (row_table,) = attention_backward(
+        p_row, rows(v_row), d_row_out, col_positions[None], False
+    )
 
     batch_size = lax.axis_size("dp") * images
     grads = unit_grads(units, coords, squashed, row_table, col_table, 1.0 / (batch_size * G))

time: 278 us -> 287 us (1.032)
  blocking collectives: 26.8 us -> 69 us
  waiting for transfers between devices: 94.1 us -> 65.6 us
  local copies, waits for them, and re-layouts: 26.8 us -> 21.7 us
    all_to_all x0 -> x1, blocking collectives: none -> 44 us  [shards(): lax.all_to_all(d_values, 'grid', split_axis=2, concat_axis=1, tiled=True)]
    all_to_all x1 -> x0, waiting for transfers between devices: 23.8 us -> none  [shards(): lax.all_to_all(d_values, 'grid', split_axis=2, concat_axis=1, tiled=True)]
    ppermute x4, starting transfers between devices: 17.5 us -> 22.1 us  [fetch_weight(): other.append(lax.ppermute(mine[step], 'dp', along_x(0, 1)))]
    ppermute x3, waiting for transfers between devices: 8.28 us -> 3.74 us  [fetch_weight(): mine.append(lax.ppermute(part, 'dp', along_x(step, 0)))]
    all_to_all x1 -> x0, starting transfers between devices: 4.12 us -> none  [shards(): lax.all_to_all(d_values, 'grid', split_axis=2, concat_axis=1, tiled=True)]
    ppermute x5, waiting for transfers between devices: 53.9 us -> 50.9 us  [fetch_weight(): other = lax.ppermute(part, 'grid', [(g, g ^ 1 << bit) for g in range(GRID)])]
    pallas_call x8 -> x7, Pallas kernels: 34 us -> 32.8 us  [the longest x1 17.3 us: row_forward(): pl.pallas_call(row_forward_kernel, grid=(n,), in_specs=[each(BLOCK)] * 3...]
  transfers between devices with their start and end apart: 15 -> 14, of which waited for: 11 -> 9; matrix products, arithmetic and copies ran while one was open for 3% -> 1% of each run, Pallas kernels for 7% -> 1%
where the time goes in v5:
time: 287 us; the launch traced here: 286 us
  blocking collectives  69 us (24%)
  waiting for transfers between devices  65.6 us (23%)
  Pallas kernels  61.7 us (21%)
  starting transfers between devices  58.8 us (20%)
  local copies, waits for them, and re-layouts  21.7 us (8%)
  matrix products  8.33 us (3%)
    ppermute x5, waiting for transfers between devices, fetch_weight(): other = lax.ppermute(part, 'grid', [(g, g ^ 1 << bit) for g in range(GRID)])  50.9 us
    all_to_all x1, blocking collectives, shards(): lax.all_to_all(d_values, 'grid', split_axis=2, concat_axis=1, tiled=True)  44 us
    ppermute x4, starting transfers between devices, fetch_weight(): other.append(lax.ppermute(mine[step], 'dp', along_x(0, 1)))  22.1 us
    pallas_call x2, Pallas kernels, attention_backward(): pl.pallas_call(functools.partial(backward_kernel, attend=attend), grid=(n...  21.5 us
    pallas_call x1, Pallas kernels, row_forward(): pl.pallas_call(row_forward_kernel, grid=(n,), in_specs=[each(BLOCK)] * 3...  17.3 us
    pallas_call x1, Pallas kernels, col_forward(): pl.pallas_call(functools.partial(forward_kernel, sent_ref=None, transpose...  15.4 us
    all_to_all x1, blocking collectives, reduce_units(): lax.all_to_all(grads.reshape(GRID, HALF, LANES), 'grid', 0, 0, tiled=True)  14.3 us
    ppermute x5, starting transfers between devices, fetch_weight(): other = lax.ppermute(part, 'grid', [(g, g ^ 1 << bit) for g in range(GRID)])  12.2 us
  transfers between devices with their start and end apart: 14, of which 9 were waited for; matrix products, arithmetic and copies ran while one was open for 1% of the time, Pallas kernels for 1%

profile of v5, /device:TPU:1, one launch (start us, length us, event | category | flops | bytes accessed | tf_op | source)
XLA Modules:
  0.0 286.2 jit_solution(3971951214785944165)
XLA Ops:
  0.6 1.5 shard_map.147
  2.2 12.0 %all-to-all-start = ((f32[32,8,128]{2,1,0:T(8,128)}), f32[32,8,128]{2,1,0:T(8,128)S(1)}, u32[]{:S(2)}, u32[]{:S(2)}) async-start(f32[32,8,128]{2,1,0:T(8,128)} %shard_map.147), calls=%async_computation | async-start | bytes 262144 | tf_op jit(solution)/shard_map/all_to_all | solution.py:380
  14.2 0.6 pad.4
  14.8 8.6 %all-to-all-done = f32[32,8,128]{2,1,0:T(8,128)S(1)} async-done(((f32[32,8,128]{2,1,0:T(8,128)}), f32[32,8,128]{2,1,0:T(8,128)S(1)}, u32[]{:S(2)}, u32[]{:S(2)}) %all-to-all-start) | async-done | bytes 131104 | tf_op jit(solution)/shard_map/all_to_all | solution.py:380
  23.4 0.7 copy-done.11
  24.0 17.3 %shard_map.148 = (bf16[6,4608,96]{2,1,0:T(8,128)(2,1)}, bf16[32,216,128]{2,1,0:T(8,128)(2,1)}, f32[48,256]{1,0:T(8,128)}, f32[48,256]{1,0:T(8,128)}) custom-call(bf16[6,96,1536]{2,1,0:T(8,128)(2,1)} %bitcast.72, bf16[6,96,1536]{2,1,0:T(8,128)(2,1)} %bitcast.73, bf16[6,96,1536]{2,1,0:T(8,128)(2,1)} %bitcast.46, f32[256,128]{1,0:T(8,128)} %bitcast.65, ...), custom_call_target="tpu_custom_call" | custom-call | flops 5435817984 | bytes 20000000 | tf_op jit(solution)/shard_map/pallas_call | solution.py:232
  41.3 15.4 %shard_map.149 = (bf16[6,4608,96]{2,1,0:T(8,128)(2,1)}, bf16[6,96,1536]{2,1,0:T(8,128)(2,1)}) custom-call(bf16[6,96,1536]{2,1,0:T(8,128)(2,1)} %bitcast.74, bf16[6,96,1536]{2,1,0:T(8,128)(2,1)} %bitcast.75, bf16[6,96,1536]{2,1,0:T(8,128)(2,1)} %bitcast.48, f32[48,256]{1,0:T(8,128)} %get-tuple-element.15.table_ref, s32[1,96]{1,0:T(1,128)} %bitcast.52), custom_call_target="tpu_custom_call" | custom-call | flops 5435817984 | bytes 20000000 | tf_op jit(solution)/shard_map/pallas_call | solution.py:254
  56.7 3.3 %copy.21 = bf16[2,3,96,1536]{3,0,1,2:T(2,128)(2,1)S(1)} copy(bf16[2,3,96,1536]{3,2,1,0:T(8,128)(2,1)} %bitcast.64) | data formatting | bytes 3538944 | tf_op jit(solution)/shard_map/reshape | solution.py:469
  60.0 44.0 %all_to_all.38 = bf16[2,3,96,1536]{3,0,1,2:T(2,128)(2,1)} all-to-all(bf16[2,3,96,1536]{3,0,1,2:T(2,128)(2,1)S(1)} %copy.21), channel_id=1, replica_groups=mesh['dp'=8,'grid'=32] {'grid'}, dimensions={2} | all-to-all | bytes 3538944 | tf_op jit(solution)/shard_map/all_to_all | solution.py:470
  104.0 8.2 %all-to-all-start.1 = ((bf16[32,216,128]{2,1,0:T(8,128)(2,1)}), bf16[32,216,128]{2,1,0:T(8,128)(2,1)}, u32[]{:S(2)}, u32[]{:S(2)}) async-start(bf16[32,216,128]{2,1,0:T(8,128)(2,1)} %get-tuple-element.17), calls=%async_computation.1 | async-start | bytes 3538944 | tf_op jit(solution)/shard_map/all_to_all | solution.py:465
  112.2 0.0 copy-done.3
  112.2 5.2 %collective-permute-start = (bf16[6,1536]{1,0:T(8,128)(2,1)S(1)}, bf16[6,1536]{1,0:T(8,128)(2,1)S(1)}, u32[]{:S(2)}, u32[]{:S(2)}) collective-permute-start(bf16[6,1536]{1,0:T(8,128)(2,1)S(1)} %copy-done.3), channel_id=1, source_target_pairs={{0,4},{1,5},{2,6},{3,7},{4,0},{5,1},{6,2},{7,3},{8,12},{9,13},{10,... | collective-permute-start | bytes 55304 | tf_op jit(solution)/shard_map/ppermute | solution.py:434
  117.4 37.3 %collective-permute-done.other_ref = bf16[6,1536]{1,0:T(8,128)(2,1)S(1)} collective-permute-done((bf16[6,1536]{1,0:T(8,128)(2,1)S(1)}, bf16[6,1536]{1,0:T(8,128)(2,1)S(1)}, u32[]{:S(2)}, u32[]{:S(2)}) %collective-permute-start) | collective-permute-done | bytes 18464 | tf_op jit(solution)/shard_map/ppermute | solution.py:434
  154.7 1.8 collective-permute-start.1
  156.5 1.5 collective-permute-done.1.other_ref
  158.0 0.3 collective-permute-start.2
  158.4 3.9 %collective-permute-done.2.other_ref = bf16[24,1536]{1,0:T(8,128)(2,1)S(1)} collective-permute-done((bf16[24,1536]{1,0:T(8,128)(2,1)S(1)}, bf16[24,1536]{1,0:T(8,128)(2,1)S(1)}, u32[]{:S(2)}, u32[]{:S(2)}) %collective-permute-start.2) | collective-permute-done | bytes 73760 | tf_op jit(solution)/shard_map/ppermute | solution.py:434
  162.3 1.7 collective-permute-start.3
  164.0 2.5 collective-permute-done.3.other_ref
  166.5 3.2 %collective-permute-start.4 = (bf16[96,1536]{1,0:T(8,128)(2,1)S(1)}, bf16[96,1536]{1,0:T(8,128)(2,1)S(1)}, u32[]{:S(2)}, u32[]{:S(2)}) collective-permute-start(bf16[96,1536]{1,0:T(8,128)(2,1)S(1)} %shard_map.153.mine_ref), channel_id=1, source_target_pairs={{0,16},{1,17},{2,18},{3,19},{4,20},{5,21},{6,22},{7,23},{8,24},{9,... | collective-permute-start | bytes 884744 | tf_op jit(solution)/shard_map/ppermute | solution.py:434
  169.7 5.7 %collective-permute-done.4.other_ref = bf16[96,1536]{1,0:T(8,128)(2,1)S(1)} collective-permute-done((bf16[96,1536]{1,0:T(8,128)(2,1)S(1)}, bf16[96,1536]{1,0:T(8,128)(2,1)S(1)}, u32[]{:S(2)}, u32[]{:S(2)}) %collective-permute-start.4) | collective-permute-done | bytes 294944 | tf_op jit(solution)/shard_map/ppermute | solution.py:434
  175.4 2.8 collective-permute-start.6
  178.3 0.9 collective-permute-start.7
  179.1 0.6 collective-permute-start.5
  179.7 7.4 %collective-permute-start.8 = (bf16[192,1536]{1,0:T(8,128)(2,1)S(1)}, bf16[192,1536]{1,0:T(8,128)(2,1)S(1)}, u32[]{:S(2)}, u32[]{:S(2)}) collective-permute-start(bf16[192,1536]{1,0:T(8,128)(2,1)S(1)} %shard_map.154.refs_0_), channel_id=1, source_target_pairs={{0,32},{32,0},{64,96},{96,64},{128,160},{160,128},{192,224},{224,1... | collective-permute-start | bytes 1769480 | tf_op jit(solution)/shard_map/ppermute | solution.py:441
  187.1 0.0 collective-permute-done.6.refs_2_
  187.1 12.0 %collective-permute-start.10 = (bf16[192,1536]{1,0:T(8,128)(2,1)S(1)}, bf16[192,1536]{1,0:T(8,128)(2,1)S(1)}, u32[]{:S(2)}, u32[]{:S(2)}) collective-permute-start(bf16[192,1536]{1,0:T(8,128)(2,1)S(1)} %collective-permute-done.6.refs_2_), channel_id=1, source_target_pairs={{0,32},{32,0},{64,96},{96,64},{128,160},{160,128},{192,224},{224,1... | collective-permute-start | bytes 1769480 | tf_op jit(solution)/shard_map/ppermute | solution.py:441
  199.1 3.7 %collective-permute-done.7.refs_3_ = bf16[192,1536]{1,0:T(8,128)(2,1)S(1)} collective-permute-done((bf16[192,1536]{1,0:T(8,128)(2,1)S(1)}, bf16[192,1536]{1,0:T(8,128)(2,1)S(1)}, u32[]{:S(2)}, u32[]{:S(2)}) %collective-permute-start.7) | collective-permute-done | bytes 589856 | tf_op jit(solution)/shard_map/ppermute | solution.py:438
  202.9 2.7 collective-permute-start.11
  205.5 0.0 collective-permute-done.5.refs_1_
  205.5 0.0 collective-permute-start.9
  205.6 0.1 add_multiply_fusion.start_ref
  205.7 0.0 collective-permute-done.8.refs_4_
  205.7 0.0 collective-permute-done.10.refs_6_
  205.7 1.6 collective-permute-done.11.refs_7_
  207.3 0.8 collective-permute-done.9.refs_5_
  208.1 1.6 shard_map.155
  209.7 2.1 copy-done
  211.9 1.2 copy.23
  213.1 1.5 copy.24
  214.6 0.0 all-to-all-done.1
  214.6 3.3 %reshape.62 = bf16[32,3,2,3,1536]{4,3,2,1,0:T(4,128)(2,1)S(1)} reshape(bf16[32,216,128]{2,1,0:T(8,128)(2,1)} %all-to-all-done.1) | data formatting | bytes 3538944 | tf_op jit(solution)/shard_map/reshape | solution.py:472
  217.9 2.3 copy.20
  220.1 5.5 %reshape.63 = bf16[576,1536]{1,0:T(8,128)(2,1)} reshape(bf16[2,3,32,3,1536]{4,3,2,1,0:T(4,128)(2,1)} %copy.20) | data formatting | bytes 3538944 | tf_op jit(solution)/shard_map/reshape | solution.py:473
  225.6 0.0 copy-done.9
  225.6 0.0 slice-start.2
  225.7 0.0 slice-start.4
  225.7 5.4 %convolution_convert_fusion = bf16[576,1536]{1,0:T(8,128)(2,1)S(1)} fusion(bf16[576,1536]{1,0:T(8,128)(2,1)S(1)} %bitcast.63, bf16[1536,1536]{1,0:T(8,128)(2,1)} %copy-done), kind=kOutput, calls=%fused_computation | convolution fusion | flops 2718793728 | bytes 8257536 | tf_op jit(solution)/shard_map/dot_general | solution.py:482
  231.1 0.0 copy-start.4
  231.1 0.0 copy-start.6
  231.2 0.0 slice-start.3
  231.2 0.0 slice-start.5
  231.2 2.9 %convolution_convert_fusion.1 = bf16[576,1536]{1,0:T(8,128)(2,1)S(1)} fusion(bf16[576,1536]{1,0:T(8,128)(2,1)S(1)} %copy-done.10, bf16[1536,1536]{1,0:T(8,128)(2,1)S(1)} %bitcast.45), kind=kOutput, calls=%fused_computation.1 | convolution fusion | flops 2718793728 | bytes 8257536 | tf_op jit(solution)/shard_map/dot_general | solution.py:474
  234.1 0.0 copy-start.5
  234.2 0.0 copy-start.7
  234.2 10.2 %shard_map.157.row_ref = f32[48,256]{1,0:T(8,128)S(1)} custom-call(bf16[6,4608,96]{2,1,0:T(8,128)(2,1)S(1)} %bitcast.57, bf16[6,96,1536]{2,1,0:T(8,128)(2,1)S(1)} %bitcast.47, bf16[6,96,1536]{2,1,0:T(8,128)(2,1)S(1)} %bitcast.55, s32[1,96]{1,0:T(1,128)S(1)} %bitcast.51), custom_call_target="tpu_custom_call" | custom-call | flops 5435817984 | bytes 20000000 | tf_op jit(solution)/shard_map/pallas_call | solution.py:272
  244.4 0.6 copy-done.1
  245.0 0.0 slice-done.5
  245.0 11.3 %shard_map.156 = (bf16[6,96,1536]{2,1,0:T(8,128)(2,1)}, f32[48,256]{1,0:T(8,128)S(1)}) custom-call(bf16[6,4608,96]{2,1,0:T(8,128)(2,1)S(1)} %bitcast.59, bf16[6,96,1536]{2,1,0:T(8,128)(2,1)S(1)} %bitcast.54, bf16[6,96,1536]{2,1,0:T(8,128)(2,1)S(1)} %bitcast.49, s32[1,96]{1,0:T(1,128)S(1)} %bitcast.53), custom_call_target="tpu_custom_call" | custom-call | flops 5435817984 | bytes 20000000 | tf_op jit(solution)/shard_map/pallas_call | solution.py:272
  256.3 0.6 copy-done.2
  256.9 2.8 shard_map.158
  259.7 14.3 %all_to_all.39 = f32[32,8,128]{2,1,0:T(8,128)S(1)} all-to-all(f32[32,8,128]{2,1,0:T(8,128)} %bitcast.67), channel_id=1, replica_groups=mesh['dp'=8,'grid'=32] {'grid'}, dimensions={0} | all-to-all | bytes 262144 | tf_op jit(solution)/shard_map/all_to_all | solution.py:392
  274.1 10.7 %all_to_all.40.got_ref = f32[8,8,128]{2,1,0:T(8,128)} all-to-all(f32[8,8,128]{2,1,0:T(8,128)S(1)} %broadcast_in_dim.48), channel_id=1, replica_groups=mesh['dp'=8,'grid'=32] {'dp'}, dimensions={0} | all-to-all | bytes 65536 | tf_op jit(solution)/shard_map/all_to_all | solution.py:394
  284.8 1.4 shard_map.159
  (34 shorter events, 0.3 us)
Async XLA Ops:
  2.2 21.2 %all-to-all-start = ((f32[32,8,128]{2,1,0:T(8,128)}), f32[32,8,128]{2,1,0:T(8,128)S(1)}, u32[]{:S(2)}, u32[]{:S(2)}) async-start(f32[32,8,128]{2,1,0:T(8,128)} %shard_map.147), calls=%async_computation | async-start | bytes 262144 | tf_op jit(solution)/shard_map/all_to_all | solution.py:380
  23.4 0.7 copy-start.11
  104.0 8.2 %copy-start.3 = (bf16[6,1536]{1,0:T(8,128)(2,1)S(1)}, bf16[6,1536]{1,0:T(8,128)(2,1)}, u32[]{:S(2)}) copy-start(bf16[6,1536]{1,0:T(8,128)(2,1)} %mine_ref.1) | copy-start | bytes 55300
  104.0 110.5 %all-to-all-start.1 = ((bf16[32,216,128]{2,1,0:T(8,128)(2,1)}), bf16[32,216,128]{2,1,0:T(8,128)(2,1)}, u32[]{:S(2)}, u32[]{:S(2)}) async-start(bf16[32,216,128]{2,1,0:T(8,128)(2,1)} %get-tuple-element.17), calls=%async_computation.1 | async-start | bytes 3538944 | tf_op jit(solution)/shard_map/all_to_all | solution.py:465
  112.2 42.5 %collective-permute-start = (bf16[6,1536]{1,0:T(8,128)(2,1)S(1)}, bf16[6,1536]{1,0:T(8,128)(2,1)S(1)}, u32[]{:S(2)}, u32[]{:S(2)}) collective-permute-start(bf16[6,1536]{1,0:T(8,128)(2,1)S(1)} %copy-done.3), channel_id=1, source_target_pairs={{0,4},{1,5},{2,6},{3,7},{4,0},{5,1},{6,2},{7,3},{8,12},{9,13},{10,... | collective-permute-start | bytes 55304 | tf_op jit(solution)/shard_map/ppermute | solution.py:434
  154.7 3.3 %collective-permute-start.1 = (bf16[12,1536]{1,0:T(8,128)(2,1)S(1)}, bf16[12,1536]{1,0:T(8,128)(2,1)S(1)}, u32[]{:S(2)}, u32[]{:S(2)}) collective-permute-start(bf16[12,1536]{1,0:T(8,128)(2,1)S(1)} %shard_map.150.mine_ref), channel_id=1, source_target_pairs={{0,1},{1,0},{2,3},{3,2},{4,5},{5,4},{6,7},{7,6},{8,9},{9,8},{10,11... | collective-permute-start | bytes 110600 | tf_op jit(solution)/shard_map/ppermute | solution.py:434
  158.0 4.2 %collective-permute-start.2 = (bf16[24,1536]{1,0:T(8,128)(2,1)S(1)}, bf16[24,1536]{1,0:T(8,128)(2,1)S(1)}, u32[]{:S(2)}, u32[]{:S(2)}) collective-permute-start(bf16[24,1536]{1,0:T(8,128)(2,1)S(1)} %shard_map.151.mine_ref), channel_id=1, source_target_pairs={{0,2},{1,3},{2,0},{3,1},{4,6},{5,7},{6,4},{7,5},{8,10},{9,11},{10,... | collective-permute-start | bytes 221192 | tf_op jit(solution)/shard_map/ppermute | solution.py:434
  162.3 4.2 %collective-permute-start.3 = (bf16[48,1536]{1,0:T(8,128)(2,1)S(1)}, bf16[48,1536]{1,0:T(8,128)(2,1)S(1)}, u32[]{:S(2)}, u32[]{:S(2)}) collective-permute-start(bf16[48,1536]{1,0:T(8,128)(2,1)S(1)} %shard_map.152.mine_ref), channel_id=1, source_target_pairs={{0,8},{1,9},{2,10},{3,11},{4,12},{5,13},{6,14},{7,15},{8,0},{9,1},... | collective-permute-start | bytes 442376 | tf_op jit(solution)/shard_map/ppermute | solution.py:434
  166.5 8.9 %collective-permute-start.4 = (bf16[96,1536]{1,0:T(8,128)(2,1)S(1)}, bf16[96,1536]{1,0:T(8,128)(2,1)S(1)}, u32[]{:S(2)}, u32[]{:S(2)}) collective-permute-start(bf16[96,1536]{1,0:T(8,128)(2,1)S(1)} %shard_map.153.mine_ref), channel_id=1, source_target_pairs={{0,16},{1,17},{2,18},{3,19},{4,20},{5,21},{6,22},{7,23},{8,24},{9,... | collective-permute-start | bytes 884744 | tf_op jit(solution)/shard_map/ppermute | solution.py:434
  175.4 11.7 %collective-permute-start.6 = (bf16[192,1536]{1,0:T(8,128)(2,1)S(1)}, bf16[192,1536]{1,0:T(8,128)(2,1)S(1)}, u32[]{:S(2)}, u32[]{:S(2)}) collective-permute-start(bf16[192,1536]{1,0:T(8,128)(2,1)S(1)} %shard_map.154.refs_0_), channel_id=1, source_target_pairs={{0,128},{32,160},{64,192},{96,224},{128,0},{160,32},{192,64},{224,... | collective-permute-start | bytes 1769480 | tf_op jit(solution)/shard_map/ppermute | solution.py:438
  178.3 24.6 %collective-permute-start.7 = (bf16[192,1536]{1,0:T(8,128)(2,1)S(1)}, bf16[192,1536]{1,0:T(8,128)(2,1)S(1)}, u32[]{:S(2)}, u32[]{:S(2)}) collective-permute-start(bf16[192,1536]{1,0:T(8,128)(2,1)S(1)} %shard_map.154.refs_0_), channel_id=1, source_target_pairs={{0,192},{32,224},{64,0},{96,32},{128,64},{160,96},{192,128},{224,1... | collective-permute-start | bytes 1769480 | tf_op jit(solution)/shard_map/ppermute | solution.py:438
  179.1 26.4 %collective-permute-start.5 = (bf16[192,1536]{1,0:T(8,128)(2,1)S(1)}, bf16[192,1536]{1,0:T(8,128)(2,1)S(1)}, u32[]{:S(2)}, u32[]{:S(2)}) collective-permute-start(bf16[192,1536]{1,0:T(8,128)(2,1)S(1)} %shard_map.154.refs_0_), channel_id=1, source_target_pairs={{0,64},{32,96},{64,128},{96,160},{128,192},{160,224},{192,0},{224,... | collective-permute-start | bytes 1769480 | tf_op jit(solution)/shard_map/ppermute | solution.py:438
  179.7 25.9 %collective-permute-start.8 = (bf16[192,1536]{1,0:T(8,128)(2,1)S(1)}, bf16[192,1536]{1,0:T(8,128)(2,1)S(1)}, u32[]{:S(2)}, u32[]{:S(2)}) collective-permute-start(bf16[192,1536]{1,0:T(8,128)(2,1)S(1)} %shard_map.154.refs_0_), channel_id=1, source_target_pairs={{0,32},{32,0},{64,96},{96,64},{128,160},{160,128},{192,224},{224,1... | collective-permute-start | bytes 1769480 | tf_op jit(solution)/shard_map/ppermute | solution.py:441
  187.1 18.6 %collective-permute-start.10 = (bf16[192,1536]{1,0:T(8,128)(2,1)S(1)}, bf16[192,1536]{1,0:T(8,128)(2,1)S(1)}, u32[]{:S(2)}, u32[]{:S(2)}) collective-permute-start(bf16[192,1536]{1,0:T(8,128)(2,1)S(1)} %collective-permute-done.6.refs_2_), channel_id=1, source_target_pairs={{0,32},{32,0},{64,96},{96,64},{128,160},{160,128},{192,224},{224,1... | collective-permute-start | bytes 1769480 | tf_op jit(solution)/shard_map/ppermute | solution.py:441
  202.9 4.4 %collective-permute-start.11 = (bf16[192,1536]{1,0:T(8,128)(2,1)S(1)}, bf16[192,1536]{1,0:T(8,128)(2,1)}, u32[]{:S(2)}, u32[]{:S(2)}) collective-permute-start(bf16[192,1536]{1,0:T(8,128)(2,1)S(1)} %collective-permute-done.7.refs_3_), channel_id=1, source_target_pairs={{0,32},{32,0},{64,96},{96,64},{128,160},{160,128},{192,224},{224,1... | collective-permute-start | bytes 1769480 | tf_op jit(solution)/shard_map/ppermute | solution.py:441
  205.5 2.6 collective-permute-start.9
  205.7 6.2 %copy-start.8 = (bf16[2,3,96,1536]{3,0,1,2:T(2,128)(2,1)S(1)}, bf16[2,3,96,1536]{3,0,1,2:T(2,128)(2,1)}, u32[]{:S(2)}) copy-start(bf16[2,3,96,1536]{3,0,1,2:T(2,128)(2,1)} %all_to_all.38) | copy-start | bytes 5308420
  209.7 2.1 copy-start
  220.1 5.5 %copy-start.9 = (bf16[2,3,96,1536]{3,2,1,0:T(8,128)(2,1)S(1)}, bf16[2,3,96,1536]{3,2,1,0:T(8,128)(2,1)}, u32[]{:S(2)}) copy-start(bf16[2,3,96,1536]{3,2,1,0:T(8,128)(2,1)} %copy.24) | copy-start | bytes 5308420
  220.1 10.9 %slice-start = ((s8[4718592]{0:T(1024)(128)(4,1)}), s8[524288]{0:T(1024)(128)(4,1)S(1)}, s32[]{:S(2)}) async-start(s8[4718592]{0:T(1024)(128)(4,1)} %bitcast.44), calls=%async_computation.5 | async-start | bytes 1048576
  225.6 5.5 %slice-start.1 = ((s8[4718592]{0:T(1024)(128)(4,1)}), s8[4194304]{0:T(1024)(128)(4,1)S(1)}, s32[]{:S(2)}) async-start(s8[4718592]{0:T(1024)(128)(4,1)} %bitcast.44), calls=%async_computation.6 | async-start | bytes 8388608
  225.6 5.5 %copy-start.10 = (bf16[576,1536]{1,0:T(8,128)(2,1)S(1)}, bf16[576,1536]{1,0:T(8,128)(2,1)}, u32[]{:S(2)}) copy-start(bf16[576,1536]{1,0:T(8,128)(2,1)} %reshape.63) | copy-start | bytes 5308420
  225.6 8.5 %slice-start.2 = ((s8[7077888]{0:T(1024)(128)(4,1)}), s8[2883584]{0:T(1024)(128)(4,1)S(1)}, s32[]{:S(2)}) async-start(s8[7077888]{0:T(1024)(128)(4,1)} %bitcast.56), calls=%async_computation.7 | async-start | bytes 5767168
  225.7 19.4 %slice-start.4 = ((s8[7077888]{0:T(1024)(128)(4,1)}), s8[4194304]{0:T(1024)(128)(4,1)S(1)}, s32[]{:S(2)}) async-start(s8[7077888]{0:T(1024)(128)(4,1)} %bitcast.58), calls=%async_computation.9 | async-start | bytes 8388608
  231.1 3.0 %copy-start.4 = (bf16[2,3,96,1536]{3,2,1,0:T(8,128)(2,1)S(1)}, bf16[2,3,96,1536]{3,2,1,0:T(8,128)(2,1)}, u32[]{:S(2)}) copy-start(bf16[2,3,96,1536]{3,2,1,0:T(8,128)(2,1)} %param.14) | copy-start | bytes 5308420
  231.1 3.0 %copy-start.6 = (s32[96]{0:T(128)S(1)}, s32[96]{0:T(128)}, u32[]{:S(2)}) copy-start(s32[96]{0:T(128)} %param.20) | copy-start | bytes 1156
  231.2 3.0 %slice-start.3 = ((s8[7077888]{0:T(1024)(128)(4,1)}), s8[4194304]{0:T(1024)(128)(4,1)S(1)}, s32[]{:S(2)}) async-start(s8[7077888]{0:T(1024)(128)(4,1)} %bitcast.56), calls=%async_computation.8 | async-start | bytes 8388608
  231.2 13.9 %slice-start.5 = ((s8[7077888]{0:T(1024)(128)(4,1)}), s8[2883584]{0:T(1024)(128)(4,1)S(1)}, s32[]{:S(2)}) async-start(s8[7077888]{0:T(1024)(128)(4,1)} %bitcast.58), calls=%async_computation.10 | async-start | bytes 5767168
  234.1 10.9 %copy-start.5 = (bf16[2,96,3,1536]{3,1,2,0:T(8,128)(2,1)S(1)}, bf16[2,96,3,1536]{3,1,2,0:T(8,128)(2,1)}, u32[]{:S(2)}) copy-start(bf16[2,96,3,1536]{3,1,2,0:T(8,128)(2,1)} %param.17) | copy-start | bytes 5308420
  234.2 10.9 %copy-start.7 = (s32[96]{0:T(128)S(1)}, s32[96]{0:T(128)}, u32[]{:S(2)}) copy-start(s32[96]{0:T(128)} %param.19) | copy-start | bytes 1156
  244.4 0.6 copy-start.1
  256.3 0.6 copy-start.2
